TPU v7x, 512 devices: a whole 4x8x8 slice. The times are simulated.
512 devices in a mesh: dp: 32 (over z, x), expert: 16 (over y, core).
Axes of the slice: x: 4, y: 8, z: 8, core: 2. Of those that a mesh axis runs over, the one named last changes fastest.
Arguments:
- tokens: bfloat16 [16384, 2048], P(('dp', 'expert')), may hold values from -6 to 6
- d_out: bfloat16 [16384, 2048], P(('dp', 'expert')), may hold values from -6 to 6
- expert_ids: int32 [16384, 4], P(('dp', 'expert')), may hold values from 0 to 127, all different within a row; in each aligned block of 32 rows (0 to 31, 32 to 63, ...) at most 2 rows name the same one
- gate_weights: float32 [16384, 4], P(('dp', 'expert')), may hold values from 0.05 to 1
- w_in: bfloat16 [512, 2048, 256], P(('dp', 'expert')), may hold values from -0.125 to 0.125
- w_out: bfloat16 [512, 256, 2048], P(('dp', 'expert')), may hold values from -0.1875 to 0.1875
Outputs:
- d_tokens: bfloat16 [16384, 2048], P(('dp', 'expert'))
- d_gates: float32 [16384, 4], P(('dp', 'expert'))
- d_w_in: bfloat16 [512, 2048, 256], P(('dp', 'expert'))
- d_w_out: bfloat16 [512, 256, 2048], P(('dp', 'expert'))
Inputs may be any that keep to these rules, and one draw needn't show every extreme that they name: `expert_ids`: each token names 4 different experts. Among the 32 tokens of one device no expert is named more than 2 times, and in every draw some device names some expert exactly 2 times.
All inputs are finite; a program needn't handle non-finite values.
Results may differ from a plain program's by a relative error of at most 0.02.
Values may be sent and summed in bfloat16 or wider, within the bound.
No kernel may reach another device: no remote copies, remote signals or barrier semaphores. Data moves between devices by JAX's collectives and lax.ppermute only.
A program may use at most 128 MiB of HBM per device.

v0:
```python
import jax
import jax.numpy as jnp
from jax import lax
from jax.sharding import PartitionSpec as P

TOPK = 4
SPLIT = 4


def on_device(tokens, d_out, expert_ids, gate_weights, w_in, w_out):
    tok_rows, model_width = tokens.shape
    dp_count = lax.axis_size("dp")
    ex_count = lax.axis_size("expert")
    experts = dp_count * ex_count // SPLIT
    slot_count = max(2 * tok_rows * TOPK // experts, 2)
    pair_count = tok_rows * TOPK
    highest = lax.Precision.HIGHEST
    flat_ids = expert_ids.reshape(pair_count)
    flat_gates = gate_weights.reshape(pair_count)
    hit_table = (flat_ids[:, None] == jnp.arange(experts, dtype=jnp.int32)[None, :]).astype(
        jnp.int32
    )
    earlier = jnp.cumsum(hit_table, axis=0) - hit_table
    slot_of = jnp.sum(earlier * hit_table, axis=1)
    target = flat_ids * slot_count + slot_of
    placed = jnp.arange(experts * slot_count, dtype=jnp.int32)
    route_pairs = (placed[:, None] == target[None, :]).astype(jnp.float32)
    pair_owner = jnp.arange(pair_count, dtype=jnp.int32) // TOPK
    pair_token = (pair_owner[:, None] == jnp.arange(tok_rows, dtype=jnp.int32)[None, :]).astype(
        jnp.float32
    )
    route_tok = jnp.dot(route_pairs, pair_token, precision=highest)
    route_bf = route_tok.astype(jnp.bfloat16)
    gate_slots = jnp.dot(route_pairs, flat_gates, precision=highest)
    gate_send = jnp.broadcast_to(
        gate_slots.reshape(experts, 1, slot_count), (experts, SPLIT, slot_count)
    ).reshape(dp_count, ex_count, slot_count)
    row_count = dp_count * ex_count * slot_count
    both_rows = jnp.concatenate([tokens, d_out], axis=1)
    slot_rows = jnp.dot(route_bf, both_rows, preferred_element_type=jnp.float32).astype(
        jnp.bfloat16
    )
    outgoing = jnp.broadcast_to(
        slot_rows.reshape(experts, 1, slot_count * 2 * model_width),
        (experts, SPLIT, slot_count * 2 * model_width),
    )
    outgoing = outgoing.reshape(dp_count, ex_count, slot_count * 2 * model_width)
    received, gate_rows = (
        lax.all_to_all(
            lax.all_to_all(outgoing, "dp", split_axis=0, concat_axis=0, tiled=True),
            "expert",
            split_axis=1,
            concat_axis=1,
            tiled=True,
        ),
        lax.all_to_all(
            lax.all_to_all(
                gate_send.astype(jnp.bfloat16), "dp", split_axis=0, concat_axis=0, tiled=True
            ),
            "expert",
            split_axis=1,
            concat_axis=1,
            tiled=True,
        ).astype(gate_send.dtype),
    )
    flat_rows = received.reshape(row_count, 2 * model_width)
    in_rows = flat_rows[:, :model_width]
    out_grads = flat_rows[:, model_width:]
    gate_col = gate_rows.reshape(row_count, 1)
    w_first = w_in[0]
    w_second = w_out[0]
    preact = jnp.dot(in_rows, w_first, preferred_element_type=jnp.float32)
    sigmas = jax.nn.sigmoid(preact)
    activated = preact * sigmas
    pulled = lax.dot_general(
        out_grads, w_second, (((1,), (1,)), ((), ())), preferred_element_type=jnp.float32
    )
    d_preact = (gate_col * pulled * sigmas * (1.0 + preact * (1.0 - sigmas))).astype(jnp.bfloat16)
    partial_dx = lax.dot_general(
        d_preact, w_first, (((1,), (1,)), ((), ())), preferred_element_type=jnp.float32
    ).astype(jnp.bfloat16)
    gate_part = jnp.sum(activated * pulled, axis=1)
    scaled_act = (gate_col * activated).astype(jnp.bfloat16)
    grad_first = lax.dot_general(
        in_rows, d_preact, (((0,), (0,)), ((), ())), preferred_element_type=jnp.float32
    ).astype(jnp.bfloat16)
    grad_second = lax.dot_general(
        scaled_act, out_grads, (((0,), (0,)), ((), ())), preferred_element_type=jnp.float32
    ).astype(jnp.bfloat16)
    returned, gate_back = (
        lax.all_to_all(
            lax.all_to_all(
                partial_dx.reshape(dp_count, ex_count, slot_count * model_width),
                "dp",
                split_axis=0,
                concat_axis=0,
                tiled=True,
            ),
            "expert",
            split_axis=1,
            concat_axis=1,
            tiled=True,
        ),
        lax.all_to_all(
            lax.all_to_all(
                gate_part.reshape(dp_count, ex_count, slot_count).astype(jnp.bfloat16),
                "dp",
                split_axis=0,
                concat_axis=0,
                tiled=True,
            ),
            "expert",
            split_axis=1,
            concat_axis=1,
            tiled=True,
        ).astype(jnp.float32),
    )
    summed = jnp.sum(
        returned.reshape(experts, SPLIT, slot_count * model_width).astype(jnp.float32), axis=1
    )
    summed = summed.reshape(experts * slot_count, model_width)
    d_tokens = lax.dot_general(
        route_tok, summed, (((0,), (0,)), ((), ())), precision=highest
    ).astype(jnp.bfloat16)
    gate_total = jnp.sum(gate_back.reshape(experts, SPLIT, slot_count), axis=1).reshape(
        experts * slot_count
    )
    d_gates = jnp.dot(gate_total, route_pairs, precision=highest).reshape(tok_rows, TOPK)
    return (d_tokens, d_gates, grad_first[None], grad_second[None])


def solution(mesh):
    placed = (
        P(("dp", "expert"), None),
        P(("dp", "expert"), None),
        P(("dp", "expert"), None),
        P(("dp", "expert"), None),
        P(("dp", "expert"), None, None),
        P(("dp", "expert"), None, None),
    )
    return jax.shard_map(
        on_device,
        mesh=mesh,
        in_specs=placed,
        out_specs=(
            P(("dp", "expert"), None),
            P(("dp", "expert"), None),
            P(("dp", "expert"), None, None),
            P(("dp", "expert"), None, None),
        ),
        check_vma=False,
    )
```

profile of v0, /device:TPU:1, one launch (start us, length us, event | category | flops | bytes accessed | tf_op | source)
XLA Modules:
  0.0 750.5 jit_solution(14090365242204254296)
XLA Ops:
  0.6 0.0 copy-start
  0.7 0.8 copy.46
  1.5 0.1 reshape.117
  1.6 0.8 copy.47
  2.4 0.1 reshape.130
  2.5 0.1 fusion.35
  2.6 0.2 reduce_window_sum.11
  2.8 0.2 select_reduce_fusion
  2.9 0.2 broadcast_compare_fusion
  3.2 0.1 fusion.30
  3.3 0.2 broadcast_in_dim.10
  3.5 0.1 convert_element_type.52
  3.6 0.6 copy.48
  4.2 13.7 %all-to-all-start = ((bf16[32,16,2]{1,2,0:T(2,128)(2,1)}), bf16[32,16,2]{1,2,0:T(2,128)(2,1)S(1)}, u32[]{:S(2)}, u32[]{:S(2)}) async-start(bf16[32,16,2]{1,2,0:T(2,128)(2,1)} %copy.48), calls=%async_computation | async-start | bytes 32768 | tf_op jit(solution)/shard_map/all_to_all | solution.py:57
  17.9 0.2 fusion.29
  18.2 3.1 convolution_convert_fusion
  21.2 2.7 broadcast_in_dim.11
  24.0 6.1 broadcast_in_dim.12
  30.0 12.5 %reshape.119 = bf16[32,16,8192]{2,1,0:T(8,128)(2,1)} reshape(bf16[128,4,8192]{2,1,0:T(4,128)(2,1)} %broadcast_in_dim.12) | data formatting | bytes 16777216 | tf_op jit(solution)/shard_map/reshape | solution.py:47
  42.5 0.0 all-to-all-done
  42.5 9.3 %all-to-all-start.2 = ((bf16[32,16,8192]{2,1,0:T(8,128)(2,1)}), bf16[32,16,8192]{2,1,0:T(8,128)(2,1)}, u32[]{:S(2)}, u32[]{:S(2)}) async-start(bf16[32,16,8192]{2,1,0:T(8,128)(2,1)} %reshape.119), calls=%async_computation.2 | async-start | bytes 16777216 | tf_op jit(solution)/shard_map/all_to_all | solution.py:50
  51.9 0.7 copy.49
  52.6 190.5 %all-to-all-done.2 = bf16[32,16,8192]{2,1,0:T(8,128)(2,1)} async-done(((bf16[32,16,8192]{2,1,0:T(8,128)(2,1)}), bf16[32,16,8192]{2,1,0:T(8,128)(2,1)}, u32[]{:S(2)}, u32[]{:S(2)}) %all-to-all-start.2) | async-done | bytes 8388640 | tf_op jit(solution)/shard_map/all_to_all | solution.py:50
  243.1 8.7 %all-to-all-start.1 = ((bf16[32,16,2]{0,2,1:T(2,128)(2,1)}), bf16[32,16,2]{0,2,1:T(2,128)(2,1)S(1)}, u32[]{:S(2)}, u32[]{:S(2)}) async-start(bf16[32,16,2]{0,2,1:T(2,128)(2,1)} %copy.49), calls=%async_computation.1 | async-start | bytes 16384 | tf_op jit(solution)/shard_map/all_to_all | solution.py:56
  251.7 11.2 %copy.52 = bf16[32,16,8192]{2,0,1:T(8,128)(2,1)} copy(bf16[32,16,8192]{2,1,0:T(8,128)(2,1)} %all-to-all-done.2) | data formatting | bytes 16777216 | tf_op jit(solution)/shard_map/all_to_all | solution.py:50
  262.9 0.0 all-to-all-done.1
  262.9 7.2 all-to-all-start.3
  270.2 0.2 copy.51
  270.4 0.2 reshape.126
  270.5 183.1 %all-to-all-done.3 = bf16[32,16,8192]{2,0,1:T(8,128)(2,1)} async-done(((bf16[32,16,8192]{2,0,1:T(8,128)(2,1)}), bf16[32,16,8192]{2,0,1:T(8,128)(2,1)}, u32[]{:S(2)}, u32[]{:S(2)}) %all-to-all-start.3) | async-done | bytes 8388640 | tf_op jit(solution)/shard_map/all_to_all | solution.py:49
  453.7 11.2 %copy.53 = bf16[32,16,8192]{2,1,0:T(8,128)(2,1)} copy(bf16[32,16,8192]{2,0,1:T(8,128)(2,1)} %all-to-all-done.3) | data formatting | bytes 16777216 | tf_op jit(solution)/shard_map/all_to_all | solution.py:49
  464.9 13.1 %reshape.120 = bf16[1024,4096]{1,0:T(8,128)(2,1)} reshape(bf16[32,16,8192]{2,1,0:T(8,128)(2,1)} %copy.53) | data formatting | bytes 16777216 | tf_op jit(solution)/shard_map/reshape | solution.py:66
  478.0 3.6 fusion.2
  481.7 1.0 copy-done.2
  482.7 0.2 copy-done.3
  482.9 1.6 multiply_reduce_fusion
  484.5 0.3 convert_element_type.61
  484.7 0.9 copy.56
  485.6 6.1 all-to-all-start.6
  491.8 3.3 convolution_convert_fusion.1
  495.1 7.1 reshape.121
  502.2 9.3 %all-to-all-start.4 = ((bf16[32,16,4096]{2,1,0:T(8,128)(2,1)}), bf16[32,16,4096]{2,1,0:T(8,128)(2,1)}, u32[]{:S(2)}, u32[]{:S(2)}) async-start(bf16[32,16,4096]{2,1,0:T(8,128)(2,1)} %reshape.121), calls=%async_computation.4 | async-start | bytes 8388608 | tf_op jit(solution)/shard_map/all_to_all | solution.py:92
  511.5 0.7 copy.57
  512.2 91.5 %all-to-all-done.4 = bf16[32,16,4096]{2,1,0:T(8,128)(2,1)} async-done(((bf16[32,16,4096]{2,1,0:T(8,128)(2,1)}), bf16[32,16,4096]{2,1,0:T(8,128)(2,1)}, u32[]{:S(2)}, u32[]{:S(2)}) %all-to-all-start.4) | async-done | bytes 4194336 | tf_op jit(solution)/shard_map/all_to_all | solution.py:92
  603.7 8.1 %all-to-all-start.7 = ((bf16[32,16,2]{0,2,1:T(2,128)(2,1)}), bf16[32,16,2]{0,2,1:T(2,128)(2,1)S(1)}, u32[]{:S(2)}, u32[]{:S(2)}) async-start(bf16[32,16,2]{0,2,1:T(2,128)(2,1)} %copy.57), calls=%async_computation.7 | async-start | bytes 16384 | tf_op jit(solution)/shard_map/all_to_all | solution.py:104
  611.8 6.4 copy.54
  618.2 0.5 all-to-all-done.7
  618.7 6.7 all-to-all-start.5
  625.4 0.1 iota_compare_fusion
  625.6 0.0 copy-start.5
  625.6 4.6 fusion.14
  630.2 4.4 fusion.17
  634.6 0.1 copy.59
  634.7 0.1 reshape.129
  634.8 0.1 reduce_sum.39
  634.9 0.1 copy.60
  635.0 0.1 reshape.132
  635.2 0.8 fusion.32
  636.0 83.0 %all-to-all-done.5 = bf16[32,16,4096]{2,0,1:T(8,128)(2,1)} async-done(((bf16[32,16,4096]{2,0,1:T(8,128)(2,1)}), bf16[32,16,4096]{2,0,1:T(8,128)(2,1)}, u32[]{:S(2)}, u32[]{:S(2)}) %all-to-all-start.5) | async-done | bytes 4194336 | tf_op jit(solution)/shard_map/all_to_all | solution.py:91
  719.0 7.8 %copy.55 = f32[32,16,4096]{2,1,0:T(8,128)} copy(bf16[32,16,4096]{2,0,1:T(8,128)(2,1)} %all-to-all-done.5) | data formatting | bytes 12582912 | tf_op jit(solution)/shard_map/convert_element_type | solution.py:119
  726.9 9.8 %reshape.127 = f32[128,4,4096]{2,1,0:T(4,128)} reshape(f32[32,16,4096]{2,1,0:T(8,128)} %copy.55) | data formatting | bytes 16777216 | tf_op jit(solution)/shard_map/convert_element_type | solution.py:119
  736.7 10.1 %reduce_sum.37 = f32[128,4096]{1,0:T(8,128)} reduce(f32[128,4,4096]{2,1,0:T(4,128)} %reshape.127, f32[]{:T(128)} %constant.30.clone.1), dimensions={1}, to_apply=%region_2.3 | reduce | flops 1572864 | bytes 10485764 | tf_op jit(solution)/shard_map/reduce_sum | solution.py:118
  746.8 1.7 reshape.122
  748.5 2.0 convolution_convert_fusion.2
  (15 shorter events, 0.1 us)
Async XLA Ops:
  0.6 477.4 %copy-start = (bf16[1,2048,256]{2,1,0:T(8,128)(2,1)S(1)}, bf16[1,2048,256]{2,1,0:T(8,128)(2,1)}, u32[]{:S(2)}) copy-start(bf16[1,2048,256]{2,1,0:T(8,128)(2,1)} %param.10) | copy-start | bytes 3145732
  4.2 38.3 %all-to-all-start = ((bf16[32,16,2]{1,2,0:T(2,128)(2,1)}), bf16[32,16,2]{1,2,0:T(2,128)(2,1)S(1)}, u32[]{:S(2)}, u32[]{:S(2)}) async-start(bf16[32,16,2]{1,2,0:T(2,128)(2,1)} %copy.48), calls=%async_computation | async-start | bytes 32768 | tf_op jit(solution)/shard_map/all_to_all | solution.py:57
  42.5 200.5 %all-to-all-start.2 = ((bf16[32,16,8192]{2,1,0:T(8,128)(2,1)}), bf16[32,16,8192]{2,1,0:T(8,128)(2,1)}, u32[]{:S(2)}, u32[]{:S(2)}) async-start(bf16[32,16,8192]{2,1,0:T(8,128)(2,1)} %reshape.119), calls=%async_computation.2 | async-start | bytes 16777216 | tf_op jit(solution)/shard_map/all_to_all | solution.py:50
  243.1 19.9 %all-to-all-start.1 = ((bf16[32,16,2]{0,2,1:T(2,128)(2,1)}), bf16[32,16,2]{0,2,1:T(2,128)(2,1)S(1)}, u32[]{:S(2)}, u32[]{:S(2)}) async-start(bf16[32,16,2]{0,2,1:T(2,128)(2,1)} %copy.49), calls=%async_computation.1 | async-start | bytes 16384 | tf_op jit(solution)/shard_map/all_to_all | solution.py:56
  262.9 190.8 %all-to-all-start.3 = ((bf16[32,16,8192]{2,0,1:T(8,128)(2,1)}), bf16[32,16,8192]{2,0,1:T(8,128)(2,1)}, u32[]{:S(2)}, u32[]{:S(2)}) async-start(bf16[32,16,8192]{2,0,1:T(8,128)(2,1)} %copy.52), calls=%async_computation.3 | async-start | bytes 16777216 | tf_op jit(solution)/shard_map/all_to_all | solution.py:49
  478.0 4.6 copy-start.2
  478.0 4.9 copy-start.3
  482.9 1.6 copy-start.4
  485.6 16.5 %all-to-all-start.6 = ((bf16[32,16,2]{1,2,0:T(2,128)(2,1)}), bf16[32,16,2]{1,2,0:T(2,128)(2,1)S(1)}, u32[]{:S(2)}, u32[]{:S(2)}) async-start(bf16[32,16,2]{1,2,0:T(2,128)(2,1)} %copy.56), calls=%async_computation.6 | async-start | bytes 32768 | tf_op jit(solution)/shard_map/all_to_all | solution.py:105
  502.2 101.6 %all-to-all-start.4 = ((bf16[32,16,4096]{2,1,0:T(8,128)(2,1)}), bf16[32,16,4096]{2,1,0:T(8,128)(2,1)}, u32[]{:S(2)}, u32[]{:S(2)}) async-start(bf16[32,16,4096]{2,1,0:T(8,128)(2,1)} %reshape.121), calls=%async_computation.4 | async-start | bytes 8388608 | tf_op jit(solution)/shard_map/all_to_all | solution.py:92
  603.7 15.0 %all-to-all-start.7 = ((bf16[32,16,2]{0,2,1:T(2,128)(2,1)}), bf16[32,16,2]{0,2,1:T(2,128)(2,1)S(1)}, u32[]{:S(2)}, u32[]{:S(2)}) async-start(bf16[32,16,2]{0,2,1:T(2,128)(2,1)} %copy.57), calls=%async_computation.7 | async-start | bytes 16384 | tf_op jit(solution)/shard_map/all_to_all | solution.py:104
  618.7 100.3 %all-to-all-start.5 = ((bf16[32,16,4096]{2,0,1:T(8,128)(2,1)}), bf16[32,16,4096]{2,0,1:T(8,128)(2,1)}, u32[]{:S(2)}, u32[]{:S(2)}) async-start(bf16[32,16,4096]{2,0,1:T(8,128)(2,1)} %copy.54), calls=%async_computation.5 | async-start | bytes 8388608 | tf_op jit(solution)/shard_map/all_to_all | solution.py:91
  625.6 4.6 copy-start.5
  736.7 13.8 %copy-start.1 = (bf16[1,2048,256]{2,1,0:T(8,128)(2,1)S(1)}, bf16[1,2048,256]{2,1,0:T(8,128)(2,1)}, u32[]{:S(2)}) copy-start(bf16[1,2048,256]{2,1,0:T(8,128)(2,1)} %param.10) | copy-start | bytes 3145732
where the time goes:
time: 752 us; the launch traced here: 750 us
  waiting for transfers between devices  549 us (73%)
  local copies, waits for them, and re-layouts  97 us (13%)
  starting transfers between devices  69.2 us (9%)
  matrix products  23.7 us (3%)
  other arithmetic  11 us (1%)
    all_to_all x1, waiting for transfers between devices, on_device(): lax.all_to_all(outgoing, 'dp', split_axis=0, concat_axis=0, tiled=True)  190 us
    all_to_all x1, waiting for transfers between devices, on_device(): lax.all_to_all(lax.all_to_all(outgoing, 'dp', split_axis=0, concat_axis=0...  183 us
    all_to_all x1, waiting for transfers between devices, on_device(): lax.all_to_all(partial_dx.reshape(dp_count, ex_count, slot_count * model_...  91.5 us
    all_to_all x1, waiting for transfers between devices, on_device(): lax.all_to_all(lax.all_to_all(partial_dx.reshape(dp_count, ex_count, slot...  83 us
    convert_element_type x2, local copies, waits for them, and re-layouts, on_device(): returned.reshape(experts, SPLIT, slot_count * model_width)  17.6 us
  transfers between devices with their start and end apart: 8, of which 5 were waited for; matrix products, arithmetic and copies ran while one was open for 9% of the time, Pallas kernels for 0%

commit v1 on v0

v1 whole, which is shorter than its diff:
```python
import jax
import jax.numpy as jnp
import numpy as np
from jax import lax
from jax.experimental import pallas as pl
from jax.experimental.pallas import tpu as pltpu
from jax.sharding import Mesh
from jax.sharding import PartitionSpec as P

TOPK = 4
LANES = 128
AXES = ("dp", "yh", "yl", "core")
ROUTE = ("dp", "yh")
GATE_ROWS = 8
HOLD_FLOPS = int(3e10)
SWAP = [(0, 1), (1, 0)]
f32, bf16 = jnp.float32, jnp.bfloat16


def dispatch_kernel(ids_ref, gates_ref, tok_ref, dout_ref, out_ref, target_ref, count_ref):
    tokens, width = tok_ref.shape[0], tok_ref.shape[1]
    out_ref[...] = jnp.zeros_like(out_ref)

    def clear(i, carry):
        count_ref[i] = 0
        return carry

    lax.fori_loop(0, count_ref.shape[0], clear, 0, unroll=8)

    def place(t, carry):
        row = tok_ref[t]
        grad = dout_ref[t].astype(f32)
        for k in range(TOPK):
            e = ids_ref[t, k]
            slot = count_ref[e]
            count_ref[e] = slot + 1
            at = 2 * e + slot
            target_ref[t, k] = at
            out_ref[at, 0:width, :] = row
            out_ref[at, width : 2 * width, :] = (grad * gates_ref[t, k]).astype(bf16)
        return carry

    lax.fori_loop(0, tokens, place, 0)


def dispatch(ids, gates, tok3, dout3, experts):
    tokens, width, _ = tok3.shape
    smem = pl.BlockSpec(memory_space=pltpu.SMEM)
    vmem = pl.BlockSpec(memory_space=pltpu.VMEM)
    return pl.pallas_call(
        dispatch_kernel,
        out_shape=(
            jax.ShapeDtypeStruct((2 * experts, 2 * width, LANES), bf16),
            jax.ShapeDtypeStruct((tokens, TOPK), jnp.int32),
        ),
        in_specs=[smem, smem, vmem, vmem],
        out_specs=(vmem, smem),
        scratch_shapes=[pltpu.SMEM((experts,), jnp.int32)],
        name="dispatch",
    )(ids, gates, tok3, dout3)


def hold(x, flops):
    anywhere = pl.BlockSpec(memory_space=pl.ANY)
    return pl.pallas_call(
        lambda x_ref, y_ref: None,
        out_shape=jax.ShapeDtypeStruct(x.shape, x.dtype),
        in_specs=[anywhere],
        out_specs=anywhere,
        input_output_aliases={0: 0},
        cost_estimate=pl.CostEstimate(flops=flops, bytes_accessed=0, transcendentals=0),
        name="hold",
    )(x)


def combine_kernel(target_ref, back_ref, dx_ref, gate_ref):
    tokens, width = dx_ref.shape[0], dx_ref.shape[1]
    lane = lax.broadcasted_iota(jnp.int32, (1, LANES), 1)

    def total(t, carry):
        acc = jnp.zeros((width, LANES), f32)
        gate = jnp.zeros((1, LANES), f32)
        for k in range(TOPK):
            at = target_ref[t, k]
            e, slot = lax.shift_right_logical(at, 1), lax.bitwise_and(at, 1)
            first = pl.multiple_of(slot * width, width)
            acc += back_ref[e, pl.ds(first, width), :].astype(f32)
            extra = back_ref[e, 2 * width : 2 * width + GATE_ROWS, :].astype(f32)
            pair = jnp.where(slot == 0, extra[0:2, :], extra[2:4, :])
            gate = jnp.where(lane == k, pair[0:1, :] + pair[1:2, :], gate)
        dx_ref[t] = acc.astype(bf16)
        gate_ref[pl.ds(t, 1), :] = gate
        return carry

    lax.fori_loop(0, tokens, total, 0)


def combine(target, back, tokens, width):
    vmem = pl.BlockSpec(memory_space=pltpu.VMEM)
    return pl.pallas_call(
        combine_kernel,
        out_shape=(
            jax.ShapeDtypeStruct((tokens, width, LANES), bf16),
            jax.ShapeDtypeStruct((tokens, LANES), f32),
        ),
        in_specs=[pl.BlockSpec(memory_space=pltpu.SMEM), vmem],
        out_specs=(vmem, vmem),
        name="combine",
    )(target, back)


def dot(a, b, ca, cb):
    return lax.dot_general(a, b, (((ca,), (cb,)), ((), ())), preferred_element_type=f32)


def on_device(tokens, d_out, expert_ids, gate_weights, w_in, w_out):
    tok_rows, model = tokens.shape
    width = model // LANES
    experts = lax.axis_size("dp") * lax.axis_size("yh")
    slots = 2 * experts
    own_in, own_out = w_in[0], w_out[0]
    hidden = own_out.shape[0]
    oth = lax.ppermute(jnp.concatenate([own_in.T, own_out], axis=0), "yl", SWAP)
    outgoing, target = dispatch(
        expert_ids,
        gate_weights,
        tokens.reshape(tok_rows, width, LANES),
        d_out.reshape(tok_rows, width, LANES),
        experts,
    )
    outgoing = outgoing.reshape(experts, 4 * width, LANES)
    arrived = lax.all_to_all(outgoing, ROUTE, split_axis=0, concat_axis=0, tiled=True)
    arrived, oth = lax.optimization_barrier((arrived, hold(oth, HOLD_FLOPS)))
    oth_in, oth_out = oth[:hidden], oth[hidden:]
    mine = arrived.reshape(slots, 2 * model)
    theirs = lax.ppermute(mine, "core", SWAP)
    rows = jnp.concatenate([mine, theirs], axis=0)
    rows_x, rows_g = rows[:, :model], rows[:, model:]

    def quarter(first, second, depth):
        preact = dot(rows_x, first, 1, depth)
        pulled = dot(rows_g, second, 1, 1)
        sig = jax.nn.sigmoid(preact)
        act = preact * sig
        d_pre = (pulled * sig * (1.0 + preact * (1.0 - sig))).astype(bf16)
        gate = jnp.sum(act * pulled, axis=1, keepdims=True)
        return d_pre, act.astype(bf16), gate

    dp_own, act_own, gate_own = quarter(own_in, own_out, 0)
    dp_oth, act_oth, gate_oth = quarter(oth_in, oth_out, 1)
    far = jnp.concatenate([dot(dp_oth, rows_x, 0, 0), dot(act_oth, rows_g, 0, 0)], axis=0).astype(bf16)
    came = lax.ppermute(far, "yl", SWAP)
    dx = dot(dp_own, own_in, 1, 1) + dot(dp_oth, oth_in, 1, 0)
    gate = gate_own + gate_oth
    dx_peer = lax.ppermute(dx[slots:].astype(bf16), "core", SWAP)
    gate_peer = lax.ppermute(gate[slots:], "core", SWAP)
    dx_sum = (dx[:slots] + dx_peer.astype(f32)).astype(bf16)
    gate_sum = gate[:slots] + gate_peer
    gate_high = gate_sum.astype(bf16)
    gate_low = (gate_sum - gate_high.astype(f32)).astype(bf16)
    gate_rows = jnp.concatenate([gate_high, gate_low], axis=1).reshape(experts, 4, 1)
    gate_rows = jnp.pad(gate_rows, ((0, 0), (0, GATE_ROWS - 4), (0, 0)))
    gate_rows = jnp.broadcast_to(gate_rows, (experts, GATE_ROWS, LANES))
    back = jnp.concatenate([dx_sum.reshape(experts, 2 * width, LANES), gate_rows], axis=1)
    returned = lax.all_to_all(back, ROUTE, split_axis=0, concat_axis=0, tiled=True)
    d_tok3, gate_rows = combine(target, returned, tok_rows, width)
    d_gates = gate_rows[:, :TOPK] / gate_weights
    d_first = (dot(rows_x, dp_own, 0, 0) + came[:hidden].T.astype(f32)).astype(bf16)
    d_second = (dot(act_own, rows_g, 0, 0) + came[hidden:].astype(f32)).astype(bf16)
    return (d_tok3.reshape(tok_rows, model), d_gates, d_first[None], d_second[None])


def solution(mesh):
    dp, expert = mesh.devices.shape
    fine = Mesh(np.asarray(mesh.devices).reshape(dp, expert // 4, 2, 2), AXES)
    flat, block = P(AXES, None), P(AXES, None, None)
    return jax.shard_map(
        on_device,
        mesh=fine,
        in_specs=(flat, flat, flat, flat, block, block),
        out_specs=(flat, flat, block, block),
        check_vma=False,
    )
```

time: 752 us -> 228 us (0.30)
  the two profiles are of different devices: /device:TPU:1 before, /device:TPU:6 now
where the time goes in v1:
time: 228 us; the launch traced here: 227 us
  waiting for transfers between devices  137 us (60%)
  starting transfers between devices  41.6 us (18%)
  matrix products  17.6 us (8%)
  local copies, waits for them, and re-layouts  16.5 us (7%)
  other arithmetic  6.84 us (3%)
  Pallas kernels  6.45 us (3%)
    all_to_all x1, waiting for transfers between devices, on_device(): lax.all_to_all(outgoing, ROUTE, split_axis=0, concat_axis=0, tiled=True)  44.8 us
    ppermute x1, waiting for transfers between devices, on_device(): came = lax.ppermute(far, 'yl', SWAP)  40.5 us
    ppermute x1, waiting for transfers between devices, on_device(): oth = lax.ppermute(jnp.concatenate([own_in.T, own_out], axis=0), 'yl', SWAP)  33 us
    all_to_all x1, starting transfers between devices, on_device(): lax.all_to_all(outgoing, ROUTE, split_axis=0, concat_axis=0, tiled=True)  19 us
    dot_general x10, matrix products, dot(): lax.dot_general(a, b, (((ca,), (cb,)), ((), ())), preferred_element_type=...  17.6 us
    all_to_all x1, waiting for transfers between devices, on_device(): lax.all_to_all(back, ROUTE, split_axis=0, concat_axis=0, tiled=True)  16.4 us
    unnamed x33, local copies, waits for them, and re-layouts  12.8 us
    all_to_all x1, starting transfers between devices, on_device(): lax.all_to_all(back, ROUTE, split_axis=0, concat_axis=0, tiled=True)  9.27 us
  transfers between devices with their start and end apart: 7, of which 5 were waited for; matrix products, arithmetic and copies ran while one was open for 10% of the time, Pallas kernels for 2%

profile of v1, /device:TPU:6, one launch (start us, length us, event | category | flops | bytes accessed | tf_op | source)
XLA Modules:
  0.0 227.3 jit_solution(2629436378929026641)
XLA Ops:
  0.6 0.0 copy-start.4
  0.6 1.6 copy.22
  2.2 0.0 copy-done.4
  2.2 0.0 copy-start.8
  2.2 0.0 copy-start.9
  2.3 0.0 copy-start.6
  2.3 0.0 copy-start.7
  2.3 1.4 pad_maximum_fusion
  3.7 3.5 %collective-permute-start = (bf16[512,2048]{1,0:T(8,128)(2,1)}, bf16[512,2048]{1,0:T(8,128)(2,1)}, u32[]{:S(2)}, u32[]{:S(2)}) collective-permute-start(bf16[512,2048]{1,0:T(8,128)(2,1)} %pad_maximum_fusion), channel_id=1, source_target_pairs={{0,2},{2,0},{1,3},{3,1},{4,6},{6,4},{5,7},{7,5},{8,10},{10,8},{9,1... | collective-permute-start | bytes 6291464 | tf_op jit(solution)/shard_map/ppermute | solution.py:123
  7.2 0.0 copy-done.8
  7.2 0.7 copy.21.gates_ref
  7.9 0.0 copy-done.9
  7.9 0.7 copy.20.ids_ref
  8.6 0.0 copy-done.6
  8.6 0.7 copy.33
  9.3 0.0 copy-done.7
  9.3 0.7 copy.34
  9.9 3.7 %dispatch.1 = (bf16[256,32,128]{2,1,0:T(8,128)(2,1)}, s32[32,4]{1,0:T(8,128)}) custom-call(s32[32,4]{1,0:T(8,128)} %copy.20.ids_ref, f32[32,4]{1,0:T(8,128)} %copy.21.gates_ref, bf16[32,16,128]{2,1,0:T(8,128)(2,1)} %bitcast.40, bf16[32,16,128]{2,1,0:T(8,128)(2,1)} %bitcast.41), custom_call_target="tpu_custom_call" | custom-call | tf_op jit(solution)/shard_map/dispatch/pallas_call | solution.py:50
  13.7 19.0 %all-to-all-start = ((bf16[128,64,128]{2,1,0:T(8,128)(2,1)}), bf16[128,64,128]{2,1,0:T(8,128)(2,1)S(1)}, u32[]{:S(2)}, u32[]{:S(2)}) async-start(bf16[128,64,128]{2,1,0:T(8,128)(2,1)} %bitcast.38), calls=%async_computation | async-start | bytes 4194304 | tf_op jit(solution)/shard_map/all_to_all | solution.py:132
  32.6 33.0 %collective-permute-done.x_ref = bf16[512,2048]{1,0:T(8,128)(2,1)} collective-permute-done((bf16[512,2048]{1,0:T(8,128)(2,1)}, bf16[512,2048]{1,0:T(8,128)(2,1)}, u32[]{:S(2)}, u32[]{:S(2)}) %collective-permute-start) | collective-permute-done | bytes 2097184 | tf_op jit(solution)/shard_map/ppermute | solution.py:123
  65.7 44.8 %all-to-all-done = bf16[128,64,128]{2,1,0:T(8,128)(2,1)S(1)} async-done(((bf16[128,64,128]{2,1,0:T(8,128)(2,1)}), bf16[128,64,128]{2,1,0:T(8,128)(2,1)S(1)}, u32[]{:S(2)}, u32[]{:S(2)}) %all-to-all-start) | async-done | bytes 2097184 | tf_op jit(solution)/shard_map/all_to_all | solution.py:132
  110.5 2.3 %reshape.47 = bf16[256,4096]{1,0:T(8,128)(2,1)} reshape(bf16[128,64,128]{2,1,0:T(8,128)(2,1)S(1)} %all-to-all-done) | data formatting | bytes 4194304 | tf_op jit(solution)/shard_map/reshape | solution.py:135
  112.8 1.9 collective-permute-start.1
  114.7 1.7 constant_dynamic-update-slice_fusion.1
  116.5 0.0 copy-start.2
  116.5 2.6 %collective-permute-done.1 = bf16[256,4096]{1,0:T(8,128)(2,1)S(1)} collective-permute-done((bf16[256,4096]{1,0:T(8,128)(2,1)}, bf16[256,4096]{1,0:T(8,128)(2,1)S(1)}, u32[]{:S(2)}, u32[]{:S(2)}) %collective-permute-start.1) | collective-permute-done | bytes 2097184 | tf_op jit(solution)/shard_map/ppermute | solution.py:136
  119.1 0.2 constant_dynamic-update-slice_fusion
  119.3 0.0 copy-done.2
  119.3 0.8 fusion.9
  120.1 0.0 copy-start.10
  120.1 2.8 %fusion.7 = f32[512,256]{0,1:T(8,128)S(1)} fusion(bf16[512,4096]{1,0:T(8,128)(2,1)S(1)} %constant_dynamic-update-slice_fusion, bf16[512,2048]{1,0:T(8,128)(2,1)} %hold.1), kind=kOutput, calls=%fused_computation.16 | convolution fusion | flops 536870912 | bytes 3670016 | tf_op jit(solution)/shard_map/dot_general | solution.py:113
  122.9 2.1 multiply_convert_fusion
  125.0 0.9 multiply_convert_fusion.1
  125.9 2.0 collective-permute-start.3
  127.9 1.0 convolution_convert_fusion.1
  128.9 0.8 fusion.17
  129.7 2.0 convolution_add_fusion
  131.7 2.0 copy-done
  133.7 0.1 slice.88
  133.8 2.3 %collective-permute-start.2 = (bf16[256,2048]{1,0:T(8,128)(2,1)S(1)}, bf16[256,2048]{1,0:T(8,128)(2,1)S(1)}, u32[]{:S(2)}, u32[]{:S(2)}) collective-permute-start(bf16[256,2048]{1,0:T(8,128)(2,1)S(1)} %slice.88), channel_id=1, source_target_pairs={{0,1},{1,0},{2,3},{3,2},{4,5},{5,4},{6,7},{7,6},{8,9},{9,8},{10,11... | collective-permute-start | bytes 3145736 | tf_op jit(solution)/shard_map/ppermute | solution.py:155
  136.1 1.0 convolution_convert_fusion
  137.1 1.5 pad_maximum_fusion.1
  138.6 3.7 %collective-permute-start.4 = (bf16[512,2048]{0,1:T(8,128)(2,1)}, bf16[512,2048]{0,1:T(8,128)(2,1)}, u32[]{:S(2)}, u32[]{:S(2)}) collective-permute-start(bf16[512,2048]{0,1:T(8,128)(2,1)} %pad_maximum_fusion.1), channel_id=1, source_target_pairs={{0,2},{2,0},{1,3},{3,1},{4,6},{6,4},{5,7},{7,5},{8,10},{10,8},{9,1... | collective-permute-start | bytes 6291464 | tf_op jit(solution)/shard_map/ppermute | solution.py:152
  142.3 0.0 collective-permute-done.3
  142.3 0.1 copy.23
  142.5 0.1 reshape.49
  142.6 0.0 collective-permute-done.2
  142.6 1.9 fusion.4
  144.5 0.5 reshape.48
  145.0 0.2 broadcast_in_dim.16
  145.2 0.0 copy-start.11
  145.2 1.3 pad_maximum_fusion.2
  146.5 9.3 %all-to-all-start.1 = ((bf16[128,40,128]{2,1,0:T(8,128)(2,1)}), bf16[128,40,128]{2,1,0:T(8,128)(2,1)S(1)}, u32[]{:S(2)}, u32[]{:S(2)}) async-start(bf16[128,40,128]{2,1,0:T(8,128)(2,1)} %pad_maximum_fusion.2), calls=%async_computation.1 | async-start | bytes 2621440 | tf_op jit(solution)/shard_map/all_to_all | solution.py:165
  155.8 40.5 %collective-permute-done.4 = bf16[512,2048]{0,1:T(8,128)(2,1)} collective-permute-done((bf16[512,2048]{0,1:T(8,128)(2,1)}, bf16[512,2048]{0,1:T(8,128)(2,1)}, u32[]{:S(2)}, u32[]{:S(2)}) %collective-permute-start.4) | collective-permute-done | bytes 2097184 | tf_op jit(solution)/shard_map/ppermute | solution.py:152
  196.3 0.0 copy-done.11
  196.3 2.8 %fusion.2 = bf16[1,256,2048]{1,2,0:T(8,128)(2,1)S(1)} fusion(bf16[512,4096]{1,0:T(8,128)(2,1)} %copy-done.3, bf16[512,2048]{0,1:T(8,128)(2,1)} %collective-permute-done.4, f32[512,256]{0,1:T(8,128)S(1)} %copy-done.11), kind=kOutput, calls=%fused_computation.7 | convolution fusion | flops 539099136 | bytes 4718592 | tf_op jit(solution)/shard_map/dot_general | solution.py:113
  199.1 1.4 copy.29
  200.5 3.6 %fusion.3 = bf16[1,2048,256]{2,1,0:T(8,128)(2,1)} fusion(bf16[512,256]{0,1:T(8,128)(2,1)S(1)} %get-tuple-element.26, bf16[512,4096]{1,0:T(8,128)(2,1)} %copy-done.3, bf16[512,2048]{0,1:T(8,128)(2,1)} %collective-permute-done.4), kind=kOutput, calls=%fused_computation.8 | convolution fusion | flops 538443776 | bytes 4456448 | tf_op jit(solution)/shard_map/dot_general | solution.py:113
  204.1 16.4 %all-to-all-done.1.back_ref = bf16[128,40,128]{2,1,0:T(8,128)(2,1)S(1)} async-done(((bf16[128,40,128]{2,1,0:T(8,128)(2,1)}), bf16[128,40,128]{2,1,0:T(8,128)(2,1)S(1)}, u32[]{:S(2)}, u32[]{:S(2)}) %all-to-all-start.1) | async-done | bytes 1310752 | tf_op jit(solution)/shard_map/all_to_all | solution.py:165
  220.5 1.1 copy-done.1
  221.6 2.7 %combine.1 = (bf16[32,16,128]{2,1,0:T(8,128)(2,1)}, f32[32,128]{1,0:T(8,128)}) custom-call(s32[32,4]{1,0:T(8,128)} %get-tuple-element.10.target_ref, bf16[128,40,128]{2,1,0:T(8,128)(2,1)} %copy-done.1), custom_call_target="tpu_custom_call" | custom-call | tf_op jit(solution)/shard_map/combine/pallas_call | solution.py:100
  224.4 1.6 copy.37
  225.9 0.7 slice_divide_fusion
  226.7 0.7 copy.28
  (13 shorter events, 0.1 us)
Async XLA Ops:
  0.6 1.6 copy-start.4
  2.2 5.0 %copy-start.8 = (f32[32,4]{0,1:T(4,128)S(1)}, f32[32,4]{0,1:T(4,128)}, u32[]{:S(2)}) copy-start(f32[32,4]{0,1:T(4,128)} %param.9) | copy-start | bytes 1540
  2.2 5.7 %copy-start.9 = (s32[32,4]{0,1:T(4,128)S(1)}, s32[32,4]{0,1:T(4,128)}, u32[]{:S(2)}) copy-start(s32[32,4]{0,1:T(4,128)} %param.8) | copy-start | bytes 1540
  2.3 6.3 %copy-start.6 = (bf16[32,2048]{1,0:T(8,128)(2,1)S(1)}, bf16[32,2048]{1,0:T(8,128)(2,1)}, u32[]{:S(2)}) copy-start(bf16[32,2048]{1,0:T(8,128)(2,1)} %param.6) | copy-start | bytes 393220
  2.3 7.0 %copy-start.7 = (bf16[32,2048]{1,0:T(8,128)(2,1)S(1)}, bf16[32,2048]{1,0:T(8,128)(2,1)}, u32[]{:S(2)}) copy-start(bf16[32,2048]{1,0:T(8,128)(2,1)} %param.7) | copy-start | bytes 393220
  3.7 62.0 %collective-permute-start = (bf16[512,2048]{1,0:T(8,128)(2,1)}, bf16[512,2048]{1,0:T(8,128)(2,1)}, u32[]{:S(2)}, u32[]{:S(2)}) collective-permute-start(bf16[512,2048]{1,0:T(8,128)(2,1)} %pad_maximum_fusion), channel_id=1, source_target_pairs={{0,2},{2,0},{1,3},{3,1},{4,6},{6,4},{5,7},{7,5},{8,10},{10,8},{9,1... | collective-permute-start | bytes 6291464 | tf_op jit(solution)/shard_map/ppermute | solution.py:123
  13.7 96.8 %all-to-all-start = ((bf16[128,64,128]{2,1,0:T(8,128)(2,1)}), bf16[128,64,128]{2,1,0:T(8,128)(2,1)S(1)}, u32[]{:S(2)}, u32[]{:S(2)}) async-start(bf16[128,64,128]{2,1,0:T(8,128)(2,1)} %bitcast.38), calls=%async_computation | async-start | bytes 4194304 | tf_op jit(solution)/shard_map/all_to_all | solution.py:132
  112.8 6.3 %collective-permute-start.1 = (bf16[256,4096]{1,0:T(8,128)(2,1)}, bf16[256,4096]{1,0:T(8,128)(2,1)S(1)}, u32[]{:S(2)}, u32[]{:S(2)}) collective-permute-start(bf16[256,4096]{1,0:T(8,128)(2,1)} %reshape.47), channel_id=1, source_target_pairs={{0,1},{1,0},{2,3},{3,2},{4,5},{5,4},{6,7},{7,6},{8,9},{9,8},{10,11... | collective-permute-start | bytes 6291464 | tf_op jit(solution)/shard_map/ppermute | solution.py:136
  116.5 2.8 %copy-start.2 = (bf16[1,2048,256]{2,1,0:T(8,128)(2,1)S(1)}, bf16[1,2048,256]{2,1,0:T(8,128)(2,1)}, u32[]{:S(2)}) copy-start(bf16[1,2048,256]{2,1,0:T(8,128)(2,1)} %param.10) | copy-start | bytes 3145732
  119.3 16.8 %copy-start.3 = (bf16[512,4096]{1,0:T(8,128)(2,1)}, bf16[512,4096]{1,0:T(8,128)(2,1)S(1)}, u32[]{:S(2)}) copy-start(bf16[512,4096]{1,0:T(8,128)(2,1)S(1)} %constant_dynamic-update-slice_fusion) | copy-start | bytes 12582916
  120.1 4.9 %copy-start.10 = (f32[512,256]{0,1:T(8,128)}, f32[512,256]{0,1:T(8,128)S(1)}, u32[]{:S(2)}) copy-start(f32[512,256]{0,1:T(8,128)S(1)} %fusion.9) | copy-start | bytes 1572868
  125.9 16.4 %collective-permute-start.3 = (f32[256,1]{0,1:T(1,128)S(1)}, f32[256,1]{0,1:T(1,128)S(1)}, u32[]{:S(2)}, u32[]{:S(2)}) collective-permute-start(f32[256,1]{0,1:T(1,128)S(1)} %bitcast.47), channel_id=1, source_target_pairs={{0,1},{1,0},{2,3},{3,2},{4,5},{5,4},{6,7},{7,6},{8,9},{9,8},{10,11... | collective-permute-start | bytes 3080 | tf_op jit(solution)/shard_map/ppermute | solution.py:156
  131.7 2.0 copy-start
  133.8 8.8 %collective-permute-start.2 = (bf16[256,2048]{1,0:T(8,128)(2,1)S(1)}, bf16[256,2048]{1,0:T(8,128)(2,1)S(1)}, u32[]{:S(2)}, u32[]{:S(2)}) collective-permute-start(bf16[256,2048]{1,0:T(8,128)(2,1)S(1)} %slice.88), channel_id=1, source_target_pairs={{0,1},{1,0},{2,3},{3,2},{4,5},{5,4},{6,7},{7,6},{8,9},{9,8},{10,11... | collective-permute-start | bytes 3145736 | tf_op jit(solution)/shard_map/ppermute | solution.py:155
  138.6 57.7 %collective-permute-start.4 = (bf16[512,2048]{0,1:T(8,128)(2,1)}, bf16[512,2048]{0,1:T(8,128)(2,1)}, u32[]{:S(2)}, u32[]{:S(2)}) collective-permute-start(bf16[512,2048]{0,1:T(8,128)(2,1)} %pad_maximum_fusion.1), channel_id=1, source_target_pairs={{0,2},{2,0},{1,3},{3,1},{4,6},{6,4},{5,7},{7,5},{8,10},{10,8},{9,1... | collective-permute-start | bytes 6291464 | tf_op jit(solution)/shard_map/ppermute | solution.py:152
  145.2 51.1 %copy-start.11 = (f32[512,256]{0,1:T(8,128)S(1)}, f32[512,256]{0,1:T(8,128)}, u32[]{:S(2)}) copy-start(f32[512,256]{0,1:T(8,128)} %copy-done.10) | copy-start | bytes 1572868
  146.5 74.0 %all-to-all-start.1 = ((bf16[128,40,128]{2,1,0:T(8,128)(2,1)}), bf16[128,40,128]{2,1,0:T(8,128)(2,1)S(1)}, u32[]{:S(2)}, u32[]{:S(2)}) async-start(bf16[128,40,128]{2,1,0:T(8,128)(2,1)} %pad_maximum_fusion.2), calls=%async_computation.1 | async-start | bytes 2621440 | tf_op jit(solution)/shard_map/all_to_all | solution.py:165
  200.5 25.4 %copy-start.5 = (f32[32,4]{1,0:T(8,128)S(1)}, f32[32,4]{1,0:T(8,128)}, u32[]{:S(2)}) copy-start(f32[32,4]{1,0:T(8,128)} %copy.21.gates_ref) | copy-start | bytes 1540
  220.5 1.1 copy-start.1

commit v2 on v1

--- a/solution.py
+++ b/solution.py
@@ -1,3 +1,5 @@
+import functools
+
 import jax
 import jax.numpy as jnp
 import numpy as np
@@ -10,7 +12,6 @@
 TOPK = 4
 LANES = 128
 AXES = ("dp", "yh", "yl", "core")
-ROUTE = ("dp", "yh")
 GATE_ROWS = 8
 HOLD_FLOPS = int(3e10)
 SWAP = [(0, 1), (1, 0)]
@@ -113,14 +114,89 @@
     return lax.dot_general(a, b, (((ca,), (cb,)), ((), ())), preferred_element_type=f32)
 
 
-def on_device(tokens, d_out, expert_ids, gate_weights, w_in, w_out):
+def experts_kernel(
+    rows_hbm, w0, w1, w2, w3, g0, g1, g2, g3, dx_ref, gate_ref, rows, weights, grads, total, in_sems, out_sems
+):
+    hidden, model = weights.shape[1] // 2, weights.shape[2]
+    loads = [pltpu.make_async_copy(rows_hbm, rows, in_sems.at[4])]
+    loads += [
+        pltpu.make_async_copy(w, weights.at[q], in_sems.at[q])
+        for q, w in enumerate((w0, w1, w2, w3))
+    ]
+    stores = [
+        pltpu.make_async_copy(grads.at[q], g, out_sems.at[q])
+        for q, g in enumerate((g0, g1, g2, g3))
+    ]
+    for load in loads:
+        load.start()
+    loads[0].wait()
+    gate = jnp.zeros((rows.shape[0], 1), f32)
+    for q in range(4):
+        loads[1 + q].wait()
+        preact = dot(rows[:, :model], weights[q, :hidden, :], 1, 1)
+        pulled = dot(rows[:, model:], weights[q, hidden:, :], 1, 1)
+        sig = jax.nn.sigmoid(preact)
+        act = preact * sig
+        d_pre = (pulled * sig * (1.0 + preact * (1.0 - sig))).astype(bf16)
+        gate += jnp.sum(act * pulled, axis=1, keepdims=True)
+        act = act.astype(bf16)
+        grads[q, :hidden, :] = dot(d_pre, rows[:, :model], 0, 0).astype(bf16)
+        grads[q, hidden:, :] = dot(act, rows[:, model:], 0, 0).astype(bf16)
+        stores[q].start()
+        part = dot(d_pre, weights[q, :hidden, :], 1, 0)
+        if q < 3:
+            total[...] = part if q == 0 else total[...] + part
+        else:
+            dx_ref[...] = (total[...] + part).astype(bf16)
+    gate_ref[...] = jnp.broadcast_to(gate, gate_ref.shape)
+    for store in stores:
+        store.wait()
+
+
+def run_experts(rows, blocks):
+    slots, model = rows.shape[0], rows.shape[1] // 2
+    anywhere = pl.BlockSpec(memory_space=pl.ANY)
+    vmem = pl.BlockSpec(memory_space=pltpu.VMEM)
+    block = jax.ShapeDtypeStruct(blocks[0].shape, bf16)
+    flops = 4 * 5 * 2 * slots * model * (blocks[0].shape[0] // 2)
+    return pl.pallas_call(
+        experts_kernel,
+        out_shape=(block,) * 4
+        + (
+            jax.ShapeDtypeStruct((slots, model), bf16),
+            jax.ShapeDtypeStruct((slots, LANES), f32),
+        ),
+        in_specs=[anywhere] * 5,
+        out_specs=(anywhere,) * 4 + (vmem, vmem),
+        scratch_shapes=[
+            pltpu.VMEM(rows.shape, bf16),
+            pltpu.VMEM((4,) + blocks[0].shape, bf16),
+            pltpu.VMEM((4,) + blocks[0].shape, bf16),
+            pltpu.VMEM((slots, model), f32),
+            pltpu.SemaphoreType.DMA((5,)),
+            pltpu.SemaphoreType.DMA((4,)),
+        ],
+        cost_estimate=pl.CostEstimate(
+            flops=flops, bytes_accessed=2 * (rows.size + 8 * blocks[0].size), transcendentals=0
+        ),
+        name="experts",
+    )(rows, *blocks)
+
+
+def exchange(x, groups):
+    return lax.all_to_all(
+        x, AXES, split_axis=0, concat_axis=0, axis_index_groups=groups, tiled=True
+    )
+
+
+def on_device(groups, tokens, d_out, expert_ids, gate_weights, w_in, w_out):
     tok_rows, model = tokens.shape
     width = model // LANES
-    experts = lax.axis_size("dp") * lax.axis_size("yh")
+    experts = len(groups[0])
     slots = 2 * experts
-    own_in, own_out = w_in[0], w_out[0]
-    hidden = own_out.shape[0]
-    oth = lax.ppermute(jnp.concatenate([own_in.T, own_out], axis=0), "yl", SWAP)
+    own = jnp.concatenate([w_in[0].T, w_out[0]], axis=0)
+    hidden = own.shape[0] // 2
+    oth = lax.ppermute(own, "yl", SWAP)
     outgoing, target = dispatch(
         expert_ids,
         gate_weights,
@@ -128,54 +204,46 @@
         d_out.reshape(tok_rows, width, LANES),
         experts,
     )
-    outgoing = outgoing.reshape(experts, 4 * width, LANES)
-    arrived = lax.all_to_all(outgoing, ROUTE, split_axis=0, concat_axis=0, tiled=True)
-    arrived, oth = lax.optimization_barrier((arrived, hold(oth, HOLD_FLOPS)))
-    oth_in, oth_out = oth[:hidden], oth[hidden:]
-    mine = arrived.reshape(slots, 2 * model)
-    theirs = lax.ppermute(mine, "core", SWAP)
-    rows = jnp.concatenate([mine, theirs], axis=0)
-    rows_x, rows_g = rows[:, :model], rows[:, model:]
-
-    def quarter(first, second, depth):
-        preact = dot(rows_x, first, 1, depth)
-        pulled = dot(rows_g, second, 1, 1)
-        sig = jax.nn.sigmoid(preact)
-        act = preact * sig
-        d_pre = (pulled * sig * (1.0 + preact * (1.0 - sig))).astype(bf16)
-        gate = jnp.sum(act * pulled, axis=1, keepdims=True)
-        return d_pre, act.astype(bf16), gate
-
-    dp_own, act_own, gate_own = quarter(own_in, own_out, 0)
-    dp_oth, act_oth, gate_oth = quarter(oth_in, oth_out, 1)
-    far = jnp.concatenate([dot(dp_oth, rows_x, 0, 0), dot(act_oth, rows_g, 0, 0)], axis=0).astype(bf16)
-    came = lax.ppermute(far, "yl", SWAP)
-    dx = dot(dp_own, own_in, 1, 1) + dot(dp_oth, oth_in, 1, 0)
-    gate = gate_own + gate_oth
-    dx_peer = lax.ppermute(dx[slots:].astype(bf16), "core", SWAP)
-    gate_peer = lax.ppermute(gate[slots:], "core", SWAP)
-    dx_sum = (dx[:slots] + dx_peer.astype(f32)).astype(bf16)
-    gate_sum = gate[:slots] + gate_peer
-    gate_high = gate_sum.astype(bf16)
-    gate_low = (gate_sum - gate_high.astype(f32)).astype(bf16)
-    gate_rows = jnp.concatenate([gate_high, gate_low], axis=1).reshape(experts, 4, 1)
+    arrived = exchange(outgoing.reshape(experts, 4 * width, LANES), groups)
+    oth = hold(oth, HOLD_FLOPS)
+    own, oth = lax.optimization_barrier((own, oth))
+    blocks = [own, lax.ppermute(own, "core", SWAP), oth, lax.ppermute(oth, "core", SWAP)]
+    arrived, *blocks = lax.optimization_barrier((arrived, *blocks))
+    rows = arrived.reshape(slots, 2 * model)
+    own_grad, peer_grad, far_own, far_peer, dx, gate = run_experts(rows, blocks)
+    gate_high = gate.astype(bf16)
+    gate_low = (gate - gate_high.astype(f32)).astype(bf16)
+    gate_rows = jnp.stack([gate_high, gate_low], axis=1).reshape(experts, 4, LANES)
     gate_rows = jnp.pad(gate_rows, ((0, 0), (0, GATE_ROWS - 4), (0, 0)))
-    gate_rows = jnp.broadcast_to(gate_rows, (experts, GATE_ROWS, LANES))
-    back = jnp.concatenate([dx_sum.reshape(experts, 2 * width, LANES), gate_rows], axis=1)
-    returned = lax.all_to_all(back, ROUTE, split_axis=0, concat_axis=0, tiled=True)
-    d_tok3, gate_rows = combine(target, returned, tok_rows, width)
-    d_gates = gate_rows[:, :TOPK] / gate_weights
-    d_first = (dot(rows_x, dp_own, 0, 0) + came[:hidden].T.astype(f32)).astype(bf16)
-    d_second = (dot(act_own, rows_g, 0, 0) + came[hidden:].astype(f32)).astype(bf16)
+    back = jnp.concatenate([dx.reshape(experts, 2 * width, LANES), gate_rows], axis=1)
+    far_peer, back = lax.optimization_barrier((lax.ppermute(far_peer, "core", SWAP), back))
+    far = (far_own.astype(f32) + far_peer.astype(f32)).astype(bf16)
+    came = hold(lax.ppermute(far, "yl", SWAP), HOLD_FLOPS)
+    back, peer_grad, _ = lax.optimization_barrier((back, peer_grad, far))
+    near_peer = lax.ppermute(peer_grad, "core", SWAP)
+    returned = exchange(back, groups)
+    total = own_grad.astype(f32) + near_peer.astype(f32) + came.astype(f32)
+    d_first, d_second = total[:hidden].T.astype(bf16), total[hidden:].astype(bf16)
+    returned, d_first, d_second = lax.optimization_barrier((returned, d_first, d_second))
+    d_tok3, gate_sums = combine(target, returned, tok_rows, width)
+    d_gates = gate_sums[:, :TOPK] / gate_weights
     return (d_tok3.reshape(tok_rows, model), d_gates, d_first[None], d_second[None])
 
 
 def solution(mesh):
     dp, expert = mesh.devices.shape
-    fine = Mesh(np.asarray(mesh.devices).reshape(dp, expert // 4, 2, 2), AXES)
+    pairs = expert // 4
+    fine = Mesh(np.asarray(mesh.devices).reshape(dp, pairs, 2, 2), AXES)
+    number = np.arange(dp * expert).reshape(dp, pairs, 2, 2)
+    near = np.arange(pairs) >= pairs // 2
+    groups = [
+        [int(number[i, k, int(near[k]) ^ side, c]) for i in range(dp) for k in range(pairs)]
+        for side in range(2)
+        for c in range(2)
+    ]
     flat, block = P(AXES, None), P(AXES, None, None)
     return jax.shard_map(
-        on_device,
+        functools.partial(on_device, groups),
         mesh=fine,
         in_specs=(flat, flat, flat, flat, block, block),
         out_specs=(flat, flat, block, block),

time: 228 us -> 209 us (0.917)
  the two profiles are of different devices: /device:TPU:6 before, /device:TPU:8 now
where the time goes in v2:
time: 209 us; the launch traced here: 208 us
  waiting for transfers between devices  121 us (58%)
  starting transfers between devices  41.7 us (20%)
  Pallas kernels  17.9 us (9%)
  local copies, waits for them, and re-layouts  14.3 us (7%)
  other arithmetic  12.3 us (6%)
    ppermute x1, waiting for transfers between devices, on_device(): came = hold(lax.ppermute(far, 'yl', SWAP), HOLD_FLOPS)  48.6 us
    ppermute x1, waiting for transfers between devices, on_device(): oth = lax.ppermute(own, 'yl', SWAP)  47.2 us
    all_to_all x2, waiting for transfers between devices, exchange(): lax.all_to_all(x, AXES, split_axis=0, concat_axis=0, axis_index_groups=gr...  25.1 us
    all_to_all x2, starting transfers between devices, exchange(): lax.all_to_all(x, AXES, split_axis=0, concat_axis=0, axis_index_groups=gr...  23.9 us
    pallas_call x1, Pallas kernels, run_experts(): pl.pallas_call(experts_kernel, out_shape=(block,) * 4 + (jax.ShapeDtypeSt...  11.5 us
    unnamed x24, local copies, waits for them, and re-layouts  8.96 us
    ppermute x1, starting transfers between devices, on_device(): oth = lax.ppermute(own, 'yl', SWAP)  7.72 us
  transfers between devices with their start and end apart: 8, of which 5 were waited for; matrix products, arithmetic and copies ran while one was open for 6% of the time, Pallas kernels for 2%

profile of v2, /device:TPU:8, one launch (start us, length us, event | category | flops | bytes accessed | tf_op | source)
XLA Modules:
  0.0 208.1 jit_solution(10139495003142798197)
XLA Ops:
  0.6 0.0 copy-start.2
  0.6 1.6 copy.14
  2.2 0.0 copy-done.2
  2.2 0.0 copy-start.6
  2.2 0.0 copy-start.7
  2.3 0.0 copy-start.4
  2.3 0.0 copy-start.5
  2.3 1.5 pad_maximum_fusion.w0
  3.8 7.7 %collective-permute-start = (bf16[512,2048]{1,0:T(8,128)(2,1)}, bf16[512,2048]{1,0:T(8,128)(2,1)}, u32[]{:S(2)}, u32[]{:S(2)}) collective-permute-start(bf16[512,2048]{1,0:T(8,128)(2,1)} %pad_maximum_fusion.w0), channel_id=1, source_target_pairs={{0,2},{2,0},{1,3},{3,1},{4,6},{6,4},{5,7},{7,5},{8,10},{10,8},{9,1... | collective-permute-start | bytes 6291464 | tf_op jit(solution)/shard_map/ppermute | solution.py:199
  11.5 0.0 copy-done.6
  11.5 0.7 copy.13.gates_ref
  12.2 0.0 copy-done.7
  12.2 0.7 copy.12.ids_ref
  12.9 0.0 copy-done.4
  12.9 0.7 copy.19
  13.6 0.0 copy-done.5
  13.6 0.7 copy.20
  14.2 3.7 %dispatch.1 = (bf16[256,32,128]{2,1,0:T(8,128)(2,1)}, s32[32,4]{1,0:T(8,128)}) custom-call(s32[32,4]{1,0:T(8,128)} %copy.12.ids_ref, f32[32,4]{1,0:T(8,128)} %copy.13.gates_ref, bf16[32,16,128]{2,1,0:T(8,128)(2,1)} %bitcast.28, bf16[32,16,128]{2,1,0:T(8,128)(2,1)} %bitcast.29), custom_call_target="tpu_custom_call" | custom-call | tf_op jit(solution)/shard_map/dispatch/pallas_call | solution.py:51
  17.9 14.1 %all-to-all-start = ((bf16[128,64,128]{2,1,0:T(8,128)(2,1)}), bf16[128,64,128]{2,1,0:T(8,128)(2,1)S(1)}, u32[]{:S(2)}, u32[]{:S(2)}) async-start(bf16[128,64,128]{2,1,0:T(8,128)(2,1)} %bitcast.24), calls=%async_computation | async-start | bytes 4194304 | tf_op jit(solution)/shard_map/all_to_all | solution.py:187
  32.1 47.2 %collective-permute-done.x_ref = bf16[512,2048]{1,0:T(8,128)(2,1)} collective-permute-done((bf16[512,2048]{1,0:T(8,128)(2,1)}, bf16[512,2048]{1,0:T(8,128)(2,1)}, u32[]{:S(2)}, u32[]{:S(2)}) %collective-permute-start) | collective-permute-done | bytes 2097184 | tf_op jit(solution)/shard_map/ppermute | solution.py:199
  79.2 1.9 collective-permute-start.1
  81.2 2.4 %collective-permute-start.2 = (bf16[512,2048]{1,0:T(8,128)(2,1)}, bf16[512,2048]{1,0:T(8,128)(2,1)}, u32[]{:S(2)}, u32[]{:S(2)}) collective-permute-start(bf16[512,2048]{1,0:T(8,128)(2,1)} %hold.2.w2), channel_id=1, source_target_pairs={{0,1},{1,0},{2,3},{3,2},{4,5},{5,4},{6,7},{7,6},{8,9},{9,8},{10,11... | collective-permute-start | bytes 6291464 | tf_op jit(solution)/shard_map/ppermute | solution.py:210
  83.6 17.9 %all-to-all-done = bf16[128,64,128]{2,1,0:T(8,128)(2,1)S(1)} async-done(((bf16[128,64,128]{2,1,0:T(8,128)(2,1)}), bf16[128,64,128]{2,1,0:T(8,128)(2,1)S(1)}, u32[]{:S(2)}, u32[]{:S(2)}) %all-to-all-start) | async-done | bytes 2097184 | tf_op jit(solution)/shard_map/all_to_all | solution.py:187
  101.5 0.0 collective-permute-done.1.w1
  101.5 0.0 collective-permute-done.2.w3
  101.5 2.3 %reshape.32.rows_hbm = bf16[256,4096]{1,0:T(8,128)(2,1)} reshape(bf16[128,64,128]{2,1,0:T(8,128)(2,1)S(1)} %all-to-all-done) | data formatting | bytes 4194304 | tf_op jit(solution)/shard_map/reshape | solution.py:212
  103.8 11.5 %experts.1 = (bf16[512,2048]{1,0:T(8,128)(2,1)}, bf16[512,2048]{1,0:T(8,128)(2,1)}, bf16[512,2048]{1,0:T(8,128)(2,1)}, bf16[512,2048]{1,0:T(8,128)(2,1)}, bf16[256,2048]{1,0:T(8,128)(2,1)}, /*index=5*/f32[256,128]{1,0:T(8,128)}) custom-call(bf16[256,4096]{1,0:T(8,128)(2,1)} %reshape.32.rows_hbm, bf16[512,2048]{1,0:T(8,128)(2,1)} %pad_maximum_fusion.w0, ...), custom_call_target="tpu_custom_call" | custom-call | flops 5368709120 | bytes 18874368 | tf_op jit(solution)/shard_map/experts/pallas_call | solution.py:162
  115.3 1.9 collective-permute-start.3
  117.2 1.0 convert_bitcast_fusion
  118.2 0.1 copy.15
  118.4 0.0 copy-start.1
  118.4 1.7 reshape.33
  120.1 1.2 fusion.1
  121.3 0.3 collective-permute-done.3
  121.7 0.0 copy-done.1
  121.7 3.7 %add_convert_fusion.1 = bf16[512,2048]{1,0:T(8,128)(2,1)} fusion(bf16[512,2048]{1,0:T(8,128)(2,1)} %collective-permute-done.3, bf16[512,2048]{1,0:T(8,128)(2,1)S(1)} %copy-done.1), kind=kLoop, calls=%fused_computation.1 | loop fusion | flops 4194304 | bytes 6291456 | tf_op jit(solution)/shard_map/convert_element_type | solution.py:220
  125.4 1.9 collective-permute-start.5
  127.3 9.7 %all-to-all-start.1 = ((bf16[128,40,128]{2,1,0:T(8,128)(2,1)}), bf16[128,40,128]{2,1,0:T(8,128)(2,1)S(1)}, u32[]{:S(2)}, u32[]{:S(2)}) async-start(bf16[128,40,128]{2,1,0:T(8,128)(2,1)} %fusion.1), calls=%async_computation.1 | async-start | bytes 2621440 | tf_op jit(solution)/shard_map/all_to_all | solution.py:187
  137.1 1.9 collective-permute-start.4
  139.0 48.6 %collective-permute-done.5.x_ref = bf16[512,2048]{1,0:T(8,128)(2,1)} collective-permute-done((bf16[512,2048]{1,0:T(8,128)(2,1)}, bf16[512,2048]{1,0:T(8,128)(2,1)}, u32[]{:S(2)}, u32[]{:S(2)}) %collective-permute-start.5) | collective-permute-done | bytes 2097184 | tf_op jit(solution)/shard_map/ppermute | solution.py:221
  187.6 0.0 collective-permute-done.4
  187.6 4.1 %add_convert_fusion = bf16[512,2048]{1,0:T(8,128)(2,1)S(1)} fusion(bf16[512,2048]{1,0:T(8,128)(2,1)} %hold.3, bf16[512,2048]{1,0:T(8,128)(2,1)} %collective-permute-done.4, bf16[512,2048]{1,0:T(8,128)(2,1)} %get-tuple-element.45), kind=kLoop, calls=%fused_computation | loop fusion | flops 6291456 | bytes 8388608 | tf_op jit(solution)/shard_map/convert.1
  191.7 0.0 copy-start.3
  191.7 1.2 fusion.3
  192.9 7.1 %all-to-all-done.1.back_ref = bf16[128,40,128]{2,1,0:T(8,128)(2,1)S(1)} async-done(((bf16[128,40,128]{2,1,0:T(8,128)(2,1)}), bf16[128,40,128]{2,1,0:T(8,128)(2,1)S(1)}, u32[]{:S(2)}, u32[]{:S(2)}) %all-to-all-start.1) | async-done | bytes 1310752 | tf_op jit(solution)/shard_map/all_to_all | solution.py:187
  200.0 0.0 copy-start
  200.0 1.1 copy-done
  201.1 2.7 %combine.1 = (bf16[32,16,128]{2,1,0:T(8,128)(2,1)}, f32[32,128]{1,0:T(8,128)}) custom-call(s32[32,4]{1,0:T(8,128)} %get-tuple-element.28.target_ref, bf16[128,40,128]{2,1,0:T(8,128)(2,1)} %copy-done), custom_call_target="tpu_custom_call" | custom-call | tf_op jit(solution)/shard_map/combine/pallas_call | solution.py:101
  203.8 1.6 copy.23
  205.4 0.0 copy-done.3
  205.4 0.7 slice_divide_fusion
  206.1 0.7 copy.17
  206.8 1.3 copy.18
  (3 shorter events, 0.0 us)
Async XLA Ops:
  0.6 1.6 copy-start.2
  2.2 9.3 %copy-start.6 = (f32[32,4]{0,1:T(4,128)S(1)}, f32[32,4]{0,1:T(4,128)}, u32[]{:S(2)}) copy-start(f32[32,4]{0,1:T(4,128)} %param.9) | copy-start | bytes 1540
  2.2 9.9 %copy-start.7 = (s32[32,4]{0,1:T(4,128)S(1)}, s32[32,4]{0,1:T(4,128)}, u32[]{:S(2)}) copy-start(s32[32,4]{0,1:T(4,128)} %param.8) | copy-start | bytes 1540
  2.3 10.6 %copy-start.4 = (bf16[32,2048]{1,0:T(8,128)(2,1)S(1)}, bf16[32,2048]{1,0:T(8,128)(2,1)}, u32[]{:S(2)}) copy-start(bf16[32,2048]{1,0:T(8,128)(2,1)} %param.6) | copy-start | bytes 393220
  2.3 11.3 %copy-start.5 = (bf16[32,2048]{1,0:T(8,128)(2,1)S(1)}, bf16[32,2048]{1,0:T(8,128)(2,1)}, u32[]{:S(2)}) copy-start(bf16[32,2048]{1,0:T(8,128)(2,1)} %param.7) | copy-start | bytes 393220
  3.8 75.5 %collective-permute-start = (bf16[512,2048]{1,0:T(8,128)(2,1)}, bf16[512,2048]{1,0:T(8,128)(2,1)}, u32[]{:S(2)}, u32[]{:S(2)}) collective-permute-start(bf16[512,2048]{1,0:T(8,128)(2,1)} %pad_maximum_fusion.w0), channel_id=1, source_target_pairs={{0,2},{2,0},{1,3},{3,1},{4,6},{6,4},{5,7},{7,5},{8,10},{10,8},{9,1... | collective-permute-start | bytes 6291464 | tf_op jit(solution)/shard_map/ppermute | solution.py:199
  17.9 83.5 %all-to-all-start = ((bf16[128,64,128]{2,1,0:T(8,128)(2,1)}), bf16[128,64,128]{2,1,0:T(8,128)(2,1)S(1)}, u32[]{:S(2)}, u32[]{:S(2)}) async-start(bf16[128,64,128]{2,1,0:T(8,128)(2,1)} %bitcast.24), calls=%async_computation | async-start | bytes 4194304 | tf_op jit(solution)/shard_map/all_to_all | solution.py:187
  79.2 22.2 %collective-permute-start.1 = (bf16[512,2048]{1,0:T(8,128)(2,1)}, bf16[512,2048]{1,0:T(8,128)(2,1)}, u32[]{:S(2)}, u32[]{:S(2)}) collective-permute-start(bf16[512,2048]{1,0:T(8,128)(2,1)} %pad_maximum_fusion.w0), channel_id=1, source_target_pairs={{0,1},{1,0},{2,3},{3,2},{4,5},{5,4},{6,7},{7,6},{8,9},{9,8},{10,11... | collective-permute-start | bytes 6291464 | tf_op jit(solution)/shard_map/ppermute | solution.py:210
  81.2 20.3 %collective-permute-start.2 = (bf16[512,2048]{1,0:T(8,128)(2,1)}, bf16[512,2048]{1,0:T(8,128)(2,1)}, u32[]{:S(2)}, u32[]{:S(2)}) collective-permute-start(bf16[512,2048]{1,0:T(8,128)(2,1)} %hold.2.w2), channel_id=1, source_target_pairs={{0,1},{1,0},{2,3},{3,2},{4,5},{5,4},{6,7},{7,6},{8,9},{9,8},{10,11... | collective-permute-start | bytes 6291464 | tf_op jit(solution)/shard_map/ppermute | solution.py:210
  115.3 6.4 %collective-permute-start.3 = (bf16[512,2048]{1,0:T(8,128)(2,1)}, bf16[512,2048]{1,0:T(8,128)(2,1)}, u32[]{:S(2)}, u32[]{:S(2)}) collective-permute-start(bf16[512,2048]{1,0:T(8,128)(2,1)} %get-tuple-element.37), channel_id=1, source_target_pairs={{0,1},{1,0},{2,3},{3,2},{4,5},{5,4},{6,7},{7,6},{8,9},{9,8},{10,11... | collective-permute-start | bytes 6291464 | tf_op jit(solution)/shard_map/ppermute | solution.py:219
  118.4 3.3 %copy-start.1 = (bf16[512,2048]{1,0:T(8,128)(2,1)S(1)}, bf16[512,2048]{1,0:T(8,128)(2,1)}, u32[]{:S(2)}) copy-start(bf16[512,2048]{1,0:T(8,128)(2,1)} %get-tuple-element.42) | copy-start | bytes 6291460
  125.4 62.2 %collective-permute-start.5 = (bf16[512,2048]{1,0:T(8,128)(2,1)}, bf16[512,2048]{1,0:T(8,128)(2,1)}, u32[]{:S(2)}, u32[]{:S(2)}) collective-permute-start(bf16[512,2048]{1,0:T(8,128)(2,1)} %add_convert_fusion.1), channel_id=1, source_target_pairs={{0,2},{2,0},{1,3},{3,1},{4,6},{6,4},{5,7},{7,5},{8,10},{10,8},{9,1... | collective-permute-start | bytes 6291464 | tf_op jit(solution)/shard_map/ppermute | solution.py:221
  127.3 72.7 %all-to-all-start.1 = ((bf16[128,40,128]{2,1,0:T(8,128)(2,1)}), bf16[128,40,128]{2,1,0:T(8,128)(2,1)S(1)}, u32[]{:S(2)}, u32[]{:S(2)}) async-start(bf16[128,40,128]{2,1,0:T(8,128)(2,1)} %fusion.1), calls=%async_computation.1 | async-start | bytes 2621440 | tf_op jit(solution)/shard_map/all_to_all | solution.py:187
  137.1 50.5 %collective-permute-start.4 = (bf16[512,2048]{1,0:T(8,128)(2,1)}, bf16[512,2048]{1,0:T(8,128)(2,1)}, u32[]{:S(2)}, u32[]{:S(2)}) collective-permute-start(bf16[512,2048]{1,0:T(8,128)(2,1)} %get-tuple-element.46), channel_id=1, source_target_pairs={{0,1},{1,0},{2,3},{3,2},{4,5},{5,4},{6,7},{7,6},{8,9},{9,8},{10,11... | collective-permute-start | bytes 6291464 | tf_op jit(solution)/shard_map/ppermute | solution.py:223
  191.7 13.7 %copy-start.3 = (f32[32,4]{1,0:T(8,128)S(1)}, f32[32,4]{1,0:T(8,128)}, u32[]{:S(2)}) copy-start(f32[32,4]{1,0:T(8,128)} %copy.13.gates_ref) | copy-start | bytes 1540
  200.0 1.1 copy-start

commit v3 on v2

v3 whole, which is shorter than its diff:
```python
import functools

import jax
import jax.numpy as jnp
import numpy as np
from jax import lax
from jax.experimental import pallas as pl
from jax.experimental.pallas import tpu as pltpu
from jax.sharding import Mesh
from jax.sharding import PartitionSpec as P

TOPK = 4
LANES = 128
AXES = ("dp", "yh", "yl", "core")
GATE_ROWS = 8
HOLD_FLOPS = int(3e10)
SWAP = [(0, 1), (1, 0)]
f32, bf16 = jnp.float32, jnp.bfloat16


def dispatch_kernel(ids_ref, gates_ref, tok_ref, dout_ref, out_ref, target_ref, count_ref):
    tokens, width = tok_ref.shape[0], tok_ref.shape[1]
    out_ref[...] = jnp.zeros_like(out_ref)

    def clear(i, carry):
        count_ref[i] = 0
        return carry

    lax.fori_loop(0, count_ref.shape[0], clear, 0, unroll=8)

    def place(t, carry):
        row = tok_ref[t]
        grad = dout_ref[t].astype(f32)
        for k in range(TOPK):
            e = ids_ref[t, k]
            slot = count_ref[e]
            count_ref[e] = slot + 1
            at = 2 * e + slot
            target_ref[t, k] = at
            out_ref[at, 0:width, :] = row
            out_ref[at, width : 2 * width, :] = (grad * gates_ref[t, k]).astype(bf16)
        return carry

    lax.fori_loop(0, tokens, place, 0)


def dispatch(ids, gates, tok3, dout3, experts):
    tokens, width, _ = tok3.shape
    smem = pl.BlockSpec(memory_space=pltpu.SMEM)
    vmem = pl.BlockSpec(memory_space=pltpu.VMEM)
    return pl.pallas_call(
        dispatch_kernel,
        out_shape=(
            jax.ShapeDtypeStruct((2 * experts, 2 * width, LANES), bf16),
            jax.ShapeDtypeStruct((tokens, TOPK), jnp.int32),
        ),
        in_specs=[smem, smem, vmem, vmem],
        out_specs=(vmem, smem),
        scratch_shapes=[pltpu.SMEM((experts,), jnp.int32)],
        name="dispatch",
    )(ids, gates, tok3, dout3)


def hold(x, flops):
    anywhere = pl.BlockSpec(memory_space=pl.ANY)
    return pl.pallas_call(
        lambda x_ref, y_ref: None,
        out_shape=jax.ShapeDtypeStruct(x.shape, x.dtype),
        in_specs=[anywhere],
        out_specs=anywhere,
        input_output_aliases={0: 0},
        cost_estimate=pl.CostEstimate(flops=flops, bytes_accessed=0, transcendentals=0),
        name="hold",
    )(x)


def combine_kernel(target_ref, back_ref, gates_ref, dx_ref, gate_ref, dx_rows, gate_rows):
    tokens, model = dx_ref.shape
    width = model // LANES
    lane = lax.broadcasted_iota(jnp.int32, (1, LANES), 1)

    def total(t, carry):
        acc = jnp.zeros((width, LANES), f32)
        gate = jnp.zeros((1, LANES), f32)
        for k in range(TOPK):
            at = target_ref[t, k]
            e, slot = lax.shift_right_logical(at, 1), lax.bitwise_and(at, 1)
            first = pl.multiple_of(slot * width, width)
            acc += back_ref[e, pl.ds(first, width), :].astype(f32)
            extra = back_ref[e, 2 * width : 2 * width + GATE_ROWS, :].astype(f32)
            pair = jnp.where(slot == 0, extra[0:2, :], extra[2:4, :])
            gate = jnp.where(lane == k, pair[0:1, :] + pair[1:2, :], gate)
        dx_rows[pl.ds(pl.multiple_of(t * width, width), width), :] = acc
        gate_rows[pl.ds(t, 1), :] = gate
        return carry

    lax.fori_loop(0, tokens, total, 0)
    for j in range(width):
        part = dx_rows[pl.ds(j, tokens, stride=width), :]
        dx_ref[:, j * LANES : (j + 1) * LANES] = part.astype(bf16)
    gate_ref[...] = gate_rows[:, :TOPK] / gates_ref[...]


def combine(target, back, gates, model):
    tokens = gates.shape[0]
    vmem = pl.BlockSpec(memory_space=pltpu.VMEM)
    return pl.pallas_call(
        combine_kernel,
        out_shape=(
            jax.ShapeDtypeStruct((tokens, model), bf16),
            jax.ShapeDtypeStruct(gates.shape, f32),
        ),
        in_specs=[pl.BlockSpec(memory_space=pltpu.SMEM), vmem, vmem],
        out_specs=(vmem, vmem),
        scratch_shapes=[
            pltpu.VMEM((tokens * model // LANES, LANES), f32),
            pltpu.VMEM((tokens, LANES), f32),
        ],
        name="combine",
    )(target, back, gates)


def dot(a, b, ca, cb):
    return lax.dot_general(a, b, (((ca,), (cb,)), ((), ())), preferred_element_type=f32)


def expert_half(rows_hbm, blocks, stores_to, rows, ins, outs, grads, total, in_sems, out_sems):
    hidden, model = outs.shape[1], outs.shape[2]
    loads = [pltpu.make_async_copy(rows_hbm, rows, in_sems.at[0])]
    for q in range(2):
        loads.append(pltpu.make_async_copy(blocks[2 * q], ins.at[q], in_sems.at[1 + 2 * q]))
        loads.append(pltpu.make_async_copy(blocks[2 * q + 1], outs.at[q], in_sems.at[2 + 2 * q]))
    stores = [
        pltpu.make_async_copy(grads.at[q], g, out_sems.at[q]) for q, g in enumerate(stores_to)
    ]
    for load in loads:
        load.start()
    loads[0].wait()
    gate = jnp.zeros((rows.shape[0], 1), f32)
    for q in range(2):
        loads[1 + 2 * q].wait()
        loads[2 + 2 * q].wait()
        preact = dot(rows[:, :model], ins[q], 1, 0)
        pulled = dot(rows[:, model:], outs[q], 1, 1)
        sig = jax.nn.sigmoid(preact)
        act = preact * sig
        d_pre = (pulled * sig * (1.0 + preact * (1.0 - sig))).astype(bf16)
        gate += jnp.sum(act * pulled, axis=1, keepdims=True)
        act = act.astype(bf16)
        grads[q, :hidden, :] = dot(d_pre, rows[:, :model], 0, 0).astype(bf16)
        grads[q, hidden:, :] = dot(act, rows[:, model:], 0, 0).astype(bf16)
        stores[q].start()
        total[...] += dot(d_pre, ins[q], 1, 1)
    return gate, stores


def far_kernel(rows_hbm, i0, o0, i1, o1, g0, g1, dx_ref, gate_ref, *scratch):
    dx_ref[...] = jnp.zeros_like(dx_ref)
    rows, ins, outs, grads, in_sems, out_sems = scratch
    gate, stores = expert_half(
        rows_hbm, (i0, o0, i1, o1), (g0, g1), rows, ins, outs, grads, dx_ref, in_sems, out_sems
    )
    gate_ref[...] = jnp.broadcast_to(gate, gate_ref.shape)
    for store in stores:
        store.wait()


def near_kernel(
    rows_hbm, i0, o0, i1, o1, dx_in, gate_in, g0, g1, back_ref, rows, ins, outs, grads, total, lines, in_sems, out_sems
):
    slots, model = total.shape
    width = model // LANES
    total[...] = dx_in[...]
    gate, stores = expert_half(
        rows_hbm, (i0, o0, i1, o1), (g0, g1), rows, ins, outs, grads, total, in_sems, out_sems
    )
    for j in range(width):
        lines[pl.ds(j, slots, stride=width), :] = total[:, j * LANES : (j + 1) * LANES]
    experts = slots // 2
    back_ref[:, : 2 * width, :] = lines[...].astype(bf16).reshape(experts, 2 * width, LANES)
    gate = gate_in[...] + gate
    high = gate.astype(bf16)
    low = (gate - high.astype(f32)).astype(bf16)
    row = lax.broadcasted_iota(jnp.int32, (experts * GATE_ROWS, slots), 0)
    slot = lax.broadcasted_iota(jnp.int32, (experts * GATE_ROWS, slots), 1)
    place = row - (slot >> 1) * GATE_ROWS - 2 * (slot & 1)
    spread = dot((place == 0).astype(bf16), high, 1, 0) + dot((place == 1).astype(bf16), low, 1, 0)
    back_ref[:, 2 * width :, :] = spread.astype(bf16).reshape(experts, GATE_ROWS, LANES)
    for store in stores:
        store.wait()


def run_experts(rows, blocks, carried=None):
    slots, model = rows.shape[0], rows.shape[1] // 2
    hidden = blocks[1].shape[0]
    width = model // LANES
    anywhere = pl.BlockSpec(memory_space=pl.ANY)
    vmem = pl.BlockSpec(memory_space=pltpu.VMEM)
    grad = jax.ShapeDtypeStruct((2 * hidden, model), bf16)
    scratch = [
        pltpu.VMEM(rows.shape, bf16),
        pltpu.VMEM((2, model, hidden), bf16),
        pltpu.VMEM((2, hidden, model), bf16),
        pltpu.VMEM((2, 2 * hidden, model), bf16),
    ]
    sems = [pltpu.SemaphoreType.DMA((5,)), pltpu.SemaphoreType.DMA((2,))]
    cost = pl.CostEstimate(
        flops=2 * 5 * 2 * slots * model * hidden,
        bytes_accessed=2 * (rows.size + 12 * hidden * model),
        transcendentals=0,
    )
    if carried is None:
        return pl.pallas_call(
            far_kernel,
            out_shape=(
                grad,
                grad,
                jax.ShapeDtypeStruct((slots, model), f32),
                jax.ShapeDtypeStruct((slots, LANES), f32),
            ),
            in_specs=[anywhere] * 5,
            out_specs=(anywhere, anywhere, vmem, vmem),
            scratch_shapes=scratch + sems,
            cost_estimate=cost,
            name="far_quarters",
        )(rows, *blocks)
    return pl.pallas_call(
        near_kernel,
        out_shape=(
            grad,
            grad,
            jax.ShapeDtypeStruct((slots // 2, 2 * width + GATE_ROWS, LANES), bf16),
        ),
        in_specs=[anywhere] * 5 + [vmem, vmem],
        out_specs=(anywhere, anywhere, vmem),
        scratch_shapes=scratch
        + [pltpu.VMEM((slots, model), f32), pltpu.VMEM((slots * width, LANES), f32)]
        + sems,
        cost_estimate=cost,
        name="near_quarters",
    )(rows, *blocks, *carried)


def finish_kernel(own_ref, peer_ref, came_ref, first_ref, second_ref):
    hidden = second_ref.shape[0]
    total = own_ref[...].astype(f32) + peer_ref[...].astype(f32) + came_ref[...].astype(f32)
    first_ref[...] = total[:hidden, :].T.astype(bf16)
    second_ref[...] = total[hidden:, :].astype(bf16)


def finish(own, peer, came):
    hidden, model = own.shape[0] // 2, own.shape[1]
    part = pl.BlockSpec((2 * hidden, 512), lambda j: (0, j))
    return pl.pallas_call(
        finish_kernel,
        grid=(model // 512,),
        out_shape=(
            jax.ShapeDtypeStruct((model, hidden), bf16),
            jax.ShapeDtypeStruct((hidden, model), bf16),
        ),
        in_specs=[part] * 3,
        out_specs=(
            pl.BlockSpec((512, hidden), lambda j: (j, 0)),
            pl.BlockSpec((hidden, 512), lambda j: (0, j)),
        ),
        name="finish",
    )(own, peer, came)


def exchange(x, groups):
    return lax.all_to_all(
        x, AXES, split_axis=0, concat_axis=0, axis_index_groups=groups, tiled=True
    )


def on_device(groups, tokens, d_out, expert_ids, gate_weights, w_in, w_out):
    tok_rows, model = tokens.shape
    width = model // LANES
    experts = len(groups[0])
    slots = 2 * experts
    own_in, own_out = w_in[0], w_out[0]
    oth_in = lax.ppermute(own_in, "yl", SWAP)
    oth_out = lax.ppermute(own_out, "yl", SWAP)
    outgoing, target = dispatch(
        expert_ids,
        gate_weights,
        tokens.reshape(tok_rows, width, LANES),
        d_out.reshape(tok_rows, width, LANES),
        experts,
    )
    arrived = exchange(outgoing.reshape(experts, 4 * width, LANES), groups)
    own_in, own_out, oth_in = lax.optimization_barrier((own_in, own_out, hold(oth_in, HOLD_FLOPS)))
    oth_out = hold(oth_out, HOLD_FLOPS)
    near = [own_in, own_out, lax.ppermute(own_in, "core", SWAP), lax.ppermute(own_out, "core", SWAP)]
    far = [oth_in, oth_out, lax.ppermute(oth_in, "core", SWAP), lax.ppermute(oth_out, "core", SWAP)]
    arrived, *blocks = lax.optimization_barrier((arrived, *near, *far))
    rows = arrived.reshape(slots, 2 * model)
    far_own, far_peer, dx, gate = run_experts(rows, blocks[4:])
    own_grad, peer_grad, back = run_experts(rows, blocks[:4], (dx, gate))
    far_peer, back = lax.optimization_barrier((lax.ppermute(far_peer, "core", SWAP), back))
    far_sum = (far_own.astype(f32) + far_peer.astype(f32)).astype(bf16)
    came = hold(lax.ppermute(far_sum, "yl", SWAP), HOLD_FLOPS)
    back, peer_grad, _ = lax.optimization_barrier((back, peer_grad, far_sum))
    near_peer = lax.ppermute(peer_grad, "core", SWAP)
    returned = exchange(back, groups)
    d_first, d_second = finish(own_grad, near_peer, came)
    returned, d_first, d_second = lax.optimization_barrier((returned, d_first, d_second))
    d_tokens, d_gates = combine(target, returned, gate_weights, model)
    return (d_tokens, d_gates, d_first[None], d_second[None])


def solution(mesh):
    dp, expert = mesh.devices.shape
    pairs = expert // 4
    fine = Mesh(np.asarray(mesh.devices).reshape(dp, pairs, 2, 2), AXES)
    number = np.arange(dp * expert).reshape(dp, pairs, 2, 2)
    near = np.arange(pairs) >= pairs // 2
    groups = [
        [int(number[i, k, int(near[k]) ^ side, c]) for i in range(dp) for k in range(pairs)]
        for side in range(2)
        for c in range(2)
    ]
    flat, block = P(AXES, None), P(AXES, None, None)
    return jax.shard_map(
        functools.partial(on_device, groups),
        mesh=fine,
        in_specs=(flat, flat, flat, flat, block, block),
        out_specs=(flat, flat, block, block),
        check_vma=False,
    )
```

time: 209 us -> 209 us (level)
  waiting for transfers between devices: 121 us -> 109 us
  Pallas kernels: 17.9 us -> 29.2 us
  starting transfers between devices: 41.7 us -> 52.5 us
  other arithmetic: 12.3 us -> 3.72 us
    ppermute x4 -> x7, waiting for transfers between devices: 95.8 us -> 74.2 us  [the longest x1 44.9 us: on_device(): came = hold(lax.ppermute(far_sum, 'yl', SWAP), HOLD_FLOPS)]
    pallas_call x2 -> x4, Pallas kernels: 14.2 us -> 25.5 us  [the longest x1 9.58 us: run_experts(): pl.pallas_call(near_kernel, out_shape=(grad, grad, jax.ShapeDtypeStruct((...]
    all_to_all x2, waiting for transfers between devices: 25.1 us -> 34.3 us  [exchange(): lax.all_to_all(x, AXES, split_axis=0, concat_axis=0, axis_index_groups=gr...]
    ppermute x4 -> x7, starting transfers between devices: 13.9 us -> 19.7 us  [the longest x1 7.73 us: on_device(): oth_in = lax.ppermute(own_in, 'yl', SWAP)]
    another operation x3 -> x0, other arithmetic: 5.11 us -> none
    all_to_all x2, starting transfers between devices: 23.9 us -> 28.8 us  [exchange(): lax.all_to_all(x, AXES, split_axis=0, concat_axis=0, axis_index_groups=gr...]
    concatenate x2 -> x0, other arithmetic: 2.72 us -> none  [the longest x1 1.48 us: on_device(): own = jnp.concatenate([w_in[0].T, w_out[0]], axis=0)]
    unnamed x24 -> x13, local copies, waits for them, and re-layouts: 8.96 us -> 10.8 us
  transfers between devices with their start and end apart: 8 -> 11, of which waited for: 5 -> 5; matrix products, arithmetic and copies ran while one was open for 6% -> 3% of each run, Pallas kernels for 2% -> 9%
where the time goes in v3:
time: 209 us; the launch traced here: 208 us
  waiting for transfers between devices  109 us (52%)
  starting transfers between devices  52.5 us (25%)
  Pallas kernels  29.2 us (14%)
  local copies, waits for them, and re-layouts  13.1 us (6%)
  other arithmetic  3.72 us (2%)
    ppermute x1, waiting for transfers between devices, on_device(): came = hold(lax.ppermute(far_sum, 'yl', SWAP), HOLD_FLOPS)  44.9 us
    all_to_all x2, waiting for transfers between devices, exchange(): lax.all_to_all(x, AXES, split_axis=0, concat_axis=0, axis_index_groups=gr...  34.3 us
    all_to_all x2, starting transfers between devices, exchange(): lax.all_to_all(x, AXES, split_axis=0, concat_axis=0, axis_index_groups=gr...  28.8 us
    ppermute x1, waiting for transfers between devices, on_device(): oth_out = lax.ppermute(own_out, 'yl', SWAP)  26.3 us
    unnamed x13, local copies, waits for them, and re-layouts  10.8 us
    pallas_call x1, Pallas kernels, run_experts(): pl.pallas_call(near_kernel, out_shape=(grad, grad, jax.ShapeDtypeStruct((...  9.58 us
    pallas_call x1, Pallas kernels, run_experts(): pl.pallas_call(far_kernel, out_shape=(grad, grad, jax.ShapeDtypeStruct((s...  8.2 us
    ppermute x1, starting transfers between devices, on_device(): oth_in = lax.ppermute(own_in, 'yl', SWAP)  7.73 us
  transfers between devices with their start and end apart: 11, of which 5 were waited for; matrix products, arithmetic and copies ran while one was open for 3% of the time, Pallas kernels for 9%

profile of v3, /device:TPU:8, one launch (start us, length us, event | category | flops | bytes accessed | tf_op | source)
XLA Modules:
  0.0 207.9 jit_solution(15413241400377862470)
XLA Ops:
  0.6 7.7 %collective-permute-start = (bf16[2048,256]{1,0:T(8,128)(2,1)}, bf16[2048,256]{1,0:T(8,128)(2,1)}, u32[]{:S(2)}, u32[]{:S(2)}) collective-permute-start(bf16[2048,256]{1,0:T(8,128)(2,1)} %bitcast.14), channel_id=1, source_target_pairs={{0,2},{2,0},{1,3},{3,1},{4,6},{6,4},{5,7},{7,5},{8,10},{10,8},{9,1... | collective-permute-start | bytes 3145736 | tf_op jit(solution)/shard_map/ppermute | solution.py:282
  8.4 1.9 collective-permute-start.3
  10.3 1.4 copy.14.gates_ref
  11.7 1.4 copy.13.ids_ref
  13.0 1.6 copy.17
  14.6 1.6 copy.18
  16.2 3.7 %dispatch.1 = (bf16[256,32,128]{2,1,0:T(8,128)(2,1)}, s32[32,4]{1,0:T(8,128)}) custom-call(s32[32,4]{1,0:T(8,128)} %copy.13.ids_ref, f32[32,4]{1,0:T(8,128)} %copy.14.gates_ref, bf16[32,16,128]{2,1,0:T(8,128)(2,1)} %bitcast.10, bf16[32,16,128]{2,1,0:T(8,128)(2,1)} %bitcast.11), custom_call_target="tpu_custom_call" | custom-call | tf_op jit(solution)/shard_map/dispatch/pallas_call | solution.py:51
  19.9 15.5 %all-to-all-start = ((bf16[128,64,128]{2,1,0:T(8,128)(2,1)}), bf16[128,64,128]{2,1,0:T(8,128)(2,1)S(1)}, u32[]{:S(2)}, u32[]{:S(2)}) async-start(bf16[128,64,128]{2,1,0:T(8,128)(2,1)} %bitcast.9), calls=%async_computation | async-start | bytes 4194304 | tf_op jit(solution)/shard_map/all_to_all | solution.py:271
  35.4 0.0 copy-start.3
  35.4 0.0 collective-permute-done.x_ref
  35.4 1.2 copy-done.3
  36.6 1.9 collective-permute-start.1
  38.5 2.4 %collective-permute-start.2 = (bf16[256,2048]{1,0:T(8,128)(2,1)}, bf16[256,2048]{1,0:T(8,128)(2,1)}, u32[]{:S(2)}, u32[]{:S(2)}) collective-permute-start(bf16[256,2048]{1,0:T(8,128)(2,1)} %bitcast.18), channel_id=1, source_target_pairs={{0,1},{1,0},{2,3},{3,2},{4,5},{5,4},{6,7},{7,6},{8,9},{9,8},{10,11... | collective-permute-start | bytes 3145736 | tf_op jit(solution)/shard_map/ppermute | solution.py:294
  40.9 1.9 collective-permute-start.4
  42.9 26.3 %collective-permute-done.3.x_ref = bf16[256,2048]{1,0:T(8,128)(2,1)} collective-permute-done((bf16[256,2048]{1,0:T(8,128)(2,1)}, bf16[256,2048]{1,0:T(8,128)(2,1)}, u32[]{:S(2)}, u32[]{:S(2)}) %collective-permute-start.3) | collective-permute-done | bytes 1048608 | tf_op jit(solution)/shard_map/ppermute | solution.py:283
  69.2 1.9 collective-permute-start.5
  71.1 0.0 collective-permute-done.1.i1
  71.1 0.0 collective-permute-done.2.o1
  71.1 0.0 collective-permute-done.4.i1
  71.1 2.9 %collective-permute-done.5.o1 = bf16[256,2048]{1,0:T(8,128)(2,1)} collective-permute-done((bf16[256,2048]{1,0:T(8,128)(2,1)}, bf16[256,2048]{1,0:T(8,128)(2,1)}, u32[]{:S(2)}, u32[]{:S(2)}) %collective-permute-start.5) | collective-permute-done | bytes 1048608 | tf_op jit(solution)/shard_map/ppermute | solution.py:295
  74.1 24.2 %all-to-all-done = bf16[128,64,128]{2,1,0:T(8,128)(2,1)S(1)} async-done(((bf16[128,64,128]{2,1,0:T(8,128)(2,1)}), bf16[128,64,128]{2,1,0:T(8,128)(2,1)S(1)}, u32[]{:S(2)}, u32[]{:S(2)}) %all-to-all-start) | async-done | bytes 2097184 | tf_op jit(solution)/shard_map/all_to_all | solution.py:271
  98.3 2.3 %reshape.23.rows_hbm = bf16[256,4096]{1,0:T(8,128)(2,1)} reshape(bf16[128,64,128]{2,1,0:T(8,128)(2,1)S(1)} %all-to-all-done) | data formatting | bytes 4194304 | tf_op jit(solution)/shard_map/reshape | solution.py:297
  100.5 8.2 %far_quarters.1 = (bf16[512,2048]{1,0:T(8,128)(2,1)}, bf16[512,2048]{1,0:T(8,128)(2,1)}, f32[256,2048]{1,0:T(8,128)}, f32[256,128]{1,0:T(8,128)}) custom-call(bf16[256,4096]{1,0:T(8,128)(2,1)} %reshape.23.rows_hbm, bf16[2048,256]{1,0:T(8,128)(2,1)} %hold.3.i0, bf16[256,2048]{1,0:T(8,128)(2,1)} %hold.4.o0, bf16[2048,256]{1,0:T(8,128)(2,1)} %collective-permute-done.4.i1, ...), custom_call_target="tpu_custom_call" | custom-call | flops 2684354560 | bytes 14680064 | tf_op jit(solution)/shard_map/far_quarters/pallas_call | solution.py:213
  108.8 1.9 collective-permute-start.6
  110.7 0.0 copy-start.1
  110.7 9.6 %near_quarters.1 = (bf16[512,2048]{1,0:T(8,128)(2,1)}, bf16[512,2048]{1,0:T(8,128)(2,1)}, bf16[128,40,128]{2,1,0:T(8,128)(2,1)}) custom-call(bf16[256,4096]{1,0:T(8,128)(2,1)} %reshape.23.rows_hbm, bf16[2048,256]{1,0:T(8,128)(2,1)} %bitcast.15, bf16[256,2048]{1,0:T(8,128)(2,1)} %bitcast.19, bf16[2048,256]{1,0:T(8,128)(2,1)} %collective-permute-done.1.i1, ...), custom_call_target="tpu_custom_call" | custom-call | flops 2684354560 | bytes 14680064 | tf_op jit(solution)/shard_map/near_quarters/pallas_call | solution.py:227
  120.3 0.0 collective-permute-done.6
  120.3 0.0 copy-done.1
  120.3 3.7 %add_convert_fusion = bf16[512,2048]{1,0:T(8,128)(2,1)} fusion(bf16[512,2048]{1,0:T(8,128)(2,1)} %collective-permute-done.6, bf16[512,2048]{1,0:T(8,128)(2,1)S(1)} %copy-done.1), kind=kLoop, calls=%fused_computation | loop fusion | flops 4194304 | bytes 6291456 | tf_op jit(solution)/shard_map/convert_element_type | solution.py:301
  124.0 1.9 collective-permute-start.8
  125.9 13.3 %all-to-all-start.1 = ((bf16[128,40,128]{2,1,0:T(8,128)(2,1)}), bf16[128,40,128]{2,1,0:T(8,128)(2,1)S(1)}, u32[]{:S(2)}, u32[]{:S(2)}) async-start(bf16[128,40,128]{2,1,0:T(8,128)(2,1)} %get-tuple-element.58), calls=%async_computation.1 | async-start | bytes 2621440 | tf_op jit(solution)/shard_map/all_to_all | solution.py:271
  139.2 2.1 %collective-permute-start.7 = (bf16[512,2048]{1,0:T(8,128)(2,1)}, bf16[512,2048]{1,0:T(8,128)(2,1)S(1)}, u32[]{:S(2)}, u32[]{:S(2)}) collective-permute-start(bf16[512,2048]{1,0:T(8,128)(2,1)} %get-tuple-element.60), channel_id=1, source_target_pairs={{0,1},{1,0},{2,3},{3,2},{4,5},{5,4},{6,7},{7,6},{8,9},{9,8},{10,11... | collective-permute-start | bytes 6291464 | tf_op jit(solution)/shard_map/ppermute | solution.py:304
  141.4 44.9 %collective-permute-done.8.x_ref = bf16[512,2048]{1,0:T(8,128)(2,1)} collective-permute-done((bf16[512,2048]{1,0:T(8,128)(2,1)}, bf16[512,2048]{1,0:T(8,128)(2,1)}, u32[]{:S(2)}, u32[]{:S(2)}) %collective-permute-start.8) | collective-permute-done | bytes 2097184 | tf_op jit(solution)/shard_map/ppermute | solution.py:302
  186.3 0.0 collective-permute-done.7.peer_ref
  186.3 0.0 copy-start.2
  186.3 1.3 copy-done.2
  187.6 4.9 %finish.1 = (bf16[2048,256]{1,0:T(8,128)(2,1)}, bf16[256,2048]{1,0:T(8,128)(2,1)}) custom-call(bf16[512,2048]{1,0:T(8,128)(2,1)} %get-tuple-element.59.own_ref, bf16[512,2048]{1,0:T(8,128)(2,1)} %copy-done.2, bf16[512,2048]{1,0:T(8,128)(2,1)} %hold.5.came_ref), custom_call_target="tpu_custom_call" | custom-call | tf_op jit(solution)/shard_map/finish/pallas_call | solution.py:254
  192.5 10.2 %all-to-all-done.1.back_ref = bf16[128,40,128]{2,1,0:T(8,128)(2,1)S(1)} async-done(((bf16[128,40,128]{2,1,0:T(8,128)(2,1)}), bf16[128,40,128]{2,1,0:T(8,128)(2,1)S(1)}, u32[]{:S(2)}, u32[]{:S(2)}) %all-to-all-start.1) | async-done | bytes 1310752 | tf_op jit(solution)/shard_map/all_to_all | solution.py:271
  202.7 0.0 copy-start
  202.7 1.1 copy-done
  203.7 2.8 %combine.1 = (bf16[32,2048]{1,0:T(8,128)(2,1)}, f32[32,4]{1,0:T(8,128)}) custom-call(s32[32,4]{1,0:T(8,128)} %get-tuple-element.36.target_ref, bf16[128,40,128]{2,1,0:T(8,128)(2,1)} %copy-done, f32[32,4]{1,0:T(8,128)} %copy.14.gates_ref), custom_call_target="tpu_custom_call" | custom-call | tf_op jit(solution)/shard_map/combine/pallas_call | solution.py:107
  206.6 1.4 copy.16
  (3 shorter events, 0.0 us)
Async XLA Ops:
  0.6 34.8 %collective-permute-start = (bf16[2048,256]{1,0:T(8,128)(2,1)}, bf16[2048,256]{1,0:T(8,128)(2,1)}, u32[]{:S(2)}, u32[]{:S(2)}) collective-permute-start(bf16[2048,256]{1,0:T(8,128)(2,1)} %bitcast.14), channel_id=1, source_target_pairs={{0,2},{2,0},{1,3},{3,1},{4,6},{6,4},{5,7},{7,5},{8,10},{10,8},{9,1... | collective-permute-start | bytes 3145736 | tf_op jit(solution)/shard_map/ppermute | solution.py:282
  8.4 60.8 %collective-permute-start.3 = (bf16[256,2048]{1,0:T(8,128)(2,1)}, bf16[256,2048]{1,0:T(8,128)(2,1)}, u32[]{:S(2)}, u32[]{:S(2)}) collective-permute-start(bf16[256,2048]{1,0:T(8,128)(2,1)} %bitcast.17), channel_id=1, source_target_pairs={{0,2},{2,0},{1,3},{3,1},{4,6},{6,4},{5,7},{7,5},{8,10},{10,8},{9,1... | collective-permute-start | bytes 3145736 | tf_op jit(solution)/shard_map/ppermute | solution.py:283
  19.9 78.3 %all-to-all-start = ((bf16[128,64,128]{2,1,0:T(8,128)(2,1)}), bf16[128,64,128]{2,1,0:T(8,128)(2,1)S(1)}, u32[]{:S(2)}, u32[]{:S(2)}) async-start(bf16[128,64,128]{2,1,0:T(8,128)(2,1)} %bitcast.9), calls=%async_computation | async-start | bytes 4194304 | tf_op jit(solution)/shard_map/all_to_all | solution.py:271
  35.4 1.2 copy-start.3
  36.6 34.5 %collective-permute-start.1 = (bf16[2048,256]{1,0:T(8,128)(2,1)S(1)}, bf16[2048,256]{1,0:T(8,128)(2,1)}, u32[]{:S(2)}, u32[]{:S(2)}) collective-permute-start(bf16[2048,256]{1,0:T(8,128)(2,1)S(1)} %bitcast.16), channel_id=1, source_target_pairs={{0,1},{1,0},{2,3},{3,2},{4,5},{5,4},{6,7},{7,6},{8,9},{9,8},{10,11... | collective-permute-start | bytes 3145736 | tf_op jit(solution)/shard_map/ppermute | solution.py:294
  38.5 32.6 %collective-permute-start.2 = (bf16[256,2048]{1,0:T(8,128)(2,1)}, bf16[256,2048]{1,0:T(8,128)(2,1)}, u32[]{:S(2)}, u32[]{:S(2)}) collective-permute-start(bf16[256,2048]{1,0:T(8,128)(2,1)} %bitcast.18), channel_id=1, source_target_pairs={{0,1},{1,0},{2,3},{3,2},{4,5},{5,4},{6,7},{7,6},{8,9},{9,8},{10,11... | collective-permute-start | bytes 3145736 | tf_op jit(solution)/shard_map/ppermute | solution.py:294
  40.9 30.2 %collective-permute-start.4 = (bf16[2048,256]{1,0:T(8,128)(2,1)}, bf16[2048,256]{1,0:T(8,128)(2,1)}, u32[]{:S(2)}, u32[]{:S(2)}) collective-permute-start(bf16[2048,256]{1,0:T(8,128)(2,1)} %hold.3.i0), channel_id=1, source_target_pairs={{0,1},{1,0},{2,3},{3,2},{4,5},{5,4},{6,7},{7,6},{8,9},{9,8},{10,11... | collective-permute-start | bytes 3145736 | tf_op jit(solution)/shard_map/ppermute | solution.py:295
  69.2 4.9 %collective-permute-start.5 = (bf16[256,2048]{1,0:T(8,128)(2,1)}, bf16[256,2048]{1,0:T(8,128)(2,1)}, u32[]{:S(2)}, u32[]{:S(2)}) collective-permute-start(bf16[256,2048]{1,0:T(8,128)(2,1)} %hold.4.o0), channel_id=1, source_target_pairs={{0,1},{1,0},{2,3},{3,2},{4,5},{5,4},{6,7},{7,6},{8,9},{9,8},{10,11... | collective-permute-start | bytes 3145736 | tf_op jit(solution)/shard_map/ppermute | solution.py:295
  108.8 11.5 %collective-permute-start.6 = (bf16[512,2048]{1,0:T(8,128)(2,1)}, bf16[512,2048]{1,0:T(8,128)(2,1)}, u32[]{:S(2)}, u32[]{:S(2)}) collective-permute-start(bf16[512,2048]{1,0:T(8,128)(2,1)} %get-tuple-element.46), channel_id=1, source_target_pairs={{0,1},{1,0},{2,3},{3,2},{4,5},{5,4},{6,7},{7,6},{8,9},{9,8},{10,11... | collective-permute-start | bytes 6291464 | tf_op jit(solution)/shard_map/ppermute | solution.py:300
  110.7 9.6 %copy-start.1 = (bf16[512,2048]{1,0:T(8,128)(2,1)S(1)}, bf16[512,2048]{1,0:T(8,128)(2,1)}, u32[]{:S(2)}) copy-start(bf16[512,2048]{1,0:T(8,128)(2,1)} %get-tuple-element.56) | copy-start | bytes 6291460
  124.0 62.3 %collective-permute-start.8 = (bf16[512,2048]{1,0:T(8,128)(2,1)}, bf16[512,2048]{1,0:T(8,128)(2,1)}, u32[]{:S(2)}, u32[]{:S(2)}) collective-permute-start(bf16[512,2048]{1,0:T(8,128)(2,1)} %add_convert_fusion), channel_id=1, source_target_pairs={{0,2},{2,0},{1,3},{3,1},{4,6},{6,4},{5,7},{7,5},{8,10},{10,8},{9,1... | collective-permute-start | bytes 6291464 | tf_op jit(solution)/shard_map/ppermute | solution.py:302
  125.9 76.7 %all-to-all-start.1 = ((bf16[128,40,128]{2,1,0:T(8,128)(2,1)}), bf16[128,40,128]{2,1,0:T(8,128)(2,1)S(1)}, u32[]{:S(2)}, u32[]{:S(2)}) async-start(bf16[128,40,128]{2,1,0:T(8,128)(2,1)} %get-tuple-element.58), calls=%async_computation.1 | async-start | bytes 2621440 | tf_op jit(solution)/shard_map/all_to_all | solution.py:271
  139.2 47.0 %collective-permute-start.7 = (bf16[512,2048]{1,0:T(8,128)(2,1)}, bf16[512,2048]{1,0:T(8,128)(2,1)S(1)}, u32[]{:S(2)}, u32[]{:S(2)}) collective-permute-start(bf16[512,2048]{1,0:T(8,128)(2,1)} %get-tuple-element.60), channel_id=1, source_target_pairs={{0,1},{1,0},{2,3},{3,2},{4,5},{5,4},{6,7},{7,6},{8,9},{9,8},{10,11... | collective-permute-start | bytes 6291464 | tf_op jit(solution)/shard_map/ppermute | solution.py:304
  186.3 1.3 copy-start.2
  202.7 1.1 copy-start

commit v4 on v3

v4 whole, which is shorter than its diff:
```python
import functools

import jax
import jax.numpy as jnp
import numpy as np
from jax import lax
from jax.experimental import pallas as pl
from jax.experimental.pallas import tpu as pltpu
from jax.sharding import Mesh
from jax.sharding import PartitionSpec as P

TOPK = 4
LANES = 128
AXES = ("dp", "yh", "yl", "core")
GATE_ROWS = 8
HOLD_FLOPS = int(3e10)
SWAP = [(0, 1), (1, 0)]
f32, bf16 = jnp.float32, jnp.bfloat16


def dispatch_kernel(
    ids_ref, gates_ref, tok_ref, dout_ref, out_ref, target_ref, count_ref, tok_lines, dout_lines
):
    tokens, model = tok_ref.shape
    width = model // LANES
    for j in range(width):
        part = slice(j * LANES, (j + 1) * LANES)
        tok_lines[pl.ds(j, tokens, stride=width), :] = tok_ref[:, part].astype(f32)
        dout_lines[pl.ds(j, tokens, stride=width), :] = dout_ref[:, part].astype(f32)
    out_ref[...] = jnp.zeros_like(out_ref)

    def clear(i, carry):
        count_ref[i] = 0
        return carry

    lax.fori_loop(0, count_ref.shape[0], clear, 0, unroll=8)

    def place(t, carry):
        lines = pl.ds(pl.multiple_of(t * width, width), width)
        row = tok_lines[lines, :].astype(bf16)
        grad = dout_lines[lines, :]
        for k in range(TOPK):
            e = ids_ref[k, t]
            slot = count_ref[e]
            count_ref[e] = slot + 1
            at = 2 * e + slot
            target_ref[k, t] = at
            out_ref[at, 0:width, :] = row
            out_ref[at, width : 2 * width, :] = (grad * gates_ref[k, t]).astype(bf16)
        return carry

    lax.fori_loop(0, tokens, place, 0)


def dispatch(ids, gates, tokens, d_out, experts):
    rows, model = tokens.shape
    width = model // LANES
    smem = pl.BlockSpec(memory_space=pltpu.SMEM)
    vmem = pl.BlockSpec(memory_space=pltpu.VMEM)
    return pl.pallas_call(
        dispatch_kernel,
        out_shape=(
            jax.ShapeDtypeStruct((2 * experts, 2 * width, LANES), bf16),
            jax.ShapeDtypeStruct((TOPK, rows), jnp.int32),
        ),
        in_specs=[smem, smem, vmem, vmem],
        out_specs=(vmem, smem),
        scratch_shapes=[
            pltpu.SMEM((experts,), jnp.int32),
            pltpu.VMEM((rows * width, LANES), f32),
            pltpu.VMEM((rows * width, LANES), f32),
        ],
        name="dispatch",
    )(ids, gates, tokens, d_out)


def hold(x, flops):
    anywhere = pl.BlockSpec(memory_space=pl.ANY)
    return pl.pallas_call(
        lambda x_ref, y_ref: None,
        out_shape=jax.ShapeDtypeStruct(x.shape, x.dtype),
        in_specs=[anywhere],
        out_specs=anywhere,
        input_output_aliases={0: 0},
        cost_estimate=pl.CostEstimate(flops=flops, bytes_accessed=0, transcendentals=0),
        name="hold",
    )(x)


def combine_kernel(target_ref, back_ref, gates_ref, dx_ref, gate_ref, dx_rows, gate_rows):
    tokens, model = dx_ref.shape
    width = model // LANES
    lane = lax.broadcasted_iota(jnp.int32, (1, LANES), 1)

    def total(t, carry):
        acc = jnp.zeros((width, LANES), f32)
        gate = jnp.zeros((1, LANES), f32)
        for k in range(TOPK):
            at = target_ref[k, t]
            e, slot = lax.shift_right_logical(at, 1), lax.bitwise_and(at, 1)
            first = pl.multiple_of(slot * width, width)
            acc += back_ref[e, pl.ds(first, width), :].astype(f32)
            extra = back_ref[e, 2 * width : 2 * width + GATE_ROWS, :].astype(f32)
            pair = jnp.where(slot == 0, extra[0:2, :], extra[2:4, :])
            gate = jnp.where(lane == k, pair[0:1, :] + pair[1:2, :], gate)
        dx_rows[pl.ds(pl.multiple_of(t * width, width), width), :] = acc
        gate_rows[pl.ds(t, 1), :] = gate
        return carry

    lax.fori_loop(0, tokens, total, 0)
    for j in range(width):
        part = dx_rows[pl.ds(j, tokens, stride=width), :]
        dx_ref[:, j * LANES : (j + 1) * LANES] = part.astype(bf16)
    gate_ref[...] = gate_rows[...].T[:TOPK, :] / gates_ref[...]


def combine(target, back, gates, model):
    tokens = gates.shape[1]
    vmem = pl.BlockSpec(memory_space=pltpu.VMEM)
    return pl.pallas_call(
        combine_kernel,
        out_shape=(
            jax.ShapeDtypeStruct((tokens, model), bf16),
            jax.ShapeDtypeStruct(gates.shape, f32),
        ),
        in_specs=[pl.BlockSpec(memory_space=pltpu.SMEM), vmem, vmem],
        out_specs=(vmem, vmem),
        scratch_shapes=[
            pltpu.VMEM((tokens * model // LANES, LANES), f32),
            pltpu.VMEM((tokens, LANES), f32),
        ],
        name="combine",
    )(target, back, gates)


def dot(a, b, ca, cb):
    return lax.dot_general(a, b, (((ca,), (cb,)), ((), ())), preferred_element_type=f32)


def experts_kernel(rows_hbm, *refs):
    blocks, stores_to, back_ref = refs[:8], refs[8:12], refs[12]
    rows, ins, outs, grads, total, lines, in_sems, out_sems = refs[13:]
    hidden, model = outs.shape[1], outs.shape[2]
    slots, width = rows.shape[0], model // LANES
    experts = slots // 2
    loads = [pltpu.make_async_copy(rows_hbm, rows, in_sems.at[0])]
    for q in range(4):
        loads.append(pltpu.make_async_copy(blocks[2 * q], ins.at[q], in_sems.at[1 + 2 * q]))
        loads.append(pltpu.make_async_copy(blocks[2 * q + 1], outs.at[q], in_sems.at[2 + 2 * q]))
    stores = [
        pltpu.make_async_copy(grads.at[q], g, out_sems.at[q]) for q, g in enumerate(stores_to)
    ]
    for load in loads:
        load.start()
    loads[0].wait()
    gate = jnp.zeros((slots, 1), f32)
    for q in range(4):
        loads[1 + 2 * q].wait()
        loads[2 + 2 * q].wait()
        preact = dot(rows[:, :model], ins[q], 1, 0)
        pulled = dot(rows[:, model:], outs[q], 1, 1)
        sig = jax.nn.sigmoid(preact)
        act = preact * sig
        d_pre = (pulled * sig * (1.0 + preact * (1.0 - sig))).astype(bf16)
        gate += jnp.sum(act * pulled, axis=1, keepdims=True)
        act = act.astype(bf16)
        grads[q, :hidden, :] = dot(d_pre, rows[:, :model], 0, 0).astype(bf16)
        grads[q, hidden:, :] = dot(act, rows[:, model:], 0, 0).astype(bf16)
        stores[q].start()
        part = dot(d_pre, ins[q], 1, 1)
        total[...] = part if q == 0 else total[...] + part
    for j in range(width):
        lines[pl.ds(j, slots, stride=width), :] = total[:, j * LANES : (j + 1) * LANES]
    back_ref[:, : 2 * width, :] = lines[...].astype(bf16).reshape(experts, 2 * width, LANES)
    gate = jnp.broadcast_to(gate, (slots, LANES))
    high = gate.astype(bf16)
    low = (gate - high.astype(f32)).astype(bf16)
    row = lax.broadcasted_iota(jnp.int32, (experts * GATE_ROWS, slots), 0)
    slot = lax.broadcasted_iota(jnp.int32, (experts * GATE_ROWS, slots), 1)
    place = row - (slot >> 1) * GATE_ROWS - 2 * (slot & 1)
    spread = dot((place == 0).astype(bf16), high, 1, 0) + dot((place == 1).astype(bf16), low, 1, 0)
    back_ref[:, 2 * width :, :] = spread.astype(bf16).reshape(experts, GATE_ROWS, LANES)
    for store in stores:
        store.wait()


def run_experts(rows, blocks):
    slots, model = rows.shape[0], rows.shape[1] // 2
    hidden = blocks[1].shape[0]
    width = model // LANES
    anywhere = pl.BlockSpec(memory_space=pl.ANY)
    vmem = pl.BlockSpec(memory_space=pltpu.VMEM)
    return pl.pallas_call(
        experts_kernel,
        out_shape=(jax.ShapeDtypeStruct((2 * hidden, model), bf16),) * 4
        + (jax.ShapeDtypeStruct((slots // 2, 2 * width + GATE_ROWS, LANES), bf16),),
        in_specs=[anywhere] * 9,
        out_specs=(anywhere,) * 4 + (vmem,),
        scratch_shapes=[
            pltpu.VMEM(rows.shape, bf16),
            pltpu.VMEM((4, model, hidden), bf16),
            pltpu.VMEM((4, hidden, model), bf16),
            pltpu.VMEM((4, 2 * hidden, model), bf16),
            pltpu.VMEM((slots, model), f32),
            pltpu.VMEM((slots * width, LANES), f32),
            pltpu.SemaphoreType.DMA((9,)),
            pltpu.SemaphoreType.DMA((4,)),
        ],
        cost_estimate=pl.CostEstimate(
            flops=4 * 5 * 2 * slots * model * hidden,
            bytes_accessed=2 * (rows.size + 16 * hidden * model),
            transcendentals=0,
        ),
        name="experts",
    )(rows, *blocks)


def finish_kernel(own_ref, peer_ref, came_ref, first_ref, second_ref):
    hidden = second_ref.shape[0]
    total = own_ref[...].astype(f32) + peer_ref[...].astype(f32) + came_ref[...].astype(f32)
    first_ref[...] = total[:hidden, :].T.astype(bf16)
    second_ref[...] = total[hidden:, :].astype(bf16)


def finish(own, peer, came):
    hidden, model = own.shape[0] // 2, own.shape[1]
    part = pl.BlockSpec((2 * hidden, 512), lambda j: (0, j))
    return pl.pallas_call(
        finish_kernel,
        grid=(model // 512,),
        out_shape=(
            jax.ShapeDtypeStruct((model, hidden), bf16),
            jax.ShapeDtypeStruct((hidden, model), bf16),
        ),
        in_specs=[part] * 3,
        out_specs=(
            pl.BlockSpec((512, hidden), lambda j: (j, 0)),
            pl.BlockSpec((hidden, 512), lambda j: (0, j)),
        ),
        name="finish",
    )(own, peer, came)


def exchange(x, groups):
    return lax.all_to_all(
        x, AXES, split_axis=0, concat_axis=0, axis_index_groups=groups, tiled=True
    )


def on_device(groups, tokens, d_out, expert_ids, gate_weights, w_in, w_out):
    tok_rows, model = tokens.shape
    width = model // LANES
    experts = len(groups[0])
    slots = 2 * experts
    own_in, own_out = w_in[0], w_out[0]
    gates = gate_weights.T
    oth_in = hold(lax.ppermute(own_in, "yl", SWAP), HOLD_FLOPS)
    outgoing, target = dispatch(expert_ids.T, gates, tokens, d_out, experts)
    arrived = exchange(outgoing.reshape(experts, 4 * width, LANES), groups)
    own_in, own_out, oth_in = lax.optimization_barrier((own_in, own_out, oth_in))
    oth_out = lax.ppermute(own_out, "yl", SWAP)
    near = [own_in, own_out, lax.ppermute(own_in, "core", SWAP), lax.ppermute(own_out, "core", SWAP)]
    far = [oth_in, oth_out, lax.ppermute(oth_in, "core", SWAP), lax.ppermute(oth_out, "core", SWAP)]
    arrived, *blocks = lax.optimization_barrier((arrived, *near, *far))
    rows = arrived.reshape(slots, 2 * model)
    own_grad, peer_grad, far_own, far_peer, back = run_experts(rows, blocks)
    returned = exchange(back, groups)
    far_peer = hold(lax.ppermute(far_peer, "core", SWAP), HOLD_FLOPS)
    far_sum = (far_own.astype(f32) + far_peer.astype(f32)).astype(bf16)
    came = lax.ppermute(far_sum, "yl", SWAP)
    near_peer = lax.ppermute(peer_grad, "core", SWAP)
    d_tokens, d_gates = combine(target, returned, gates, model)
    came, d_tokens, d_gates = lax.optimization_barrier((came, d_tokens, d_gates))
    d_first, d_second = finish(own_grad, near_peer, came)
    return (d_tokens, d_gates.T, d_first[None], d_second[None])


def solution(mesh):
    dp, expert = mesh.devices.shape
    pairs = expert // 4
    fine = Mesh(np.asarray(mesh.devices).reshape(dp, pairs, 2, 2), AXES)
    number = np.arange(dp * expert).reshape(dp, pairs, 2, 2)
    near = np.arange(pairs) >= pairs // 2
    groups = [
        [int(number[i, k, int(near[k]) ^ side, c]) for i in range(dp) for k in range(pairs)]
        for side in range(2)
        for c in range(2)
    ]
    flat, block = P(AXES, None), P(AXES, None, None)
    return jax.shard_map(
        functools.partial(on_device, groups),
        mesh=fine,
        in_specs=(flat, flat, flat, flat, block, block),
        out_specs=(flat, flat, block, block),
        check_vma=False,
    )
```

time: 209 us -> 211 us (level)
  the two profiles are of different devices: /device:TPU:8 before, /device:TPU:20 now
where the time goes in v4:
time: 211 us
  waiting for transfers between devices  107 us (51%)
  starting transfers between devices  67.4 us (32%)
  Pallas kernels  22.9 us (11%)
  local copies, waits for them, and re-layouts  8.67 us (4%)
  other arithmetic  3.74 us (2%)
    ppermute x1, waiting for transfers between devices, on_device(): oth_out = lax.ppermute(own_out, 'yl', SWAP)  44.1 us
    all_to_all x2, starting transfers between devices, exchange(): lax.all_to_all(x, AXES, split_axis=0, concat_axis=0, axis_index_groups=gr...  42.3 us
    ppermute x1, waiting for transfers between devices, on_device(): came = lax.ppermute(far_sum, 'yl', SWAP)  31.9 us
    all_to_all x2, waiting for transfers between devices, exchange(): lax.all_to_all(x, AXES, split_axis=0, concat_axis=0, axis_index_groups=gr...  26.8 us
    pallas_call x1, Pallas kernels, run_experts(): pl.pallas_call(experts_kernel, out_shape=(jax.ShapeDtypeStruct((2 * hidde...  11.5 us
    unnamed x16, local copies, waits for them, and re-layouts  6.3 us
    pallas_call x1, Pallas kernels, finish(): pl.pallas_call(finish_kernel, grid=(model // 512,), out_shape=(jax.ShapeD...  4.88 us
    ppermute x1, starting transfers between devices, on_device(): came = lax.ppermute(far_sum, 'yl', SWAP)  4.74 us
  transfers between devices with their start and end apart: 11, of which 5 were waited for; matrix products, arithmetic and copies ran while one was open for 2% of the time, Pallas kernels for 3%

profile of v4, /device:TPU:20, one launch (start us, length us, event | category | flops | bytes accessed | tf_op | source)
XLA Modules:
  0.0 210.6 jit_solution(14834821353353673787)
XLA Ops:
  0.6 3.5 %collective-permute-start = (bf16[2048,256]{1,0:T(8,128)(2,1)}, bf16[2048,256]{1,0:T(8,128)(2,1)}, u32[]{:S(2)}, u32[]{:S(2)}) collective-permute-start(bf16[2048,256]{1,0:T(8,128)(2,1)} %bitcast.12), channel_id=1, source_target_pairs={{0,2},{2,0},{1,3},{3,1},{4,6},{6,4},{5,7},{7,5},{8,10},{10,8},{9,1... | collective-permute-start | bytes 3145736 | tf_op jit(solution)/shard_map/ppermute | solution.py:257
  4.1 3.7 %dispatch.1 = (bf16[256,32,128]{2,1,0:T(8,128)(2,1)}, s32[4,32]{1,0:T(4,128)}) custom-call(s32[4,32]{1,0:T(4,128)} %bitcast.11, f32[4,32]{1,0:T(4,128)} %bitcast.9, bf16[32,2048]{1,0:T(8,128)(2,1)} %tok_ref.1, bf16[32,2048]{1,0:T(8,128)(2,1)} %dout_ref.1), custom_call_target="tpu_custom_call" | custom-call | tf_op jit(solution)/shard_map/dispatch/pallas_call | solution.py:60
  7.8 18.7 %all-to-all-start = ((bf16[128,64,128]{2,1,0:T(8,128)(2,1)}), bf16[128,64,128]{2,1,0:T(8,128)(2,1)S(1)}, u32[]{:S(2)}, u32[]{:S(2)}) async-start(bf16[128,64,128]{2,1,0:T(8,128)(2,1)} %bitcast.8), calls=%async_computation | async-start | bytes 4194304 | tf_op jit(solution)/shard_map/all_to_all | solution.py:245
  26.5 0.0 copy-start.3
  26.5 3.9 %collective-permute-done.x_ref = bf16[2048,256]{1,0:T(8,128)(2,1)} collective-permute-done((bf16[2048,256]{1,0:T(8,128)(2,1)}, bf16[2048,256]{1,0:T(8,128)(2,1)}, u32[]{:S(2)}, u32[]{:S(2)}) %collective-permute-start) | collective-permute-done | bytes 1048608 | tf_op jit(solution)/shard_map/ppermute | solution.py:257
  30.4 4.7 %collective-permute-start.3 = (bf16[256,2048]{1,0:T(8,128)(2,1)}, bf16[256,2048]{1,0:T(8,128)(2,1)S(1)}, u32[]{:S(2)}, u32[]{:S(2)}) collective-permute-start(bf16[256,2048]{1,0:T(8,128)(2,1)} %bitcast.15), channel_id=1, source_target_pairs={{0,2},{2,0},{1,3},{3,1},{4,6},{6,4},{5,7},{7,5},{8,10},{10,8},{9,1... | collective-permute-start | bytes 3145736 | tf_op jit(solution)/shard_map/ppermute | solution.py:261
  35.1 1.9 collective-permute-start.2
  37.0 0.0 copy-done.3
  37.1 2.4 %collective-permute-start.1 = (bf16[2048,256]{1,0:T(8,128)(2,1)S(1)}, bf16[2048,256]{1,0:T(8,128)(2,1)S(1)}, u32[]{:S(2)}, u32[]{:S(2)}) collective-permute-start(bf16[2048,256]{1,0:T(8,128)(2,1)S(1)} %bitcast.14), channel_id=1, source_target_pairs={{0,1},{1,0},{2,3},{3,2},{4,5},{5,4},{6,7},{7,6},{8,9},{9,8},{10,11... | collective-permute-start | bytes 3145736 | tf_op jit(solution)/shard_map/ppermute | solution.py:262
  39.5 1.9 collective-permute-start.4
  41.4 44.1 %collective-permute-done.3.refs_5_ = bf16[256,2048]{1,0:T(8,128)(2,1)S(1)} collective-permute-done((bf16[256,2048]{1,0:T(8,128)(2,1)}, bf16[256,2048]{1,0:T(8,128)(2,1)S(1)}, u32[]{:S(2)}, u32[]{:S(2)}) %collective-permute-start.3) | collective-permute-done | bytes 1048608 | tf_op jit(solution)/shard_map/ppermute | solution.py:261
  85.5 0.0 copy-start.4
  85.5 1.9 collective-permute-start.5
  87.4 0.0 collective-permute-done.1.refs_2_
  87.4 0.0 copy-start.6
  87.4 0.0 collective-permute-done.4.refs_6_
  87.4 0.0 copy-start.7
  87.4 0.0 collective-permute-done.2.refs_3_
  87.4 0.0 copy-done.4
  87.4 0.9 copy-done.6
  88.4 0.3 copy-done.7
  88.7 0.0 copy-start.5
  88.7 1.0 copy-done.5
  89.7 0.5 collective-permute-done.5.refs_7_
  90.1 0.0 all-to-all-done
  90.1 2.4 %reshape.15.rows_hbm = bf16[256,4096]{1,0:T(8,128)(2,1)} reshape(bf16[128,64,128]{2,1,0:T(8,128)(2,1)S(1)} %all-to-all-done) | data formatting | bytes 4194304 | tf_op jit(solution)/shard_map/reshape | solution.py:265
  92.5 11.5 %experts.1 = (bf16[512,2048]{1,0:T(8,128)(2,1)}, bf16[512,2048]{1,0:T(8,128)(2,1)}, bf16[512,2048]{1,0:T(8,128)(2,1)}, bf16[512,2048]{1,0:T(8,128)(2,1)}, bf16[128,40,128]{2,1,0:T(8,128)(2,1)}) custom-call(bf16[256,4096]{1,0:T(8,128)(2,1)} %reshape.15.rows_hbm, bf16[2048,256]{1,0:T(8,128)(2,1)} %bitcast.13, bf16[256,2048]{1,0:T(8,128)(2,1)} %bitcast.17, ...), custom_call_target="tpu_custom_call" | custom-call | flops 5368709120 | bytes 18874368 | tf_op jit(solution)/shard_map/experts/pallas_call | solution.py:193
  104.0 2.0 collective-permute-start.6
  106.0 23.7 %all-to-all-start.1 = ((bf16[128,40,128]{2,1,0:T(8,128)(2,1)}), bf16[128,40,128]{2,1,0:T(8,128)(2,1)S(1)}, u32[]{:S(2)}, u32[]{:S(2)}) async-start(bf16[128,40,128]{2,1,0:T(8,128)(2,1)} %get-tuple-element.46), calls=%async_computation.1 | async-start | bytes 2621440 | tf_op jit(solution)/shard_map/all_to_all | solution.py:245
  129.7 0.0 copy-start.2
  129.7 0.0 collective-permute-done.6.x_ref
  129.7 1.6 copy-done.2
  131.3 3.7 %add_convert_fusion = bf16[512,2048]{1,0:T(8,128)(2,1)} fusion(bf16[512,2048]{1,0:T(8,128)(2,1)} %hold.3, bf16[512,2048]{1,0:T(8,128)(2,1)S(1)} %copy-done.2), kind=kLoop, calls=%fused_computation | loop fusion | flops 4194304 | bytes 6291456 | tf_op jit(solution)/shard_map/convert_element_type | solution.py:269
  135.0 4.7 %collective-permute-start.7 = (bf16[512,2048]{1,0:T(8,128)(2,1)}, bf16[512,2048]{1,0:T(8,128)(2,1)S(1)}, u32[]{:S(2)}, u32[]{:S(2)}) collective-permute-start(bf16[512,2048]{1,0:T(8,128)(2,1)} %add_convert_fusion), channel_id=1, source_target_pairs={{0,2},{2,0},{1,3},{3,1},{4,6},{6,4},{5,7},{7,5},{8,10},{10,8},{9,1... | collective-permute-start | bytes 6291464 | tf_op jit(solution)/shard_map/ppermute | solution.py:270
  139.8 1.9 collective-permute-start.8
  141.7 26.8 %all-to-all-done.1.back_ref = bf16[128,40,128]{2,1,0:T(8,128)(2,1)S(1)} async-done(((bf16[128,40,128]{2,1,0:T(8,128)(2,1)}), bf16[128,40,128]{2,1,0:T(8,128)(2,1)S(1)}, u32[]{:S(2)}, u32[]{:S(2)}) %all-to-all-start.1) | async-done | bytes 1310752 | tf_op jit(solution)/shard_map/all_to_all | solution.py:245
  168.5 0.0 copy-start
  168.5 1.1 copy-done
  169.6 2.9 %combine.1 = (bf16[32,2048]{1,0:T(8,128)(2,1)}, f32[4,32]{1,0:T(4,128)}) custom-call(s32[4,32]{1,0:T(4,128)} %get-tuple-element.45.target_ref, bf16[128,40,128]{2,1,0:T(8,128)(2,1)} %copy-done, f32[4,32]{1,0:T(4,128)} %bitcast.10), custom_call_target="tpu_custom_call" | custom-call | tf_op jit(solution)/shard_map/combine/pallas_call | solution.py:120
  172.5 31.9 %collective-permute-done.7.came_ref = bf16[512,2048]{1,0:T(8,128)(2,1)S(1)} collective-permute-done((bf16[512,2048]{1,0:T(8,128)(2,1)}, bf16[512,2048]{1,0:T(8,128)(2,1)S(1)}, u32[]{:S(2)}, u32[]{:S(2)}) %collective-permute-start.7) | collective-permute-done | bytes 2097184 | tf_op jit(solution)/shard_map/ppermute | solution.py:270
  204.4 0.0 copy-start.1
  204.4 0.0 collective-permute-done.8.peer_ref
  204.4 1.4 copy-done.1
  205.8 4.9 %finish.1 = (bf16[2048,256]{1,0:T(8,128)(2,1)}, bf16[256,2048]{1,0:T(8,128)(2,1)}) custom-call(bf16[512,2048]{1,0:T(8,128)(2,1)} %get-tuple-element.51.own_ref, bf16[512,2048]{1,0:T(8,128)(2,1)} %collective-permute-done.8.peer_ref, bf16[512,2048]{1,0:T(8,128)(2,1)} %copy-done.1), custom_call_target="tpu_custom_call" | custom-call | tf_op jit(solution)/shard_map/finish/pallas_call | solution.py:228
  (2 shorter events, 0.0 us)
Async XLA Ops:
  0.6 29.8 %collective-permute-start = (bf16[2048,256]{1,0:T(8,128)(2,1)}, bf16[2048,256]{1,0:T(8,128)(2,1)}, u32[]{:S(2)}, u32[]{:S(2)}) collective-permute-start(bf16[2048,256]{1,0:T(8,128)(2,1)} %bitcast.12), channel_id=1, source_target_pairs={{0,2},{2,0},{1,3},{3,1},{4,6},{6,4},{5,7},{7,5},{8,10},{10,8},{9,1... | collective-permute-start | bytes 3145736 | tf_op jit(solution)/shard_map/ppermute | solution.py:257
  7.8 82.3 %all-to-all-start = ((bf16[128,64,128]{2,1,0:T(8,128)(2,1)}), bf16[128,64,128]{2,1,0:T(8,128)(2,1)S(1)}, u32[]{:S(2)}, u32[]{:S(2)}) async-start(bf16[128,64,128]{2,1,0:T(8,128)(2,1)} %bitcast.8), calls=%async_computation | async-start | bytes 4194304 | tf_op jit(solution)/shard_map/all_to_all | solution.py:245
  26.5 10.6 %copy-start.3 = (bf16[1,2048,256]{2,1,0:T(8,128)(2,1)S(1)}, bf16[1,2048,256]{2,1,0:T(8,128)(2,1)}, u32[]{:S(2)}) copy-start(bf16[1,2048,256]{2,1,0:T(8,128)(2,1)} %param.10) | copy-start | bytes 3145732
  30.4 55.0 %collective-permute-start.3 = (bf16[256,2048]{1,0:T(8,128)(2,1)}, bf16[256,2048]{1,0:T(8,128)(2,1)S(1)}, u32[]{:S(2)}, u32[]{:S(2)}) collective-permute-start(bf16[256,2048]{1,0:T(8,128)(2,1)} %bitcast.15), channel_id=1, source_target_pairs={{0,2},{2,0},{1,3},{3,1},{4,6},{6,4},{5,7},{7,5},{8,10},{10,8},{9,1... | collective-permute-start | bytes 3145736 | tf_op jit(solution)/shard_map/ppermute | solution.py:261
  35.1 52.3 %collective-permute-start.2 = (bf16[256,2048]{1,0:T(8,128)(2,1)}, bf16[256,2048]{1,0:T(8,128)(2,1)S(1)}, u32[]{:S(2)}, u32[]{:S(2)}) collective-permute-start(bf16[256,2048]{1,0:T(8,128)(2,1)} %bitcast.16), channel_id=1, source_target_pairs={{0,1},{1,0},{2,3},{3,2},{4,5},{5,4},{6,7},{7,6},{8,9},{9,8},{10,11... | collective-permute-start | bytes 3145736 | tf_op jit(solution)/shard_map/ppermute | solution.py:262
  37.1 50.3 %collective-permute-start.1 = (bf16[2048,256]{1,0:T(8,128)(2,1)S(1)}, bf16[2048,256]{1,0:T(8,128)(2,1)S(1)}, u32[]{:S(2)}, u32[]{:S(2)}) collective-permute-start(bf16[2048,256]{1,0:T(8,128)(2,1)S(1)} %bitcast.14), channel_id=1, source_target_pairs={{0,1},{1,0},{2,3},{3,2},{4,5},{5,4},{6,7},{7,6},{8,9},{9,8},{10,11... | collective-permute-start | bytes 3145736 | tf_op jit(solution)/shard_map/ppermute | solution.py:262
  39.5 47.9 %collective-permute-start.4 = (bf16[2048,256]{1,0:T(8,128)(2,1)}, bf16[2048,256]{1,0:T(8,128)(2,1)S(1)}, u32[]{:S(2)}, u32[]{:S(2)}) collective-permute-start(bf16[2048,256]{1,0:T(8,128)(2,1)} %hold.2.refs_4_), channel_id=1, source_target_pairs={{0,1},{1,0},{2,3},{3,2},{4,5},{5,4},{6,7},{7,6},{8,9},{9,8},{10,11... | collective-permute-start | bytes 3145736 | tf_op jit(solution)/shard_map/ppermute | solution.py:263
  85.5 2.0 copy-start.4
  85.5 4.7 %collective-permute-start.5 = (bf16[256,2048]{1,0:T(8,128)(2,1)S(1)}, bf16[256,2048]{1,0:T(8,128)(2,1)}, u32[]{:S(2)}, u32[]{:S(2)}) collective-permute-start(bf16[256,2048]{1,0:T(8,128)(2,1)S(1)} %collective-permute-done.3.refs_5_), channel_id=1, source_target_pairs={{0,1},{1,0},{2,3},{3,2},{4,5},{5,4},{6,7},{7,6},{8,9},{9,8},{10,11... | collective-permute-start | bytes 3145736 | tf_op jit(solution)/shard_map/ppermute | solution.py:263
  87.4 1.0 copy-start.6
  87.4 1.3 copy-start.7
  88.7 1.0 copy-start.5
  104.0 25.7 %collective-permute-start.6 = (bf16[512,2048]{1,0:T(8,128)(2,1)}, bf16[512,2048]{1,0:T(8,128)(2,1)}, u32[]{:S(2)}, u32[]{:S(2)}) collective-permute-start(bf16[512,2048]{1,0:T(8,128)(2,1)} %get-tuple-element.44), channel_id=1, source_target_pairs={{0,1},{1,0},{2,3},{3,2},{4,5},{5,4},{6,7},{7,6},{8,9},{9,8},{10,11... | collective-permute-start | bytes 6291464 | tf_op jit(solution)/shard_map/ppermute | solution.py:268
  106.0 62.5 %all-to-all-start.1 = ((bf16[128,40,128]{2,1,0:T(8,128)(2,1)}), bf16[128,40,128]{2,1,0:T(8,128)(2,1)S(1)}, u32[]{:S(2)}, u32[]{:S(2)}) async-start(bf16[128,40,128]{2,1,0:T(8,128)(2,1)} %get-tuple-element.46), calls=%async_computation.1 | async-start | bytes 2621440 | tf_op jit(solution)/shard_map/all_to_all | solution.py:245
  129.7 1.6 copy-start.2
  135.0 69.3 %collective-permute-start.7 = (bf16[512,2048]{1,0:T(8,128)(2,1)}, bf16[512,2048]{1,0:T(8,128)(2,1)S(1)}, u32[]{:S(2)}, u32[]{:S(2)}) collective-permute-start(bf16[512,2048]{1,0:T(8,128)(2,1)} %add_convert_fusion), channel_id=1, source_target_pairs={{0,2},{2,0},{1,3},{3,1},{4,6},{6,4},{5,7},{7,5},{8,10},{10,8},{9,1... | collective-permute-start | bytes 6291464 | tf_op jit(solution)/shard_map/ppermute | solution.py:270
  139.8 64.6 %collective-permute-start.8 = (bf16[512,2048]{1,0:T(8,128)(2,1)}, bf16[512,2048]{1,0:T(8,128)(2,1)}, u32[]{:S(2)}, u32[]{:S(2)}) collective-permute-start(bf16[512,2048]{1,0:T(8,128)(2,1)} %get-tuple-element.52), channel_id=1, source_target_pairs={{0,1},{1,0},{2,3},{3,2},{4,5},{5,4},{6,7},{7,6},{8,9},{9,8},{10,11... | collective-permute-start | bytes 6291464 | tf_op jit(solution)/shard_map/ppermute | solution.py:271
  168.5 1.1 copy-start
  204.4 1.4 copy-start.1

commit v5 on v4

--- a/solution.py
+++ b/solution.py
@@ -138,8 +138,8 @@
 
 
 def experts_kernel(rows_hbm, *refs):
-    blocks, stores_to, back_ref = refs[:8], refs[8:12], refs[12]
-    rows, ins, outs, grads, total, lines, in_sems, out_sems = refs[13:]
+    blocks, stores_to, back_ref = refs[:8], refs[8:16], refs[16]
+    rows, ins, outs, grads, total, lines, in_sems, out_sems = refs[17:]
     hidden, model = outs.shape[1], outs.shape[2]
     slots, width = rows.shape[0], model // LANES
     experts = slots // 2
@@ -164,9 +164,10 @@
         d_pre = (pulled * sig * (1.0 + preact * (1.0 - sig))).astype(bf16)
         gate += jnp.sum(act * pulled, axis=1, keepdims=True)
         act = act.astype(bf16)
-        grads[q, :hidden, :] = dot(d_pre, rows[:, :model], 0, 0).astype(bf16)
-        grads[q, hidden:, :] = dot(act, rows[:, model:], 0, 0).astype(bf16)
-        stores[q].start()
+        grads[2 * q] = dot(d_pre, rows[:, :model], 0, 0).astype(bf16)
+        grads[2 * q + 1] = dot(act, rows[:, model:], 0, 0).astype(bf16)
+        stores[2 * q].start()
+        stores[2 * q + 1].start()
         part = dot(d_pre, ins[q], 1, 1)
         total[...] = part if q == 0 else total[...] + part
     for j in range(width):
@@ -192,19 +193,19 @@
     vmem = pl.BlockSpec(memory_space=pltpu.VMEM)
     return pl.pallas_call(
         experts_kernel,
-        out_shape=(jax.ShapeDtypeStruct((2 * hidden, model), bf16),) * 4
+        out_shape=(jax.ShapeDtypeStruct((hidden, model), bf16),) * 8
         + (jax.ShapeDtypeStruct((slots // 2, 2 * width + GATE_ROWS, LANES), bf16),),
         in_specs=[anywhere] * 9,
-        out_specs=(anywhere,) * 4 + (vmem,),
+        out_specs=(anywhere,) * 8 + (vmem,),
         scratch_shapes=[
             pltpu.VMEM(rows.shape, bf16),
             pltpu.VMEM((4, model, hidden), bf16),
             pltpu.VMEM((4, hidden, model), bf16),
-            pltpu.VMEM((4, 2 * hidden, model), bf16),
+            pltpu.VMEM((8, hidden, model), bf16),
             pltpu.VMEM((slots, model), f32),
             pltpu.VMEM((slots * width, LANES), f32),
             pltpu.SemaphoreType.DMA((9,)),
-            pltpu.SemaphoreType.DMA((4,)),
+            pltpu.SemaphoreType.DMA((8,)),
         ],
         cost_estimate=pl.CostEstimate(
             flops=4 * 5 * 2 * slots * model * hidden,
@@ -215,28 +216,21 @@
     )(rows, *blocks)
 
 
-def finish_kernel(own_ref, peer_ref, came_ref, first_ref, second_ref):
-    hidden = second_ref.shape[0]
+def finish_kernel(flip, own_ref, peer_ref, came_ref, out_ref):
     total = own_ref[...].astype(f32) + peer_ref[...].astype(f32) + came_ref[...].astype(f32)
-    first_ref[...] = total[:hidden, :].T.astype(bf16)
-    second_ref[...] = total[hidden:, :].astype(bf16)
-
-
-def finish(own, peer, came):
-    hidden, model = own.shape[0] // 2, own.shape[1]
-    part = pl.BlockSpec((2 * hidden, 512), lambda j: (0, j))
-    return pl.pallas_call(
-        finish_kernel,
+    out_ref[...] = (total.T if flip else total).astype(bf16)
+
+
+def finish(own, peer, came, flip):
+    hidden, model = own.shape
+    part = pl.BlockSpec((hidden, 512), lambda j: (0, j))
+    return pl.pallas_call(
+        functools.partial(finish_kernel, flip),
         grid=(model // 512,),
-        out_shape=(
-            jax.ShapeDtypeStruct((model, hidden), bf16),
-            jax.ShapeDtypeStruct((hidden, model), bf16),
-        ),
+        out_shape=jax.ShapeDtypeStruct((model, hidden) if flip else (hidden, model), bf16),
         in_specs=[part] * 3,
-        out_specs=(
-            pl.BlockSpec((512, hidden), lambda j: (j, 0)),
-            pl.BlockSpec((hidden, 512), lambda j: (0, j)),
-        ),
+        out_specs=pl.BlockSpec((512, hidden), lambda j: (j, 0)) if flip else part,
+        cost_estimate=pl.CostEstimate(flops=0, bytes_accessed=8 * own.size, transcendentals=0),
         name="finish",
     )(own, peer, came)
 
@@ -257,21 +251,32 @@
     oth_in = hold(lax.ppermute(own_in, "yl", SWAP), HOLD_FLOPS)
     outgoing, target = dispatch(expert_ids.T, gates, tokens, d_out, experts)
     arrived = exchange(outgoing.reshape(experts, 4 * width, LANES), groups)
+    oth_out = lax.ppermute(own_out, "yl", SWAP)
     own_in, own_out, oth_in = lax.optimization_barrier((own_in, own_out, oth_in))
-    oth_out = lax.ppermute(own_out, "yl", SWAP)
     near = [own_in, own_out, lax.ppermute(own_in, "core", SWAP), lax.ppermute(own_out, "core", SWAP)]
     far = [oth_in, oth_out, lax.ppermute(oth_in, "core", SWAP), lax.ppermute(oth_out, "core", SWAP)]
     arrived, *blocks = lax.optimization_barrier((arrived, *near, *far))
     rows = arrived.reshape(slots, 2 * model)
-    own_grad, peer_grad, far_own, far_peer, back = run_experts(rows, blocks)
+    own_gi, own_go, peer_gi, peer_go, far_gi, far_go, send_gi, send_go, back = run_experts(rows, blocks)
+
+    def add(a, b):
+        return (a.astype(f32) + b.astype(f32)).astype(bf16)
+
+    sum_in = add(far_gi, lax.ppermute(send_gi, "core", SWAP))
+    came_in = hold(lax.ppermute(sum_in, "yl", SWAP), HOLD_FLOPS)
+    back, send_go, _ = lax.optimization_barrier((back, send_go, sum_in))
     returned = exchange(back, groups)
-    far_peer = hold(lax.ppermute(far_peer, "core", SWAP), HOLD_FLOPS)
-    far_sum = (far_own.astype(f32) + far_peer.astype(f32)).astype(bf16)
-    came = lax.ppermute(far_sum, "yl", SWAP)
-    near_peer = lax.ppermute(peer_grad, "core", SWAP)
+    got_go = hold(lax.ppermute(send_go, "core", SWAP), HOLD_FLOPS)
+    sum_out = add(far_go, got_go)
+    sum_out, peer_gi, peer_go = lax.optimization_barrier((sum_out, peer_gi, peer_go))
+    came_out = lax.ppermute(sum_out, "yl", SWAP)
+    near_in = lax.ppermute(peer_gi, "core", SWAP)
+    near_out = lax.ppermute(peer_go, "core", SWAP)
+    d_first = finish(own_gi, near_in, came_in, True)
+    returned, d_first = lax.optimization_barrier((returned, d_first))
     d_tokens, d_gates = combine(target, returned, gates, model)
-    came, d_tokens, d_gates = lax.optimization_barrier((came, d_tokens, d_gates))
-    d_first, d_second = finish(own_grad, near_peer, came)
+    came_out, d_tokens, d_gates = lax.optimization_barrier((came_out, d_tokens, d_gates))
+    d_second = finish(own_go, near_out, came_out, False)
     return (d_tokens, d_gates.T, d_first[None], d_second[None])
 
 

time: 211 us -> 200 us (0.948)
  the two profiles are of different devices: /device:TPU:20 before, /device:TPU:48 now
where the time goes in v5:
time: 200 us; the launch traced here: 199 us
  waiting for transfers between devices  98.1 us (49%)
  starting transfers between devices  61.4 us (31%)
  Pallas kernels  25.9 us (13%)
  local copies, waits for them, and re-layouts  8.19 us (4%)
  other arithmetic  4.2 us (2%)
    ppermute x1, waiting for transfers between devices, on_device(): oth_out = lax.ppermute(own_out, 'yl', SWAP)  48.5 us
    all_to_all x2, starting transfers between devices, exchange(): lax.all_to_all(x, AXES, split_axis=0, concat_axis=0, axis_index_groups=gr...  35.7 us
    ppermute x1, waiting for transfers between devices, on_device(): came_out = lax.ppermute(sum_out, 'yl', SWAP)  12.4 us
    ppermute x1, waiting for transfers between devices, on_device(): came_in = hold(lax.ppermute(sum_in, 'yl', SWAP), HOLD_FLOPS)  11.8 us
    pallas_call x1, Pallas kernels, run_experts(): pl.pallas_call(experts_kernel, out_shape=(jax.ShapeDtypeStruct((hidden, m...  11.5 us
    ppermute x1, waiting for transfers between devices, on_device(): oth_in = hold(lax.ppermute(own_in, 'yl', SWAP), HOLD_FLOPS)  11.2 us
    all_to_all x2, waiting for transfers between devices, exchange(): lax.all_to_all(x, AXES, split_axis=0, concat_axis=0, axis_index_groups=gr...  10.8 us
    pallas_call x2, Pallas kernels, finish(): pl.pallas_call(functools.partial(finish_kernel, flip), grid=(model // 512...  7.9 us
  transfers between devices with their start and end apart: 14, of which 7 were waited for; matrix products, arithmetic and copies ran while one was open for 1% of the time, Pallas kernels for 5%

profile of v5, /device:TPU:48, one launch (start us, length us, event | category | flops | bytes accessed | tf_op | source)
XLA Modules:
  0.0 198.7 jit_solution(14005969282037689692)
XLA Ops:
  0.6 2.6 %collective-permute-start = (bf16[2048,256]{1,0:T(8,128)(2,1)}, bf16[2048,256]{1,0:T(8,128)(2,1)}, u32[]{:S(2)}, u32[]{:S(2)}) collective-permute-start(bf16[2048,256]{1,0:T(8,128)(2,1)} %bitcast.14), channel_id=1, source_target_pairs={{0,2},{2,0},{1,3},{3,1},{4,6},{6,4},{5,7},{7,5},{8,10},{10,8},{9,1... | collective-permute-start | bytes 3145736 | tf_op jit(solution)/shard_map/ppermute | solution.py:251
  3.2 3.7 %dispatch.1 = (bf16[256,32,128]{2,1,0:T(8,128)(2,1)}, s32[4,32]{1,0:T(4,128)}) custom-call(s32[4,32]{1,0:T(4,128)} %bitcast.13, f32[4,32]{1,0:T(4,128)} %bitcast.11, bf16[32,2048]{1,0:T(8,128)(2,1)} %tok_ref.1, bf16[32,2048]{1,0:T(8,128)(2,1)} %dout_ref.1), custom_call_target="tpu_custom_call" | custom-call | tf_op jit(solution)/shard_map/dispatch/pallas_call | solution.py:60
  6.9 19.3 %all-to-all-start = ((bf16[128,64,128]{2,1,0:T(8,128)(2,1)}), bf16[128,64,128]{2,1,0:T(8,128)(2,1)S(1)}, u32[]{:S(2)}, u32[]{:S(2)}) async-start(bf16[128,64,128]{2,1,0:T(8,128)(2,1)} %bitcast.8), calls=%async_computation | async-start | bytes 4194304 | tf_op jit(solution)/shard_map/all_to_all | solution.py:239
  26.2 0.0 copy-start.4
  26.2 2.5 %collective-permute-start.3 = (bf16[256,2048]{1,0:T(8,128)(2,1)}, bf16[256,2048]{1,0:T(8,128)(2,1)}, u32[]{:S(2)}, u32[]{:S(2)}) collective-permute-start(bf16[256,2048]{1,0:T(8,128)(2,1)} %bitcast.17), channel_id=1, source_target_pairs={{0,2},{2,0},{1,3},{3,1},{4,6},{6,4},{5,7},{7,5},{8,10},{10,8},{9,1... | collective-permute-start | bytes 3145736 | tf_op jit(solution)/shard_map/ppermute | solution.py:254
  28.7 11.2 %collective-permute-done.x_ref = bf16[2048,256]{1,0:T(8,128)(2,1)} collective-permute-done((bf16[2048,256]{1,0:T(8,128)(2,1)}, bf16[2048,256]{1,0:T(8,128)(2,1)}, u32[]{:S(2)}, u32[]{:S(2)}) %collective-permute-start) | collective-permute-done | bytes 1048608 | tf_op jit(solution)/shard_map/ppermute | solution.py:251
  39.9 0.0 copy-done.4
  39.9 1.9 collective-permute-start.1
  41.9 2.4 %collective-permute-start.2 = (bf16[256,2048]{1,0:T(8,128)(2,1)}, bf16[256,2048]{1,0:T(8,128)(2,1)S(1)}, u32[]{:S(2)}, u32[]{:S(2)}) collective-permute-start(bf16[256,2048]{1,0:T(8,128)(2,1)} %bitcast.18), channel_id=1, source_target_pairs={{0,1},{1,0},{2,3},{3,2},{4,5},{5,4},{6,7},{7,6},{8,9},{9,8},{10,11... | collective-permute-start | bytes 3145736 | tf_op jit(solution)/shard_map/ppermute | solution.py:256
  44.3 1.9 collective-permute-start.4
  46.2 48.5 %collective-permute-done.3.refs_5_ = bf16[256,2048]{1,0:T(8,128)(2,1)} collective-permute-done((bf16[256,2048]{1,0:T(8,128)(2,1)}, bf16[256,2048]{1,0:T(8,128)(2,1)}, u32[]{:S(2)}, u32[]{:S(2)}) %collective-permute-start.3) | collective-permute-done | bytes 1048608 | tf_op jit(solution)/shard_map/ppermute | solution.py:254
  94.7 1.9 collective-permute-start.5
  96.6 0.0 collective-permute-done.1.refs_2_
  96.6 0.0 copy-start.5
  96.6 0.0 collective-permute-done.2.refs_3_
  96.6 0.0 copy-start.6
  96.6 0.0 collective-permute-done.4.refs_6_
  96.6 0.9 copy-done.5
  97.6 0.3 copy-done.6
  97.9 0.0 copy-start.7
  97.9 1.0 copy-done.7
  98.9 0.7 collective-permute-done.5.refs_7_
  99.5 0.0 all-to-all-done
  99.6 2.3 %reshape.15.rows_hbm = bf16[256,4096]{1,0:T(8,128)(2,1)} reshape(bf16[128,64,128]{2,1,0:T(8,128)(2,1)S(1)} %all-to-all-done) | data formatting | bytes 4194304 | tf_op jit(solution)/shard_map/reshape | solution.py:259
  101.8 11.5 %experts.1 = (bf16[256,2048]{1,0:T(8,128)(2,1)}, bf16[256,2048]{1,0:T(8,128)(2,1)}, bf16[256,2048]{1,0:T(8,128)(2,1)}, bf16[256,2048]{1,0:T(8,128)(2,1)}, bf16[2...) custom-call(bf16[256,4096]{1,0:T(8,128)(2,1)} %reshape.15.rows_hbm, ...), custom_call_target="tpu_custom_call" | custom-call | flops 5368709120 | bytes 18874368 | tf_op jit(solution)/shard_map/experts/pallas_call | solution.py:194
  113.3 2.0 %collective-permute-start.6 = (bf16[256,2048]{1,0:T(8,128)(2,1)}, bf16[256,2048]{1,0:T(8,128)(2,1)S(1)}, u32[]{:S(2)}, u32[]{:S(2)}) collective-permute-start(bf16[256,2048]{1,0:T(8,128)(2,1)} %get-tuple-element.56), channel_id=1, source_target_pairs={{0,1},{1,0},{2,3},{3,2},{4,5},{5,4},{6,7},{7,6},{8,9},{9,8},{10,11... | collective-permute-start | bytes 3145736 | tf_op jit(solution)/shard_map/ppermute | solution.py:265
  115.4 2.7 %collective-permute-done.6 = bf16[256,2048]{1,0:T(8,128)(2,1)S(1)} collective-permute-done((bf16[256,2048]{1,0:T(8,128)(2,1)}, bf16[256,2048]{1,0:T(8,128)(2,1)S(1)}, u32[]{:S(2)}, u32[]{:S(2)}) %collective-permute-start.6) | collective-permute-done | bytes 1048608 | tf_op jit(solution)/shard_map/ppermute | solution.py:265
  118.1 2.6 %add_convert_fusion.1 = bf16[256,2048]{1,0:T(8,128)(2,1)} fusion(bf16[256,2048]{1,0:T(8,128)(2,1)S(1)} %collective-permute-done.6, bf16[256,2048]{1,0:T(8,128)(2,1)} %get-tuple-element.55), kind=kLoop, calls=%fused_computation.1 | loop fusion | flops 2097152 | bytes 3145728 | tf_op jit(solution)/shard_map/convert_element_type | solution.py:263
  120.7 2.0 %collective-permute-start.7 = (bf16[256,2048]{1,0:T(8,128)(2,1)}, bf16[256,2048]{1,0:T(8,128)(2,1)S(1)}, u32[]{:S(2)}, u32[]{:S(2)}) collective-permute-start(bf16[256,2048]{1,0:T(8,128)(2,1)} %get-tuple-element.57), channel_id=1, source_target_pairs={{0,1},{1,0},{2,3},{3,2},{4,5},{5,4},{6,7},{7,6},{8,9},{9,8},{10,11... | collective-permute-start | bytes 3145736 | tf_op jit(solution)/shard_map/ppermute | solution.py:269
  122.7 1.9 collective-permute-start.10
  124.7 16.5 %all-to-all-start.1 = ((bf16[128,40,128]{2,1,0:T(8,128)(2,1)}), bf16[128,40,128]{2,1,0:T(8,128)(2,1)S(1)}, u32[]{:S(2)}, u32[]{:S(2)}) async-start(bf16[128,40,128]{2,1,0:T(8,128)(2,1)} %get-tuple-element.62), calls=%async_computation.1 | async-start | bytes 2621440 | tf_op jit(solution)/shard_map/all_to_all | solution.py:239
  141.1 0.0 copy-start.1
  141.1 0.0 collective-permute-done.7.x_ref
  141.1 0.0 copy-start.2
  141.2 1.0 copy-done.2
  142.1 0.6 copy-done.1
  142.7 1.6 add_convert_fusion
  144.3 2.1 %collective-permute-start.8 = (bf16[256,2048]{1,0:T(8,128)(2,1)S(1)}, bf16[256,2048]{1,0:T(8,128)(2,1)S(1)}, u32[]{:S(2)}, u32[]{:S(2)}) collective-permute-start(bf16[256,2048]{1,0:T(8,128)(2,1)S(1)} %add_convert_fusion), channel_id=1, source_target_pairs={{0,2},{2,0},{1,3},{3,1},{4,6},{6,4},{5,7},{7,5},{8,10},{10,8},{9,1... | collective-permute-start | bytes 3145736 | tf_op jit(solution)/shard_map/ppermute | solution.py:272
  146.5 1.9 collective-permute-start.9
  148.4 2.4 %collective-permute-start.11 = (bf16[256,2048]{1,0:T(8,128)(2,1)}, bf16[256,2048]{1,0:T(8,128)(2,1)}, u32[]{:S(2)}, u32[]{:S(2)}) collective-permute-start(bf16[256,2048]{1,0:T(8,128)(2,1)} %get-tuple-element.72), channel_id=1, source_target_pairs={{0,1},{1,0},{2,3},{3,2},{4,5},{5,4},{6,7},{7,6},{8,9},{9,8},{10,11... | collective-permute-start | bytes 3145736 | tf_op jit(solution)/shard_map/ppermute | solution.py:274
  150.8 11.8 %collective-permute-done.10.x_ref = bf16[256,2048]{1,0:T(8,128)(2,1)} collective-permute-done((bf16[256,2048]{1,0:T(8,128)(2,1)}, bf16[256,2048]{1,0:T(8,128)(2,1)}, u32[]{:S(2)}, u32[]{:S(2)}) %collective-permute-start.10) | collective-permute-done | bytes 1048608 | tf_op jit(solution)/shard_map/ppermute | solution.py:266
  162.6 0.0 collective-permute-done.9.peer_ref
  162.6 4.0 %finish.2 = bf16[2048,256]{1,0:T(8,128)(2,1)} custom-call(bf16[256,2048]{1,0:T(8,128)(2,1)} %get-tuple-element.63.own_ref, bf16[256,2048]{1,0:T(8,128)(2,1)} %collective-permute-done.9.peer_ref, bf16[256,2048]{1,0:T(8,128)(2,1)} %hold.5.came_ref), custom_call_target="tpu_custom_call" | custom-call | bytes 4194304 | tf_op jit(solution)/shard_map/finish/pallas_call | solution.py:227
  166.7 10.8 %all-to-all-done.1.back_ref = bf16[128,40,128]{2,1,0:T(8,128)(2,1)S(1)} async-done(((bf16[128,40,128]{2,1,0:T(8,128)(2,1)}), bf16[128,40,128]{2,1,0:T(8,128)(2,1)S(1)}, u32[]{:S(2)}, u32[]{:S(2)}) %all-to-all-start.1) | async-done | bytes 1310752 | tf_op jit(solution)/shard_map/all_to_all | solution.py:239
  177.5 0.0 copy-start
  177.5 1.1 copy-done
  178.6 2.9 %combine.1 = (bf16[32,2048]{1,0:T(8,128)(2,1)}, f32[4,32]{1,0:T(4,128)}) custom-call(s32[4,32]{1,0:T(4,128)} %get-tuple-element.61.target_ref, bf16[128,40,128]{2,1,0:T(8,128)(2,1)} %copy-done, f32[4,32]{1,0:T(4,128)} %bitcast.12), custom_call_target="tpu_custom_call" | custom-call | tf_op jit(solution)/shard_map/combine/pallas_call | solution.py:120
  181.4 12.4 %collective-permute-done.8.came_ref = bf16[256,2048]{1,0:T(8,128)(2,1)S(1)} collective-permute-done((bf16[256,2048]{1,0:T(8,128)(2,1)S(1)}, bf16[256,2048]{1,0:T(8,128)(2,1)S(1)}, u32[]{:S(2)}, u32[]{:S(2)}) %collective-permute-start.8) | collective-permute-done | bytes 1048608 | tf_op jit(solution)/shard_map/ppermute | solution.py:272
  193.8 0.0 copy-start.3
  193.8 0.0 collective-permute-done.11.peer_ref
  193.8 1.0 copy-done.3
  194.8 3.9 %finish.3 = bf16[256,2048]{1,0:T(8,128)(2,1)} custom-call(bf16[256,2048]{1,0:T(8,128)(2,1)} %get-tuple-element.71.own_ref, bf16[256,2048]{1,0:T(8,128)(2,1)} %collective-permute-done.11.peer_ref, bf16[256,2048]{1,0:T(8,128)(2,1)} %copy-done.3), custom_call_target="tpu_custom_call" | custom-call | bytes 4194304 | tf_op jit(solution)/shard_map/finish/pallas_call | solution.py:227
  (3 shorter events, 0.0 us)
Async XLA Ops:
  0.6 39.3 %collective-permute-start = (bf16[2048,256]{1,0:T(8,128)(2,1)}, bf16[2048,256]{1,0:T(8,128)(2,1)}, u32[]{:S(2)}, u32[]{:S(2)}) collective-permute-start(bf16[2048,256]{1,0:T(8,128)(2,1)} %bitcast.14), channel_id=1, source_target_pairs={{0,2},{2,0},{1,3},{3,1},{4,6},{6,4},{5,7},{7,5},{8,10},{10,8},{9,1... | collective-permute-start | bytes 3145736 | tf_op jit(solution)/shard_map/ppermute | solution.py:251
  6.9 92.6 %all-to-all-start = ((bf16[128,64,128]{2,1,0:T(8,128)(2,1)}), bf16[128,64,128]{2,1,0:T(8,128)(2,1)S(1)}, u32[]{:S(2)}, u32[]{:S(2)}) async-start(bf16[128,64,128]{2,1,0:T(8,128)(2,1)} %bitcast.8), calls=%async_computation | async-start | bytes 4194304 | tf_op jit(solution)/shard_map/all_to_all | solution.py:239
  26.2 13.7 %copy-start.4 = (bf16[1,2048,256]{2,1,0:T(8,128)(2,1)S(1)}, bf16[1,2048,256]{2,1,0:T(8,128)(2,1)}, u32[]{:S(2)}) copy-start(bf16[1,2048,256]{2,1,0:T(8,128)(2,1)} %param.10) | copy-start | bytes 3145732
  26.2 68.5 %collective-permute-start.3 = (bf16[256,2048]{1,0:T(8,128)(2,1)}, bf16[256,2048]{1,0:T(8,128)(2,1)}, u32[]{:S(2)}, u32[]{:S(2)}) collective-permute-start(bf16[256,2048]{1,0:T(8,128)(2,1)} %bitcast.17), channel_id=1, source_target_pairs={{0,2},{2,0},{1,3},{3,1},{4,6},{6,4},{5,7},{7,5},{8,10},{10,8},{9,1... | collective-permute-start | bytes 3145736 | tf_op jit(solution)/shard_map/ppermute | solution.py:254
  39.9 56.6 %collective-permute-start.1 = (bf16[2048,256]{1,0:T(8,128)(2,1)S(1)}, bf16[2048,256]{1,0:T(8,128)(2,1)S(1)}, u32[]{:S(2)}, u32[]{:S(2)}) collective-permute-start(bf16[2048,256]{1,0:T(8,128)(2,1)S(1)} %bitcast.16), channel_id=1, source_target_pairs={{0,1},{1,0},{2,3},{3,2},{4,5},{5,4},{6,7},{7,6},{8,9},{9,8},{10,11... | collective-permute-start | bytes 3145736 | tf_op jit(solution)/shard_map/ppermute | solution.py:256
  41.9 54.8 %collective-permute-start.2 = (bf16[256,2048]{1,0:T(8,128)(2,1)}, bf16[256,2048]{1,0:T(8,128)(2,1)S(1)}, u32[]{:S(2)}, u32[]{:S(2)}) collective-permute-start(bf16[256,2048]{1,0:T(8,128)(2,1)} %bitcast.18), channel_id=1, source_target_pairs={{0,1},{1,0},{2,3},{3,2},{4,5},{5,4},{6,7},{7,6},{8,9},{9,8},{10,11... | collective-permute-start | bytes 3145736 | tf_op jit(solution)/shard_map/ppermute | solution.py:256
  44.3 52.4 %collective-permute-start.4 = (bf16[2048,256]{1,0:T(8,128)(2,1)}, bf16[2048,256]{1,0:T(8,128)(2,1)S(1)}, u32[]{:S(2)}, u32[]{:S(2)}) collective-permute-start(bf16[2048,256]{1,0:T(8,128)(2,1)} %hold.3.refs_4_), channel_id=1, source_target_pairs={{0,1},{1,0},{2,3},{3,2},{4,5},{5,4},{6,7},{7,6},{8,9},{9,8},{10,11... | collective-permute-start | bytes 3145736 | tf_op jit(solution)/shard_map/ppermute | solution.py:257
  94.7 4.9 %collective-permute-start.5 = (bf16[256,2048]{1,0:T(8,128)(2,1)}, bf16[256,2048]{1,0:T(8,128)(2,1)}, u32[]{:S(2)}, u32[]{:S(2)}) collective-permute-start(bf16[256,2048]{1,0:T(8,128)(2,1)} %collective-permute-done.3.refs_5_), channel_id=1, source_target_pairs={{0,1},{1,0},{2,3},{3,2},{4,5},{5,4},{6,7},{7,6},{8,9},{9,8},{10,11... | collective-permute-start | bytes 3145736 | tf_op jit(solution)/shard_map/ppermute | solution.py:257
  96.6 1.0 copy-start.5
  96.6 1.3 copy-start.6
  97.9 1.0 copy-start.7
  113.3 4.8 %collective-permute-start.6 = (bf16[256,2048]{1,0:T(8,128)(2,1)}, bf16[256,2048]{1,0:T(8,128)(2,1)S(1)}, u32[]{:S(2)}, u32[]{:S(2)}) collective-permute-start(bf16[256,2048]{1,0:T(8,128)(2,1)} %get-tuple-element.56), channel_id=1, source_target_pairs={{0,1},{1,0},{2,3},{3,2},{4,5},{5,4},{6,7},{7,6},{8,9},{9,8},{10,11... | collective-permute-start | bytes 3145736 | tf_op jit(solution)/shard_map/ppermute | solution.py:265
  120.7 20.4 %collective-permute-start.7 = (bf16[256,2048]{1,0:T(8,128)(2,1)}, bf16[256,2048]{1,0:T(8,128)(2,1)S(1)}, u32[]{:S(2)}, u32[]{:S(2)}) collective-permute-start(bf16[256,2048]{1,0:T(8,128)(2,1)} %get-tuple-element.57), channel_id=1, source_target_pairs={{0,1},{1,0},{2,3},{3,2},{4,5},{5,4},{6,7},{7,6},{8,9},{9,8},{10,11... | collective-permute-start | bytes 3145736 | tf_op jit(solution)/shard_map/ppermute | solution.py:269
  122.7 39.9 %collective-permute-start.10 = (bf16[256,2048]{1,0:T(8,128)(2,1)}, bf16[256,2048]{1,0:T(8,128)(2,1)}, u32[]{:S(2)}, u32[]{:S(2)}) collective-permute-start(bf16[256,2048]{1,0:T(8,128)(2,1)} %add_convert_fusion.1), channel_id=1, source_target_pairs={{0,2},{2,0},{1,3},{3,1},{4,6},{6,4},{5,7},{7,5},{8,10},{10,8},{9,1... | collective-permute-start | bytes 3145736 | tf_op jit(solution)/shard_map/ppermute | solution.py:266
  124.7 52.8 %all-to-all-start.1 = ((bf16[128,40,128]{2,1,0:T(8,128)(2,1)}), bf16[128,40,128]{2,1,0:T(8,128)(2,1)S(1)}, u32[]{:S(2)}, u32[]{:S(2)}) async-start(bf16[128,40,128]{2,1,0:T(8,128)(2,1)} %get-tuple-element.62), calls=%async_computation.1 | async-start | bytes 2621440 | tf_op jit(solution)/shard_map/all_to_all | solution.py:239
  141.1 1.6 copy-start.1
  141.1 1.0 copy-start.2
  144.3 49.5 %collective-permute-start.8 = (bf16[256,2048]{1,0:T(8,128)(2,1)S(1)}, bf16[256,2048]{1,0:T(8,128)(2,1)S(1)}, u32[]{:S(2)}, u32[]{:S(2)}) collective-permute-start(bf16[256,2048]{1,0:T(8,128)(2,1)S(1)} %add_convert_fusion), channel_id=1, source_target_pairs={{0,2},{2,0},{1,3},{3,1},{4,6},{6,4},{5,7},{7,5},{8,10},{10,8},{9,1... | collective-permute-start | bytes 3145736 | tf_op jit(solution)/shard_map/ppermute | solution.py:272
  146.5 16.1 %collective-permute-start.9 = (bf16[256,2048]{1,0:T(8,128)(2,1)}, bf16[256,2048]{1,0:T(8,128)(2,1)}, u32[]{:S(2)}, u32[]{:S(2)}) collective-permute-start(bf16[256,2048]{1,0:T(8,128)(2,1)} %get-tuple-element.64), channel_id=1, source_target_pairs={{0,1},{1,0},{2,3},{3,2},{4,5},{5,4},{6,7},{7,6},{8,9},{9,8},{10,11... | collective-permute-start | bytes 3145736 | tf_op jit(solution)/shard_map/ppermute | solution.py:273
  148.4 45.4 %collective-permute-start.11 = (bf16[256,2048]{1,0:T(8,128)(2,1)}, bf16[256,2048]{1,0:T(8,128)(2,1)}, u32[]{:S(2)}, u32[]{:S(2)}) collective-permute-start(bf16[256,2048]{1,0:T(8,128)(2,1)} %get-tuple-element.72), channel_id=1, source_target_pairs={{0,1},{1,0},{2,3},{3,2},{4,5},{5,4},{6,7},{7,6},{8,9},{9,8},{10,11... | collective-permute-start | bytes 3145736 | tf_op jit(solution)/shard_map/ppermute | solution.py:274
  177.5 1.1 copy-start
  193.8 1.0 copy-start.3

commit v6 on v5

--- a/solution.py
+++ b/solution.py
@@ -138,25 +138,40 @@
 
 
 def experts_kernel(rows_hbm, *refs):
-    blocks, stores_to, back_ref = refs[:8], refs[8:16], refs[16]
-    rows, ins, outs, grads, total, lines, in_sems, out_sems = refs[17:]
+    blocks, stores_to, back_ref = refs[:10], refs[10:18], refs[18]
+    rows, ins, outs, grads, total, lines, in_sems, out_sems = refs[19:]
     hidden, model = outs.shape[1], outs.shape[2]
     slots, width = rows.shape[0], model // LANES
     experts = slots // 2
+    half = hidden // 2
     loads = [pltpu.make_async_copy(rows_hbm, rows, in_sems.at[0])]
+    places = []
     for q in range(4):
-        loads.append(pltpu.make_async_copy(blocks[2 * q], ins.at[q], in_sems.at[1 + 2 * q]))
-        loads.append(pltpu.make_async_copy(blocks[2 * q + 1], outs.at[q], in_sems.at[2 + 2 * q]))
-    stores = [
-        pltpu.make_async_copy(grads.at[q], g, out_sems.at[q]) for q, g in enumerate(stores_to)
+        places.append((q, ins.at[q]))
+        if q < 2:
+            places.append((q, outs.at[q]))
+        else:
+            places += [(q, outs.at[q, pl.ds(0, half), :]), (q, outs.at[q, pl.ds(half, half), :])]
+    loads += [
+        pltpu.make_async_copy(block, place, in_sems.at[1 + n])
+        for n, (block, (_, place)) in enumerate(zip(blocks, places))
     ]
+    stores = []
+    for q in range(4):
+        cut = hidden if q < 2 else hidden + half
+        first = pltpu.make_async_copy(grads.at[q, pl.ds(0, cut), :], stores_to[2 * q], out_sems.at[2 * q])
+        second = pltpu.make_async_copy(
+            grads.at[q, pl.ds(cut, 2 * hidden - cut), :], stores_to[2 * q + 1], out_sems.at[2 * q + 1]
+        )
+        stores += [first, second]
     for load in loads:
         load.start()
     loads[0].wait()
     gate = jnp.zeros((slots, 1), f32)
     for q in range(4):
-        loads[1 + 2 * q].wait()
-        loads[2 + 2 * q].wait()
+        for load, (user, _) in zip(loads[1:], places):
+            if user == q:
+                load.wait()
         preact = dot(rows[:, :model], ins[q], 1, 0)
         pulled = dot(rows[:, model:], outs[q], 1, 1)
         sig = jax.nn.sigmoid(preact)
@@ -164,8 +179,8 @@
         d_pre = (pulled * sig * (1.0 + preact * (1.0 - sig))).astype(bf16)
         gate += jnp.sum(act * pulled, axis=1, keepdims=True)
         act = act.astype(bf16)
-        grads[2 * q] = dot(d_pre, rows[:, :model], 0, 0).astype(bf16)
-        grads[2 * q + 1] = dot(act, rows[:, model:], 0, 0).astype(bf16)
+        grads[q, :hidden, :] = dot(d_pre, rows[:, :model], 0, 0).astype(bf16)
+        grads[q, hidden:, :] = dot(act, rows[:, model:], 0, 0).astype(bf16)
         stores[2 * q].start()
         stores[2 * q + 1].start()
         part = dot(d_pre, ins[q], 1, 1)
@@ -193,18 +208,21 @@
     vmem = pl.BlockSpec(memory_space=pltpu.VMEM)
     return pl.pallas_call(
         experts_kernel,
-        out_shape=(jax.ShapeDtypeStruct((hidden, model), bf16),) * 8
+        out_shape=tuple(
+            jax.ShapeDtypeStruct((r, model), bf16)
+            for r in [hidden] * 4 + [hidden + hidden // 2, hidden // 2] * 2
+        )
         + (jax.ShapeDtypeStruct((slots // 2, 2 * width + GATE_ROWS, LANES), bf16),),
-        in_specs=[anywhere] * 9,
+        in_specs=[anywhere] * 11,
         out_specs=(anywhere,) * 8 + (vmem,),
         scratch_shapes=[
             pltpu.VMEM(rows.shape, bf16),
             pltpu.VMEM((4, model, hidden), bf16),
             pltpu.VMEM((4, hidden, model), bf16),
-            pltpu.VMEM((8, hidden, model), bf16),
+            pltpu.VMEM((4, 2 * hidden, model), bf16),
             pltpu.VMEM((slots, model), f32),
             pltpu.VMEM((slots * width, LANES), f32),
-            pltpu.SemaphoreType.DMA((9,)),
+            pltpu.SemaphoreType.DMA((11,)),
             pltpu.SemaphoreType.DMA((8,)),
         ],
         cost_estimate=pl.CostEstimate(
@@ -216,23 +234,48 @@
     )(rows, *blocks)
 
 
-def finish_kernel(flip, own_ref, peer_ref, came_ref, out_ref):
+def finish_first_kernel(own_ref, peer_ref, came_ref, out_ref):
     total = own_ref[...].astype(f32) + peer_ref[...].astype(f32) + came_ref[...].astype(f32)
-    out_ref[...] = (total.T if flip else total).astype(bf16)
-
-
-def finish(own, peer, came, flip):
+    out_ref[...] = total.T.astype(bf16)
+
+
+def finish_second_kernel(own_ref, peer_ref, upper_ref, lower_ref, out_ref):
+    half = upper_ref.shape[0]
+    total = own_ref[...].astype(f32) + peer_ref[...].astype(f32)
+    out_ref[:half, :] = (total[:half, :] + upper_ref[...].astype(f32)).astype(bf16)
+    out_ref[half:, :] = (total[half:, :] + lower_ref[...].astype(f32)).astype(bf16)
+
+
+def finish_first(own, peer, came):
     hidden, model = own.shape
     part = pl.BlockSpec((hidden, 512), lambda j: (0, j))
     return pl.pallas_call(
-        functools.partial(finish_kernel, flip),
+        finish_first_kernel,
         grid=(model // 512,),
-        out_shape=jax.ShapeDtypeStruct((model, hidden) if flip else (hidden, model), bf16),
+        out_shape=jax.ShapeDtypeStruct((model, hidden), bf16),
         in_specs=[part] * 3,
-        out_specs=pl.BlockSpec((512, hidden), lambda j: (j, 0)) if flip else part,
-        cost_estimate=pl.CostEstimate(flops=0, bytes_accessed=8 * own.size, transcendentals=0),
-        name="finish",
+        out_specs=pl.BlockSpec((512, hidden), lambda j: (j, 0)),
+        name="finish_first",
     )(own, peer, came)
+
+
+def finish_second(own, peer, came, rest):
+    hidden, model = own.shape
+    half = hidden // 2
+    part = pl.BlockSpec((hidden, 512), lambda j: (0, j))
+    return pl.pallas_call(
+        finish_second_kernel,
+        grid=(model // 512,),
+        out_shape=jax.ShapeDtypeStruct((hidden, model), bf16),
+        in_specs=[
+            part,
+            part,
+            pl.BlockSpec((half, 512), lambda j: (2, j)),
+            pl.BlockSpec((half, 512), lambda j: (0, j)),
+        ],
+        out_specs=part,
+        name="finish_second",
+    )(own, peer, came, rest)
 
 
 def exchange(x, groups):
@@ -248,35 +291,38 @@
     slots = 2 * experts
     own_in, own_out = w_in[0], w_out[0]
     gates = gate_weights.T
+    half = own_out.shape[0] // 2
     oth_in = hold(lax.ppermute(own_in, "yl", SWAP), HOLD_FLOPS)
+    oth_upper = hold(lax.ppermute(own_out[:half], "yl", SWAP), HOLD_FLOPS)
     outgoing, target = dispatch(expert_ids.T, gates, tokens, d_out, experts)
     arrived = exchange(outgoing.reshape(experts, 4 * width, LANES), groups)
-    oth_out = lax.ppermute(own_out, "yl", SWAP)
     own_in, own_out, oth_in = lax.optimization_barrier((own_in, own_out, oth_in))
+    oth_lower = lax.ppermute(own_out[half:], "yl", SWAP)
     near = [own_in, own_out, lax.ppermute(own_in, "core", SWAP), lax.ppermute(own_out, "core", SWAP)]
-    far = [oth_in, oth_out, lax.ppermute(oth_in, "core", SWAP), lax.ppermute(oth_out, "core", SWAP)]
+    far = [oth_in, oth_upper, oth_lower]
+    far += [lax.ppermute(w, "core", SWAP) for w in far]
     arrived, *blocks = lax.optimization_barrier((arrived, *near, *far))
     rows = arrived.reshape(slots, 2 * model)
-    own_gi, own_go, peer_gi, peer_go, far_gi, far_go, send_gi, send_go, back = run_experts(rows, blocks)
+    own_gi, own_go, peer_gi, peer_go, far_a, far_b, send_a, send_b, back = run_experts(rows, blocks)
 
     def add(a, b):
         return (a.astype(f32) + b.astype(f32)).astype(bf16)
 
-    sum_in = add(far_gi, lax.ppermute(send_gi, "core", SWAP))
-    came_in = hold(lax.ppermute(sum_in, "yl", SWAP), HOLD_FLOPS)
-    back, send_go, _ = lax.optimization_barrier((back, send_go, sum_in))
+    sum_a = add(far_a, lax.ppermute(send_a, "core", SWAP))
+    came_a = hold(lax.ppermute(sum_a, "yl", SWAP), HOLD_FLOPS)
+    back, send_b, _ = lax.optimization_barrier((back, send_b, sum_a))
     returned = exchange(back, groups)
-    got_go = hold(lax.ppermute(send_go, "core", SWAP), HOLD_FLOPS)
-    sum_out = add(far_go, got_go)
-    sum_out, peer_gi, peer_go = lax.optimization_barrier((sum_out, peer_gi, peer_go))
-    came_out = lax.ppermute(sum_out, "yl", SWAP)
+    got_b = hold(lax.ppermute(send_b, "core", SWAP), HOLD_FLOPS)
+    sum_b = add(far_b, got_b)
+    sum_b, peer_gi, peer_go = lax.optimization_barrier((sum_b, peer_gi, peer_go))
+    came_b = lax.ppermute(sum_b, "yl", SWAP)
     near_in = lax.ppermute(peer_gi, "core", SWAP)
     near_out = lax.ppermute(peer_go, "core", SWAP)
-    d_first = finish(own_gi, near_in, came_in, True)
+    d_first = finish_first(own_gi, near_in, came_a)
     returned, d_first = lax.optimization_barrier((returned, d_first))
     d_tokens, d_gates = combine(target, returned, gates, model)
-    came_out, d_tokens, d_gates = lax.optimization_barrier((came_out, d_tokens, d_gates))
-    d_second = finish(own_go, near_out, came_out, False)
+    came_b, d_tokens, d_gates = lax.optimization_barrier((came_b, d_tokens, d_gates))
+    d_second = finish_second(own_go, near_out, came_a, came_b)
     return (d_tokens, d_gates.T, d_first[None], d_second[None])
 
 

time: 200 us -> 199 us (level)
  the two profiles are of different devices: /device:TPU:48 before, /device:TPU:20 now
where the time goes in v6:
time: 199 us; the launch traced here: 198 us
  waiting for transfers between devices  80.2 us (40%)
  starting transfers between devices  74.7 us (38%)
  Pallas kernels  25.9 us (13%)
  local copies, waits for them, and re-layouts  11 us (6%)
  other arithmetic  5.16 us (3%)
    all_to_all x2, starting transfers between devices, exchange(): lax.all_to_all(x, AXES, split_axis=0, concat_axis=0, axis_index_groups=gr...  40 us
    ppermute x1, waiting for transfers between devices, on_device(): oth_lower = lax.ppermute(own_out[half:], 'yl', SWAP)  34.7 us
    all_to_all x2, waiting for transfers between devices, exchange(): lax.all_to_all(x, AXES, split_axis=0, concat_axis=0, axis_index_groups=gr...  19.2 us
    ppermute x1, waiting for transfers between devices, on_device(): came_a = hold(lax.ppermute(sum_a, 'yl', SWAP), HOLD_FLOPS)  15.6 us
    pallas_call x1, Pallas kernels, run_experts(): pl.pallas_call(experts_kernel, out_shape=tuple((jax.ShapeDtypeStruct((r,...  11.5 us
    unnamed x14, local copies, waits for them, and re-layouts  6.03 us
    ppermute x3, starting transfers between devices, on_device(): far += [lax.ppermute(w, 'core', SWAP) for w in far]  6.02 us
    convert_element_type x2, other arithmetic, add(): return (a.astype(f32) + b.astype(f32)).astype(bf16)  5.16 us
  transfers between devices with their start and end apart: 16, of which 6 were waited for; matrix products, arithmetic and copies ran while one was open for 2% of the time, Pallas kernels for 5%

profile of v6, /device:TPU:20, one launch (start us, length us, event | category | flops | bytes accessed | tf_op | source)
XLA Modules:
  0.0 197.9 jit_solution(14344532634183013106)
XLA Ops:
  0.6 3.5 %collective-permute-start = (bf16[2048,256]{1,0:T(8,128)(2,1)}, bf16[2048,256]{1,0:T(8,128)(2,1)}, u32[]{:S(2)}, u32[]{:S(2)}) collective-permute-start(bf16[2048,256]{1,0:T(8,128)(2,1)} %bitcast.19), channel_id=1, source_target_pairs={{0,2},{2,0},{1,3},{3,1},{4,6},{6,4},{5,7},{7,5},{8,10},{10,8},{9,1... | collective-permute-start | bytes 3145736 | tf_op jit(solution)/shard_map/ppermute | solution.py:295
  4.1 1.9 slice_bitcast_fusion
  6.0 2.3 %collective-permute-start.3 = (bf16[128,2048]{1,0:T(8,128)(2,1)}, bf16[128,2048]{1,0:T(8,128)(2,1)}, u32[]{:S(2)}, u32[]{:S(2)}) collective-permute-start(bf16[128,2048]{1,0:T(8,128)(2,1)} %slice_bitcast_fusion), channel_id=1, source_target_pairs={{0,2},{2,0},{1,3},{3,1},{4,6},{6,4},{5,7},{7,5},{8,10},{10,8},{9,1... | collective-permute-start | bytes 1572872 | tf_op jit(solution)/shard_map/ppermute | solution.py:296
  8.4 3.7 %dispatch.1 = (bf16[256,32,128]{2,1,0:T(8,128)(2,1)}, s32[4,32]{1,0:T(4,128)}) custom-call(s32[4,32]{1,0:T(4,128)} %bitcast.18, f32[4,32]{1,0:T(4,128)} %bitcast.16, bf16[32,2048]{1,0:T(8,128)(2,1)} %tok_ref.1, bf16[32,2048]{1,0:T(8,128)(2,1)} %dout_ref.1), custom_call_target="tpu_custom_call" | custom-call | tf_op jit(solution)/shard_map/dispatch/pallas_call | solution.py:60
  12.1 18.9 %all-to-all-start = ((bf16[128,64,128]{2,1,0:T(8,128)(2,1)}), bf16[128,64,128]{2,1,0:T(8,128)(2,1)S(1)}, u32[]{:S(2)}, u32[]{:S(2)}) async-start(bf16[128,64,128]{2,1,0:T(8,128)(2,1)} %bitcast.10), calls=%async_computation | async-start | bytes 4194304 | tf_op jit(solution)/shard_map/all_to_all | solution.py:282
  31.0 0.0 copy-start.2
  31.0 0.0 collective-permute-done.x_ref
  31.0 1.2 copy-done.2
  32.2 0.8 slice.11
  33.0 1.9 collective-permute-start.2
  34.9 3.3 %collective-permute-start.4 = (bf16[128,2048]{1,0:T(8,128)(2,1)}, bf16[128,2048]{1,0:T(8,128)(2,1)}, u32[]{:S(2)}, u32[]{:S(2)}) collective-permute-start(bf16[128,2048]{1,0:T(8,128)(2,1)} %slice.11), channel_id=1, source_target_pairs={{0,2},{2,0},{1,3},{3,1},{4,6},{6,4},{5,7},{7,5},{8,10},{10,8},{9,1... | collective-permute-start | bytes 1572872 | tf_op jit(solution)/shard_map/ppermute | solution.py:300
  38.2 2.1 %collective-permute-start.1 = (bf16[2048,256]{1,0:T(8,128)(2,1)}, bf16[2048,256]{1,0:T(8,128)(2,1)}, u32[]{:S(2)}, u32[]{:S(2)}) collective-permute-start(bf16[2048,256]{1,0:T(8,128)(2,1)} %bitcast.20), channel_id=1, source_target_pairs={{0,1},{1,0},{2,3},{3,2},{4,5},{5,4},{6,7},{7,6},{8,9},{9,8},{10,11... | collective-permute-start | bytes 3145736 | tf_op jit(solution)/shard_map/ppermute | solution.py:301
  40.3 2.2 %collective-permute-start.5 = (bf16[2048,256]{1,0:T(8,128)(2,1)}, bf16[2048,256]{1,0:T(8,128)(2,1)}, u32[]{:S(2)}, u32[]{:S(2)}) collective-permute-start(bf16[2048,256]{1,0:T(8,128)(2,1)} %hold.4.refs_4_), channel_id=1, source_target_pairs={{0,1},{1,0},{2,3},{3,2},{4,5},{5,4},{6,7},{7,6},{8,9},{9,8},{10,11... | collective-permute-start | bytes 3145736 | tf_op jit(solution)/shard_map/ppermute | solution.py:303
  42.5 5.1 %collective-permute-done.3.x_ref = bf16[128,2048]{1,0:T(8,128)(2,1)} collective-permute-done((bf16[128,2048]{1,0:T(8,128)(2,1)}, bf16[128,2048]{1,0:T(8,128)(2,1)}, u32[]{:S(2)}, u32[]{:S(2)}) %collective-permute-start.3) | collective-permute-done | bytes 524320 | tf_op jit(solution)/shard_map/ppermute | solution.py:296
  47.6 1.9 collective-permute-start.6
  49.5 34.7 %collective-permute-done.4.refs_6_ = bf16[128,2048]{1,0:T(8,128)(2,1)} collective-permute-done((bf16[128,2048]{1,0:T(8,128)(2,1)}, bf16[128,2048]{1,0:T(8,128)(2,1)}, u32[]{:S(2)}, u32[]{:S(2)}) %collective-permute-start.4) | collective-permute-done | bytes 524320 | tf_op jit(solution)/shard_map/ppermute | solution.py:300
  84.3 1.9 collective-permute-start.7
  86.2 0.0 collective-permute-done.6.refs_8_
  86.2 0.0 copy-start.5
  86.2 2.1 %collective-permute-done.7.refs_9_ = bf16[128,2048]{1,0:T(8,128)(2,1)S(1)} collective-permute-done((bf16[128,2048]{1,0:T(8,128)(2,1)}, bf16[128,2048]{1,0:T(8,128)(2,1)S(1)}, u32[]{:S(2)}, u32[]{:S(2)}) %collective-permute-start.7) | collective-permute-done | bytes 524320 | tf_op jit(solution)/shard_map/ppermute | solution.py:303
  88.3 0.0 copy-start.6
  88.3 0.0 collective-permute-done.1.refs_2_
  88.3 0.0 collective-permute-done.5.refs_7_
  88.3 0.0 copy-done.5
  88.3 0.8 copy-done.6
  89.1 0.0 collective-permute-done.2.refs_3_
  89.1 0.0 all-to-all-done
  89.1 2.3 %reshape.16.rows_hbm = bf16[256,4096]{1,0:T(8,128)(2,1)} reshape(bf16[128,64,128]{2,1,0:T(8,128)(2,1)S(1)} %all-to-all-done) | data formatting | bytes 4194304 | tf_op jit(solution)/shard_map/reshape | solution.py:305
  91.4 11.5 %experts.1 = (bf16[256,2048]{1,0:T(8,128)(2,1)}, bf16[256,2048]{1,0:T(8,128)(2,1)}, bf16[256,2048]{1,0:T(8,128)(2,1)}, bf16[256,2048]{1,0:T(8,128)(2,1)}, bf16[3...) custom-call(bf16[256,4096]{1,0:T(8,128)(2,1)} %reshape.16.rows_hbm, ...), custom_call_target="tpu_custom_call" | custom-call | flops 5368709120 | bytes 18874368 | tf_op jit(solution)/shard_map/experts/pallas_call | solution.py:209
  102.8 2.0 %collective-permute-start.8 = (bf16[384,2048]{1,0:T(8,128)(2,1)}, bf16[384,2048]{1,0:T(8,128)(2,1)S(1)}, u32[]{:S(2)}, u32[]{:S(2)}) collective-permute-start(bf16[384,2048]{1,0:T(8,128)(2,1)} %get-tuple-element.60), channel_id=1, source_target_pairs={{0,1},{1,0},{2,3},{3,2},{4,5},{5,4},{6,7},{7,6},{8,9},{9,8},{10,11... | collective-permute-start | bytes 4718600 | tf_op jit(solution)/shard_map/ppermute | solution.py:311
  104.9 3.5 %collective-permute-done.8 = bf16[384,2048]{1,0:T(8,128)(2,1)S(1)} collective-permute-done((bf16[384,2048]{1,0:T(8,128)(2,1)}, bf16[384,2048]{1,0:T(8,128)(2,1)S(1)}, u32[]{:S(2)}, u32[]{:S(2)}) %collective-permute-start.8) | collective-permute-done | bytes 1572896 | tf_op jit(solution)/shard_map/ppermute | solution.py:311
  108.3 3.2 %add_convert_fusion = bf16[384,2048]{1,0:T(8,128)(2,1)} fusion(bf16[384,2048]{1,0:T(8,128)(2,1)S(1)} %collective-permute-done.8, bf16[384,2048]{1,0:T(8,128)(2,1)} %get-tuple-element.59), kind=kLoop, calls=%fused_computation | loop fusion | flops 3145728 | bytes 4718592 | tf_op jit(solution)/shard_map/convert_element_type | solution.py:309
  111.5 2.0 %collective-permute-start.9 = (bf16[128,2048]{1,0:T(8,128)(2,1)}, bf16[128,2048]{1,0:T(8,128)(2,1)}, u32[]{:S(2)}, u32[]{:S(2)}) collective-permute-start(bf16[128,2048]{1,0:T(8,128)(2,1)} %get-tuple-element.61), channel_id=1, source_target_pairs={{0,1},{1,0},{2,3},{3,2},{4,5},{5,4},{6,7},{7,6},{8,9},{9,8},{10,11... | collective-permute-start | bytes 1572872 | tf_op jit(solution)/shard_map/ppermute | solution.py:315
  113.6 3.2 %collective-permute-start.12 = (bf16[384,2048]{1,0:T(8,128)(2,1)}, bf16[384,2048]{1,0:T(8,128)(2,1)S(1)}, u32[]{:S(2)}, u32[]{:S(2)}) collective-permute-start(bf16[384,2048]{1,0:T(8,128)(2,1)} %add_convert_fusion), channel_id=1, source_target_pairs={{0,2},{2,0},{1,3},{3,1},{4,6},{6,4},{5,7},{7,5},{8,10},{10,8},{9,1... | collective-permute-start | bytes 4718600 | tf_op jit(solution)/shard_map/ppermute | solution.py:312
  116.8 21.1 %all-to-all-start.1 = ((bf16[128,40,128]{2,1,0:T(8,128)(2,1)}), bf16[128,40,128]{2,1,0:T(8,128)(2,1)S(1)}, u32[]{:S(2)}, u32[]{:S(2)}) async-start(bf16[128,40,128]{2,1,0:T(8,128)(2,1)} %get-tuple-element.66), calls=%async_computation.1 | async-start | bytes 2621440 | tf_op jit(solution)/shard_map/all_to_all | solution.py:282
  138.0 0.0 copy-start.3
  138.0 0.0 collective-permute-done.9.x_ref
  138.0 1.0 copy-done.3
  139.0 2.0 add_convert_fusion.1
  141.0 3.9 %collective-permute-start.10 = (bf16[128,2048]{1,0:T(8,128)(2,1)}, bf16[128,2048]{1,0:T(8,128)(2,1)S(1)}, u32[]{:S(2)}, u32[]{:S(2)}) collective-permute-start(bf16[128,2048]{1,0:T(8,128)(2,1)} %add_convert_fusion.1), channel_id=1, source_target_pairs={{0,2},{2,0},{1,3},{3,1},{4,6},{6,4},{5,7},{7,5},{8,10},{10,8},{9,1... | collective-permute-start | bytes 1572872 | tf_op jit(solution)/shard_map/ppermute | solution.py:318
  144.9 1.9 collective-permute-start.11
  146.8 2.4 %collective-permute-start.13 = (bf16[256,2048]{1,0:T(8,128)(2,1)}, bf16[256,2048]{1,0:T(8,128)(2,1)}, u32[]{:S(2)}, u32[]{:S(2)}) collective-permute-start(bf16[256,2048]{1,0:T(8,128)(2,1)} %get-tuple-element.76), channel_id=1, source_target_pairs={{0,1},{1,0},{2,3},{3,2},{4,5},{5,4},{6,7},{7,6},{8,9},{9,8},{10,11... | collective-permute-start | bytes 3145736 | tf_op jit(solution)/shard_map/ppermute | solution.py:320
  149.2 15.6 %collective-permute-done.12.x_ref = bf16[384,2048]{1,0:T(8,128)(2,1)S(1)} collective-permute-done((bf16[384,2048]{1,0:T(8,128)(2,1)}, bf16[384,2048]{1,0:T(8,128)(2,1)S(1)}, u32[]{:S(2)}, u32[]{:S(2)}) %collective-permute-start.12) | collective-permute-done | bytes 1572896 | tf_op jit(solution)/shard_map/ppermute | solution.py:312
  164.9 0.0 copy-start
  164.9 1.2 copy-done
  166.0 0.0 collective-permute-done.11.peer_ref
  166.0 4.0 %finish_first.1 = bf16[2048,256]{1,0:T(8,128)(2,1)} custom-call(bf16[256,2048]{1,0:T(8,128)(2,1)} %get-tuple-element.67.own_ref, bf16[256,2048]{1,0:T(8,128)(2,1)} %collective-permute-done.11.peer_ref, bf16[384,2048]{1,0:T(8,128)(2,1)} %hold.7.came_ref.upper_ref), custom_call_target="tpu_custom_call" | custom-call | tf_op jit(solution)/shard_map/finish_first/pallas_call | solution.py:252
  170.1 19.2 %all-to-all-done.1.back_ref = bf16[128,40,128]{2,1,0:T(8,128)(2,1)S(1)} async-done(((bf16[128,40,128]{2,1,0:T(8,128)(2,1)}), bf16[128,40,128]{2,1,0:T(8,128)(2,1)S(1)}, u32[]{:S(2)}, u32[]{:S(2)}) %all-to-all-start.1) | async-done | bytes 1310752 | tf_op jit(solution)/shard_map/all_to_all | solution.py:282
  189.3 0.0 copy-start.1
  189.3 1.1 copy-done.1
  190.3 2.9 %combine.1 = (bf16[32,2048]{1,0:T(8,128)(2,1)}, f32[4,32]{1,0:T(4,128)}) custom-call(s32[4,32]{1,0:T(4,128)} %get-tuple-element.65.target_ref, bf16[128,40,128]{2,1,0:T(8,128)(2,1)} %copy-done.1, f32[4,32]{1,0:T(4,128)} %bitcast.17), custom_call_target="tpu_custom_call" | custom-call | tf_op jit(solution)/shard_map/combine/pallas_call | solution.py:120
  193.2 0.0 collective-permute-done.10.lower_ref
  193.2 0.0 copy-start.4
  193.2 0.0 collective-permute-done.13.peer_ref
  193.2 0.8 copy-done.4
  194.0 3.9 %finish_second.1 = bf16[256,2048]{1,0:T(8,128)(2,1)} custom-call(bf16[256,2048]{1,0:T(8,128)(2,1)} %get-tuple-element.75.own_ref, bf16[256,2048]{1,0:T(8,128)(2,1)} %collective-permute-done.13.peer_ref, bf16[384,2048]{1,0:T(8,128)(2,1)} %hold.7.came_ref.upper_ref, bf16[128,2048]{1,0:T(8,128)(2,1)} %copy-done.4), custom_call_target="tpu_custom_call" | custom-call | tf_op jit(solution)/shard_map/finish_second/pallas_call | solution.py:266
  (4 shorter events, 0.0 us)
Async XLA Ops:
  0.6 30.3 %collective-permute-start = (bf16[2048,256]{1,0:T(8,128)(2,1)}, bf16[2048,256]{1,0:T(8,128)(2,1)}, u32[]{:S(2)}, u32[]{:S(2)}) collective-permute-start(bf16[2048,256]{1,0:T(8,128)(2,1)} %bitcast.19), channel_id=1, source_target_pairs={{0,2},{2,0},{1,3},{3,1},{4,6},{6,4},{5,7},{7,5},{8,10},{10,8},{9,1... | collective-permute-start | bytes 3145736 | tf_op jit(solution)/shard_map/ppermute | solution.py:295
  6.0 41.6 %collective-permute-start.3 = (bf16[128,2048]{1,0:T(8,128)(2,1)}, bf16[128,2048]{1,0:T(8,128)(2,1)}, u32[]{:S(2)}, u32[]{:S(2)}) collective-permute-start(bf16[128,2048]{1,0:T(8,128)(2,1)} %slice_bitcast_fusion), channel_id=1, source_target_pairs={{0,2},{2,0},{1,3},{3,1},{4,6},{6,4},{5,7},{7,5},{8,10},{10,8},{9,1... | collective-permute-start | bytes 1572872 | tf_op jit(solution)/shard_map/ppermute | solution.py:296
  12.1 77.0 %all-to-all-start = ((bf16[128,64,128]{2,1,0:T(8,128)(2,1)}), bf16[128,64,128]{2,1,0:T(8,128)(2,1)S(1)}, u32[]{:S(2)}, u32[]{:S(2)}) async-start(bf16[128,64,128]{2,1,0:T(8,128)(2,1)} %bitcast.10), calls=%async_computation | async-start | bytes 4194304 | tf_op jit(solution)/shard_map/all_to_all | solution.py:282
  31.0 1.2 copy-start.2
  33.0 56.1 %collective-permute-start.2 = (bf16[256,2048]{1,0:T(8,128)(2,1)S(1)}, bf16[256,2048]{1,0:T(8,128)(2,1)}, u32[]{:S(2)}, u32[]{:S(2)}) collective-permute-start(bf16[256,2048]{1,0:T(8,128)(2,1)S(1)} %bitcast.14), channel_id=1, source_target_pairs={{0,1},{1,0},{2,3},{3,2},{4,5},{5,4},{6,7},{7,6},{8,9},{9,8},{10,11... | collective-permute-start | bytes 3145736 | tf_op jit(solution)/shard_map/ppermute | solution.py:301
  34.9 49.3 %collective-permute-start.4 = (bf16[128,2048]{1,0:T(8,128)(2,1)}, bf16[128,2048]{1,0:T(8,128)(2,1)}, u32[]{:S(2)}, u32[]{:S(2)}) collective-permute-start(bf16[128,2048]{1,0:T(8,128)(2,1)} %slice.11), channel_id=1, source_target_pairs={{0,2},{2,0},{1,3},{3,1},{4,6},{6,4},{5,7},{7,5},{8,10},{10,8},{9,1... | collective-permute-start | bytes 1572872 | tf_op jit(solution)/shard_map/ppermute | solution.py:300
  38.2 50.1 %collective-permute-start.1 = (bf16[2048,256]{1,0:T(8,128)(2,1)}, bf16[2048,256]{1,0:T(8,128)(2,1)}, u32[]{:S(2)}, u32[]{:S(2)}) collective-permute-start(bf16[2048,256]{1,0:T(8,128)(2,1)} %bitcast.20), channel_id=1, source_target_pairs={{0,1},{1,0},{2,3},{3,2},{4,5},{5,4},{6,7},{7,6},{8,9},{9,8},{10,11... | collective-permute-start | bytes 3145736 | tf_op jit(solution)/shard_map/ppermute | solution.py:301
  40.3 47.9 %collective-permute-start.5 = (bf16[2048,256]{1,0:T(8,128)(2,1)}, bf16[2048,256]{1,0:T(8,128)(2,1)}, u32[]{:S(2)}, u32[]{:S(2)}) collective-permute-start(bf16[2048,256]{1,0:T(8,128)(2,1)} %hold.4.refs_4_), channel_id=1, source_target_pairs={{0,1},{1,0},{2,3},{3,2},{4,5},{5,4},{6,7},{7,6},{8,9},{9,8},{10,11... | collective-permute-start | bytes 3145736 | tf_op jit(solution)/shard_map/ppermute | solution.py:303
  47.6 38.5 %collective-permute-start.6 = (bf16[128,2048]{1,0:T(8,128)(2,1)}, bf16[128,2048]{1,0:T(8,128)(2,1)S(1)}, u32[]{:S(2)}, u32[]{:S(2)}) collective-permute-start(bf16[128,2048]{1,0:T(8,128)(2,1)} %hold.5.refs_5_), channel_id=1, source_target_pairs={{0,1},{1,0},{2,3},{3,2},{4,5},{5,4},{6,7},{7,6},{8,9},{9,8},{10,11... | collective-permute-start | bytes 1572872 | tf_op jit(solution)/shard_map/ppermute | solution.py:303
  84.3 4.0 %collective-permute-start.7 = (bf16[128,2048]{1,0:T(8,128)(2,1)}, bf16[128,2048]{1,0:T(8,128)(2,1)S(1)}, u32[]{:S(2)}, u32[]{:S(2)}) collective-permute-start(bf16[128,2048]{1,0:T(8,128)(2,1)} %collective-permute-done.4.refs_6_), channel_id=1, source_target_pairs={{0,1},{1,0},{2,3},{3,2},{4,5},{5,4},{6,7},{7,6},{8,9},{9,8},{10,11... | collective-permute-start | bytes 1572872 | tf_op jit(solution)/shard_map/ppermute | solution.py:303
  86.2 2.1 %copy-start.5 = (bf16[128,2048]{1,0:T(8,128)(2,1)}, bf16[128,2048]{1,0:T(8,128)(2,1)S(1)}, u32[]{:S(2)}) copy-start(bf16[128,2048]{1,0:T(8,128)(2,1)S(1)} %collective-permute-done.6.refs_8_) | copy-start | bytes 1572868
  88.3 0.8 copy-start.6
  102.8 5.5 %collective-permute-start.8 = (bf16[384,2048]{1,0:T(8,128)(2,1)}, bf16[384,2048]{1,0:T(8,128)(2,1)S(1)}, u32[]{:S(2)}, u32[]{:S(2)}) collective-permute-start(bf16[384,2048]{1,0:T(8,128)(2,1)} %get-tuple-element.60), channel_id=1, source_target_pairs={{0,1},{1,0},{2,3},{3,2},{4,5},{5,4},{6,7},{7,6},{8,9},{9,8},{10,11... | collective-permute-start | bytes 4718600 | tf_op jit(solution)/shard_map/ppermute | solution.py:311
  111.5 26.4 %collective-permute-start.9 = (bf16[128,2048]{1,0:T(8,128)(2,1)}, bf16[128,2048]{1,0:T(8,128)(2,1)}, u32[]{:S(2)}, u32[]{:S(2)}) collective-permute-start(bf16[128,2048]{1,0:T(8,128)(2,1)} %get-tuple-element.61), channel_id=1, source_target_pairs={{0,1},{1,0},{2,3},{3,2},{4,5},{5,4},{6,7},{7,6},{8,9},{9,8},{10,11... | collective-permute-start | bytes 1572872 | tf_op jit(solution)/shard_map/ppermute | solution.py:315
  113.6 51.3 %collective-permute-start.12 = (bf16[384,2048]{1,0:T(8,128)(2,1)}, bf16[384,2048]{1,0:T(8,128)(2,1)S(1)}, u32[]{:S(2)}, u32[]{:S(2)}) collective-permute-start(bf16[384,2048]{1,0:T(8,128)(2,1)} %add_convert_fusion), channel_id=1, source_target_pairs={{0,2},{2,0},{1,3},{3,1},{4,6},{6,4},{5,7},{7,5},{8,10},{10,8},{9,1... | collective-permute-start | bytes 4718600 | tf_op jit(solution)/shard_map/ppermute | solution.py:312
  116.8 72.5 %all-to-all-start.1 = ((bf16[128,40,128]{2,1,0:T(8,128)(2,1)}), bf16[128,40,128]{2,1,0:T(8,128)(2,1)S(1)}, u32[]{:S(2)}, u32[]{:S(2)}) async-start(bf16[128,40,128]{2,1,0:T(8,128)(2,1)} %get-tuple-element.66), calls=%async_computation.1 | async-start | bytes 2621440 | tf_op jit(solution)/shard_map/all_to_all | solution.py:282
  138.0 1.0 copy-start.3
  141.0 52.2 %collective-permute-start.10 = (bf16[128,2048]{1,0:T(8,128)(2,1)}, bf16[128,2048]{1,0:T(8,128)(2,1)S(1)}, u32[]{:S(2)}, u32[]{:S(2)}) collective-permute-start(bf16[128,2048]{1,0:T(8,128)(2,1)} %add_convert_fusion.1), channel_id=1, source_target_pairs={{0,2},{2,0},{1,3},{3,1},{4,6},{6,4},{5,7},{7,5},{8,10},{10,8},{9,1... | collective-permute-start | bytes 1572872 | tf_op jit(solution)/shard_map/ppermute | solution.py:318
  144.9 21.2 %collective-permute-start.11 = (bf16[256,2048]{1,0:T(8,128)(2,1)}, bf16[256,2048]{1,0:T(8,128)(2,1)}, u32[]{:S(2)}, u32[]{:S(2)}) collective-permute-start(bf16[256,2048]{1,0:T(8,128)(2,1)} %get-tuple-element.68), channel_id=1, source_target_pairs={{0,1},{1,0},{2,3},{3,2},{4,5},{5,4},{6,7},{7,6},{8,9},{9,8},{10,11... | collective-permute-start | bytes 3145736 | tf_op jit(solution)/shard_map/ppermute | solution.py:319
  146.8 46.4 %collective-permute-start.13 = (bf16[256,2048]{1,0:T(8,128)(2,1)}, bf16[256,2048]{1,0:T(8,128)(2,1)}, u32[]{:S(2)}, u32[]{:S(2)}) collective-permute-start(bf16[256,2048]{1,0:T(8,128)(2,1)} %get-tuple-element.76), channel_id=1, source_target_pairs={{0,1},{1,0},{2,3},{3,2},{4,5},{5,4},{6,7},{7,6},{8,9},{9,8},{10,11... | collective-permute-start | bytes 3145736 | tf_op jit(solution)/shard_map/ppermute | solution.py:320
  164.9 1.2 copy-start
  189.3 1.1 copy-start.1
  193.2 0.8 copy-start.4

commit v7 on v6

--- a/solution.py
+++ b/solution.py
@@ -13,6 +13,8 @@
 LANES = 128
 AXES = ("dp", "yh", "yl", "core")
 GATE_ROWS = 8
+AHEAD_OUT = 192
+AHEAD_GRAD = 64
 HOLD_FLOPS = int(3e10)
 SWAP = [(0, 1), (1, 0)]
 f32, bf16 = jnp.float32, jnp.bfloat16
@@ -143,7 +145,6 @@
     hidden, model = outs.shape[1], outs.shape[2]
     slots, width = rows.shape[0], model // LANES
     experts = slots // 2
-    half = hidden // 2
     loads = [pltpu.make_async_copy(rows_hbm, rows, in_sems.at[0])]
     places = []
     for q in range(4):
@@ -151,14 +152,15 @@
         if q < 2:
             places.append((q, outs.at[q]))
         else:
-            places += [(q, outs.at[q, pl.ds(0, half), :]), (q, outs.at[q, pl.ds(half, half), :])]
+            ahead, behind = pl.ds(0, AHEAD_OUT), pl.ds(AHEAD_OUT, hidden - AHEAD_OUT)
+            places += [(q, outs.at[q, ahead, :]), (q, outs.at[q, behind, :])]
     loads += [
         pltpu.make_async_copy(block, place, in_sems.at[1 + n])
         for n, (block, (_, place)) in enumerate(zip(blocks, places))
     ]
     stores = []
     for q in range(4):
-        cut = hidden if q < 2 else hidden + half
+        cut = hidden if q < 2 else hidden + AHEAD_GRAD
         first = pltpu.make_async_copy(grads.at[q, pl.ds(0, cut), :], stores_to[2 * q], out_sems.at[2 * q])
         second = pltpu.make_async_copy(
             grads.at[q, pl.ds(cut, 2 * hidden - cut), :], stores_to[2 * q + 1], out_sems.at[2 * q + 1]
@@ -210,7 +212,7 @@
         experts_kernel,
         out_shape=tuple(
             jax.ShapeDtypeStruct((r, model), bf16)
-            for r in [hidden] * 4 + [hidden + hidden // 2, hidden // 2] * 2
+            for r in [hidden] * 4 + [hidden + AHEAD_GRAD, hidden - AHEAD_GRAD] * 2
         )
         + (jax.ShapeDtypeStruct((slots // 2, 2 * width + GATE_ROWS, LANES), bf16),),
         in_specs=[anywhere] * 11,
@@ -261,17 +263,16 @@
 
 def finish_second(own, peer, came, rest):
     hidden, model = own.shape
-    half = hidden // 2
-    part = pl.BlockSpec((hidden, 512), lambda j: (0, j))
+    part = pl.BlockSpec((hidden, 1024), lambda j: (0, j))
     return pl.pallas_call(
         finish_second_kernel,
-        grid=(model // 512,),
+        grid=(model // 1024,),
         out_shape=jax.ShapeDtypeStruct((hidden, model), bf16),
         in_specs=[
             part,
             part,
-            pl.BlockSpec((half, 512), lambda j: (2, j)),
-            pl.BlockSpec((half, 512), lambda j: (0, j)),
+            pl.BlockSpec((AHEAD_GRAD, 1024), lambda j: (hidden // AHEAD_GRAD, j)),
+            pl.BlockSpec((hidden - AHEAD_GRAD, 1024), lambda j: (0, j)),
         ],
         out_specs=part,
         name="finish_second",
@@ -291,13 +292,12 @@
     slots = 2 * experts
     own_in, own_out = w_in[0], w_out[0]
     gates = gate_weights.T
-    half = own_out.shape[0] // 2
     oth_in = hold(lax.ppermute(own_in, "yl", SWAP), HOLD_FLOPS)
-    oth_upper = hold(lax.ppermute(own_out[:half], "yl", SWAP), HOLD_FLOPS)
+    oth_upper = hold(lax.ppermute(own_out[:AHEAD_OUT], "yl", SWAP), HOLD_FLOPS)
     outgoing, target = dispatch(expert_ids.T, gates, tokens, d_out, experts)
     arrived = exchange(outgoing.reshape(experts, 4 * width, LANES), groups)
     own_in, own_out, oth_in = lax.optimization_barrier((own_in, own_out, oth_in))
-    oth_lower = lax.ppermute(own_out[half:], "yl", SWAP)
+    oth_lower = hold(lax.ppermute(own_out[AHEAD_OUT:], "yl", SWAP), HOLD_FLOPS)
     near = [own_in, own_out, lax.ppermute(own_in, "core", SWAP), lax.ppermute(own_out, "core", SWAP)]
     far = [oth_in, oth_upper, oth_lower]
     far += [lax.ppermute(w, "core", SWAP) for w in far]

time: 199 us -> 197 us (0.990)
  the two profiles are of different devices: /device:TPU:20 before, /device:TPU:48 now
where the time goes in v7:
time: 197 us; the launch traced here: 196 us
  waiting for transfers between devices  93.1 us (47%)
  starting transfers between devices  62.5 us (32%)
  Pallas kernels  24.8 us (13%)
  local copies, waits for them, and re-layouts  9.73 us (5%)
  other arithmetic  5.15 us (3%)
    all_to_all x2, starting transfers between devices, exchange(): lax.all_to_all(x, AXES, split_axis=0, concat_axis=0, axis_index_groups=gr...  32.1 us
    ppermute x1, waiting for transfers between devices, on_device(): oth_upper = hold(lax.ppermute(own_out[:AHEAD_OUT], 'yl', SWAP), HOLD_FLOPS)  23.7 us
    all_to_all x2, waiting for transfers between devices, exchange(): lax.all_to_all(x, AXES, split_axis=0, concat_axis=0, axis_index_groups=gr...  21.8 us
    ppermute x1, waiting for transfers between devices, on_device(): came_a = hold(lax.ppermute(sum_a, 'yl', SWAP), HOLD_FLOPS)  21 us
    ppermute x1, waiting for transfers between devices, on_device(): oth_lower = hold(lax.ppermute(own_out[AHEAD_OUT:], 'yl', SWAP), HOLD_FLOPS)  17 us
    pallas_call x1, Pallas kernels, run_experts(): pl.pallas_call(experts_kernel, out_shape=tuple((jax.ShapeDtypeStruct((r,...  11.5 us
    ppermute x3, starting transfers between devices, on_device(): far += [lax.ppermute(w, 'core', SWAP) for w in far]  6.23 us
    unnamed x12, local copies, waits for them, and re-layouts  5.34 us
  transfers between devices with their start and end apart: 16, of which 8 were waited for; matrix products, arithmetic and copies ran while one was open for 2% of the time, Pallas kernels for 5%

profile of v7, /device:TPU:48, one launch (start us, length us, event | category | flops | bytes accessed | tf_op | source)
XLA Modules:
  0.0 196.1 jit_solution(2311068329907834098)
XLA Ops:
  0.6 2.6 %collective-permute-start = (bf16[2048,256]{1,0:T(8,128)(2,1)}, bf16[2048,256]{1,0:T(8,128)(2,1)}, u32[]{:S(2)}, u32[]{:S(2)}) collective-permute-start(bf16[2048,256]{1,0:T(8,128)(2,1)} %bitcast.19), channel_id=1, source_target_pairs={{0,2},{2,0},{1,3},{3,1},{4,6},{6,4},{5,7},{7,5},{8,10},{10,8},{9,1... | collective-permute-start | bytes 3145736 | tf_op jit(solution)/shard_map/ppermute | solution.py:295
  3.2 2.1 %slice_bitcast_fusion = bf16[192,2048]{1,0:T(8,128)(2,1)} fusion(bf16[1,256,2048]{2,1,0:T(8,128)(2,1)} %param.11), kind=kLoop, calls=%fused_computation.2 | loop fusion | bytes 1572864 | tf_op jit(solution)/shard_map/slice | solution.py:296
  5.3 3.2 %collective-permute-start.3 = (bf16[192,2048]{1,0:T(8,128)(2,1)}, bf16[192,2048]{1,0:T(8,128)(2,1)}, u32[]{:S(2)}, u32[]{:S(2)}) collective-permute-start(bf16[192,2048]{1,0:T(8,128)(2,1)} %slice_bitcast_fusion), channel_id=1, source_target_pairs={{0,2},{2,0},{1,3},{3,1},{4,6},{6,4},{5,7},{7,5},{8,10},{10,8},{9,1... | collective-permute-start | bytes 2359304 | tf_op jit(solution)/shard_map/ppermute | solution.py:296
  8.6 3.7 %dispatch.1 = (bf16[256,32,128]{2,1,0:T(8,128)(2,1)}, s32[4,32]{1,0:T(4,128)}) custom-call(s32[4,32]{1,0:T(4,128)} %bitcast.18, f32[4,32]{1,0:T(4,128)} %bitcast.16, bf16[32,2048]{1,0:T(8,128)(2,1)} %tok_ref.1, bf16[32,2048]{1,0:T(8,128)(2,1)} %dout_ref.1), custom_call_target="tpu_custom_call" | custom-call | tf_op jit(solution)/shard_map/dispatch/pallas_call | solution.py:62
  12.3 19.3 %all-to-all-start = ((bf16[128,64,128]{2,1,0:T(8,128)(2,1)}), bf16[128,64,128]{2,1,0:T(8,128)(2,1)S(1)}, u32[]{:S(2)}, u32[]{:S(2)}) async-start(bf16[128,64,128]{2,1,0:T(8,128)(2,1)} %bitcast.10), calls=%async_computation | async-start | bytes 4194304 | tf_op jit(solution)/shard_map/all_to_all | solution.py:283
  31.5 0.0 copy-start.2
  31.6 0.0 collective-permute-done.x_ref
  31.6 1.2 copy-done.2
  32.8 1.9 collective-permute-start.4
  34.7 23.7 %collective-permute-done.3.x_ref = bf16[192,2048]{1,0:T(8,128)(2,1)} collective-permute-done((bf16[192,2048]{1,0:T(8,128)(2,1)}, bf16[192,2048]{1,0:T(8,128)(2,1)}, u32[]{:S(2)}, u32[]{:S(2)}) %collective-permute-start.3) | collective-permute-done | bytes 786464 | tf_op jit(solution)/shard_map/ppermute | solution.py:296
  58.4 1.9 collective-permute-start.6
  60.3 2.4 %collective-permute-start.2 = (bf16[256,2048]{1,0:T(8,128)(2,1)S(1)}, bf16[256,2048]{1,0:T(8,128)(2,1)}, u32[]{:S(2)}, u32[]{:S(2)}) collective-permute-start(bf16[256,2048]{1,0:T(8,128)(2,1)S(1)} %bitcast.15), channel_id=1, source_target_pairs={{0,1},{1,0},{2,3},{3,2},{4,5},{5,4},{6,7},{7,6},{8,9},{9,8},{10,11... | collective-permute-start | bytes 3145736 | tf_op jit(solution)/shard_map/ppermute | solution.py:301
  62.7 1.9 collective-permute-start.1
  64.6 2.4 %collective-permute-start.5 = (bf16[2048,256]{1,0:T(8,128)(2,1)}, bf16[2048,256]{1,0:T(8,128)(2,1)}, u32[]{:S(2)}, u32[]{:S(2)}) collective-permute-start(bf16[2048,256]{1,0:T(8,128)(2,1)} %hold.5.refs_4_), channel_id=1, source_target_pairs={{0,1},{1,0},{2,3},{3,2},{4,5},{5,4},{6,7},{7,6},{8,9},{9,8},{10,11... | collective-permute-start | bytes 3145736 | tf_op jit(solution)/shard_map/ppermute | solution.py:303
  67.1 17.0 %collective-permute-done.4.x_ref = bf16[64,2048]{1,0:T(8,128)(2,1)} collective-permute-done((bf16[64,2048]{1,0:T(8,128)(2,1)S(1)}, bf16[64,2048]{1,0:T(8,128)(2,1)}, u32[]{:S(2)}, u32[]{:S(2)}) %collective-permute-start.4) | collective-permute-done | bytes 262176 | tf_op jit(solution)/shard_map/ppermute | solution.py:300
  84.0 1.9 collective-permute-start.7
  85.9 0.0 collective-permute-done.6.refs_8_
  86.0 1.7 collective-permute-done.7.refs_9_
  87.7 0.0 copy-start.5
  87.7 0.0 collective-permute-done.1.refs_2_
  87.7 0.0 collective-permute-done.5.refs_7_
  87.7 0.0 collective-permute-done.2.refs_3_
  87.7 9.9 %all-to-all-done = bf16[128,64,128]{2,1,0:T(8,128)(2,1)S(1)} async-done(((bf16[128,64,128]{2,1,0:T(8,128)(2,1)}), bf16[128,64,128]{2,1,0:T(8,128)(2,1)S(1)}, u32[]{:S(2)}, u32[]{:S(2)}) %all-to-all-start) | async-done | bytes 2097184 | tf_op jit(solution)/shard_map/all_to_all | solution.py:283
  97.5 2.3 %reshape.16.rows_hbm = bf16[256,4096]{1,0:T(8,128)(2,1)} reshape(bf16[128,64,128]{2,1,0:T(8,128)(2,1)S(1)} %all-to-all-done) | data formatting | bytes 4194304 | tf_op jit(solution)/shard_map/reshape | solution.py:305
  99.8 0.0 copy-done.5
  99.8 11.5 %experts.1 = (bf16[256,2048]{1,0:T(8,128)(2,1)}, bf16[256,2048]{1,0:T(8,128)(2,1)}, bf16[256,2048]{1,0:T(8,128)(2,1)}, bf16[256,2048]{1,0:T(8,128)(2,1)}, bf16[3...) custom-call(bf16[256,4096]{1,0:T(8,128)(2,1)} %reshape.16.rows_hbm, ...), custom_call_target="tpu_custom_call" | custom-call | flops 5368709120 | bytes 18874368 | tf_op jit(solution)/shard_map/experts/pallas_call | solution.py:211
  111.3 1.9 collective-permute-start.8
  113.2 3.2 %collective-permute-done.8 = bf16[320,2048]{1,0:T(8,128)(2,1)S(1)} collective-permute-done((bf16[320,2048]{1,0:T(8,128)(2,1)}, bf16[320,2048]{1,0:T(8,128)(2,1)S(1)}, u32[]{:S(2)}, u32[]{:S(2)}) %collective-permute-start.8) | collective-permute-done | bytes 1310752 | tf_op jit(solution)/shard_map/ppermute | solution.py:311
  116.4 2.9 %add_convert_fusion = bf16[320,2048]{1,0:T(8,128)(2,1)} fusion(bf16[320,2048]{1,0:T(8,128)(2,1)S(1)} %collective-permute-done.8, bf16[320,2048]{1,0:T(8,128)(2,1)} %get-tuple-element.59), kind=kLoop, calls=%fused_computation | loop fusion | flops 2621440 | bytes 3932160 | tf_op jit(solution)/shard_map/convert_element_type | solution.py:309
  119.3 2.0 %collective-permute-start.9 = (bf16[192,2048]{1,0:T(8,128)(2,1)}, bf16[192,2048]{1,0:T(8,128)(2,1)}, u32[]{:S(2)}, u32[]{:S(2)}) collective-permute-start(bf16[192,2048]{1,0:T(8,128)(2,1)} %get-tuple-element.61), channel_id=1, source_target_pairs={{0,1},{1,0},{2,3},{3,2},{4,5},{5,4},{6,7},{7,6},{8,9},{9,8},{10,11... | collective-permute-start | bytes 2359304 | tf_op jit(solution)/shard_map/ppermute | solution.py:315
  121.4 1.9 collective-permute-start.12
  123.3 12.8 %all-to-all-start.1 = ((bf16[128,40,128]{2,1,0:T(8,128)(2,1)}), bf16[128,40,128]{2,1,0:T(8,128)(2,1)S(1)}, u32[]{:S(2)}, u32[]{:S(2)}) async-start(bf16[128,40,128]{2,1,0:T(8,128)(2,1)} %get-tuple-element.66), calls=%async_computation.1 | async-start | bytes 2621440 | tf_op jit(solution)/shard_map/all_to_all | solution.py:283
  136.1 0.0 copy-start.4
  136.1 0.0 collective-permute-done.9.x_ref
  136.1 1.1 copy-done.4
  137.2 2.3 %add_convert_fusion.1 = bf16[192,2048]{1,0:T(8,128)(2,1)} fusion(bf16[192,2048]{1,0:T(8,128)(2,1)} %hold.8, bf16[192,2048]{1,0:T(8,128)(2,1)S(1)} %copy-done.4), kind=kLoop, calls=%fused_computation.1 | loop fusion | flops 1572864 | bytes 2359296 | tf_op jit(solution)/shard_map/convert_element_type | solution.py:309
  139.5 1.9 collective-permute-start.10
  141.4 1.9 collective-permute-start.11
  143.3 2.4 %collective-permute-start.13 = (bf16[256,2048]{1,0:T(8,128)(2,1)}, bf16[256,2048]{1,0:T(8,128)(2,1)}, u32[]{:S(2)}, u32[]{:S(2)}) collective-permute-start(bf16[256,2048]{1,0:T(8,128)(2,1)} %get-tuple-element.76), channel_id=1, source_target_pairs={{0,1},{1,0},{2,3},{3,2},{4,5},{5,4},{6,7},{7,6},{8,9},{9,8},{10,11... | collective-permute-start | bytes 3145736 | tf_op jit(solution)/shard_map/ppermute | solution.py:320
  145.8 21.0 %collective-permute-done.12.x_ref = bf16[320,2048]{1,0:T(8,128)(2,1)S(1)} collective-permute-done((bf16[320,2048]{1,0:T(8,128)(2,1)}, bf16[320,2048]{1,0:T(8,128)(2,1)S(1)}, u32[]{:S(2)}, u32[]{:S(2)}) %collective-permute-start.12) | collective-permute-done | bytes 1310752 | tf_op jit(solution)/shard_map/ppermute | solution.py:312
  166.8 0.0 copy-start.1
  166.8 1.1 copy-done.1
  167.9 0.0 collective-permute-done.11.peer_ref
  167.9 4.0 %finish_first.1 = bf16[2048,256]{1,0:T(8,128)(2,1)} custom-call(bf16[256,2048]{1,0:T(8,128)(2,1)} %get-tuple-element.67.own_ref, bf16[256,2048]{1,0:T(8,128)(2,1)} %collective-permute-done.11.peer_ref, bf16[320,2048]{1,0:T(8,128)(2,1)} %hold.9.came_ref.upper_ref), custom_call_target="tpu_custom_call" | custom-call | tf_op jit(solution)/shard_map/finish_first/pallas_call | solution.py:254
  171.9 12.0 %all-to-all-done.1.back_ref = bf16[128,40,128]{2,1,0:T(8,128)(2,1)S(1)} async-done(((bf16[128,40,128]{2,1,0:T(8,128)(2,1)}), bf16[128,40,128]{2,1,0:T(8,128)(2,1)S(1)}, u32[]{:S(2)}, u32[]{:S(2)}) %all-to-all-start.1) | async-done | bytes 1310752 | tf_op jit(solution)/shard_map/all_to_all | solution.py:283
  183.8 0.0 copy-start
  183.8 1.1 copy-done
  184.9 2.9 %combine.1 = (bf16[32,2048]{1,0:T(8,128)(2,1)}, f32[4,32]{1,0:T(4,128)}) custom-call(s32[4,32]{1,0:T(4,128)} %get-tuple-element.65.target_ref, bf16[128,40,128]{2,1,0:T(8,128)(2,1)} %copy-done, f32[4,32]{1,0:T(4,128)} %bitcast.17), custom_call_target="tpu_custom_call" | custom-call | tf_op jit(solution)/shard_map/combine/pallas_call | solution.py:122
  187.8 4.7 %collective-permute-done.10.lower_ref = bf16[192,2048]{1,0:T(8,128)(2,1)S(1)} collective-permute-done((bf16[192,2048]{1,0:T(8,128)(2,1)}, bf16[192,2048]{1,0:T(8,128)(2,1)S(1)}, u32[]{:S(2)}, u32[]{:S(2)}) %collective-permute-start.10) | collective-permute-done | bytes 786464 | tf_op jit(solution)/shard_map/ppermute | solution.py:318
  192.4 0.0 copy-start.3
  192.5 0.0 collective-permute-done.13.peer_ref
  192.5 0.9 copy-done.3
  193.3 2.8 %finish_second.1 = bf16[256,2048]{1,0:T(8,128)(2,1)} custom-call(bf16[256,2048]{1,0:T(8,128)(2,1)} %get-tuple-element.75.own_ref, bf16[256,2048]{1,0:T(8,128)(2,1)} %collective-permute-done.13.peer_ref, bf16[320,2048]{1,0:T(8,128)(2,1)} %hold.9.came_ref.upper_ref, bf16[192,2048]{1,0:T(8,128)(2,1)} %copy-done.3), custom_call_target="tpu_custom_call" | custom-call | tf_op jit(solution)/shard_map/finish_second/pallas_call | solution.py:267
  (6 shorter events, 0.0 us)
Async XLA Ops:
  0.6 30.9 %collective-permute-start = (bf16[2048,256]{1,0:T(8,128)(2,1)}, bf16[2048,256]{1,0:T(8,128)(2,1)}, u32[]{:S(2)}, u32[]{:S(2)}) collective-permute-start(bf16[2048,256]{1,0:T(8,128)(2,1)} %bitcast.19), channel_id=1, source_target_pairs={{0,2},{2,0},{1,3},{3,1},{4,6},{6,4},{5,7},{7,5},{8,10},{10,8},{9,1... | collective-permute-start | bytes 3145736 | tf_op jit(solution)/shard_map/ppermute | solution.py:295
  5.3 53.1 %collective-permute-start.3 = (bf16[192,2048]{1,0:T(8,128)(2,1)}, bf16[192,2048]{1,0:T(8,128)(2,1)}, u32[]{:S(2)}, u32[]{:S(2)}) collective-permute-start(bf16[192,2048]{1,0:T(8,128)(2,1)} %slice_bitcast_fusion), channel_id=1, source_target_pairs={{0,2},{2,0},{1,3},{3,1},{4,6},{6,4},{5,7},{7,5},{8,10},{10,8},{9,1... | collective-permute-start | bytes 2359304 | tf_op jit(solution)/shard_map/ppermute | solution.py:296
  12.3 85.3 %all-to-all-start = ((bf16[128,64,128]{2,1,0:T(8,128)(2,1)}), bf16[128,64,128]{2,1,0:T(8,128)(2,1)S(1)}, u32[]{:S(2)}, u32[]{:S(2)}) async-start(bf16[128,64,128]{2,1,0:T(8,128)(2,1)} %bitcast.10), calls=%async_computation | async-start | bytes 4194304 | tf_op jit(solution)/shard_map/all_to_all | solution.py:283
  31.5 1.2 copy-start.2
  32.8 51.2 %collective-permute-start.4 = (bf16[64,2048]{1,0:T(8,128)(2,1)S(1)}, bf16[64,2048]{1,0:T(8,128)(2,1)}, u32[]{:S(2)}, u32[]{:S(2)}) collective-permute-start(bf16[64,2048]{1,0:T(8,128)(2,1)S(1)} %slice.11), channel_id=1, source_target_pairs={{0,2},{2,0},{1,3},{3,1},{4,6},{6,4},{5,7},{7,5},{8,10},{10,8},{9,1... | collective-permute-start | bytes 786440 | tf_op jit(solution)/shard_map/ppermute | solution.py:300
  58.4 27.6 %collective-permute-start.6 = (bf16[192,2048]{1,0:T(8,128)(2,1)}, bf16[192,2048]{1,0:T(8,128)(2,1)}, u32[]{:S(2)}, u32[]{:S(2)}) collective-permute-start(bf16[192,2048]{1,0:T(8,128)(2,1)} %hold.6.refs_5_), channel_id=1, source_target_pairs={{0,1},{1,0},{2,3},{3,2},{4,5},{5,4},{6,7},{7,6},{8,9},{9,8},{10,11... | collective-permute-start | bytes 2359304 | tf_op jit(solution)/shard_map/ppermute | solution.py:303
  60.3 27.4 %collective-permute-start.2 = (bf16[256,2048]{1,0:T(8,128)(2,1)S(1)}, bf16[256,2048]{1,0:T(8,128)(2,1)}, u32[]{:S(2)}, u32[]{:S(2)}) collective-permute-start(bf16[256,2048]{1,0:T(8,128)(2,1)S(1)} %bitcast.15), channel_id=1, source_target_pairs={{0,1},{1,0},{2,3},{3,2},{4,5},{5,4},{6,7},{7,6},{8,9},{9,8},{10,11... | collective-permute-start | bytes 3145736 | tf_op jit(solution)/shard_map/ppermute | solution.py:301
  62.7 24.9 %collective-permute-start.1 = (bf16[2048,256]{1,0:T(8,128)(2,1)}, bf16[2048,256]{1,0:T(8,128)(2,1)}, u32[]{:S(2)}, u32[]{:S(2)}) collective-permute-start(bf16[2048,256]{1,0:T(8,128)(2,1)} %bitcast.20), channel_id=1, source_target_pairs={{0,1},{1,0},{2,3},{3,2},{4,5},{5,4},{6,7},{7,6},{8,9},{9,8},{10,11... | collective-permute-start | bytes 3145736 | tf_op jit(solution)/shard_map/ppermute | solution.py:301
  64.6 23.0 %collective-permute-start.5 = (bf16[2048,256]{1,0:T(8,128)(2,1)}, bf16[2048,256]{1,0:T(8,128)(2,1)}, u32[]{:S(2)}, u32[]{:S(2)}) collective-permute-start(bf16[2048,256]{1,0:T(8,128)(2,1)} %hold.5.refs_4_), channel_id=1, source_target_pairs={{0,1},{1,0},{2,3},{3,2},{4,5},{5,4},{6,7},{7,6},{8,9},{9,8},{10,11... | collective-permute-start | bytes 3145736 | tf_op jit(solution)/shard_map/ppermute | solution.py:303
  84.0 3.6 %collective-permute-start.7 = (bf16[64,2048]{1,0:T(8,128)(2,1)}, bf16[64,2048]{1,0:T(8,128)(2,1)S(1)}, u32[]{:S(2)}, u32[]{:S(2)}) collective-permute-start(bf16[64,2048]{1,0:T(8,128)(2,1)} %hold.7.refs_6_), channel_id=1, source_target_pairs={{0,1},{1,0},{2,3},{3,2},{4,5},{5,4},{6,7},{7,6},{8,9},{9,8},{10,11... | collective-permute-start | bytes 786440 | tf_op jit(solution)/shard_map/ppermute | solution.py:303
  87.7 12.2 %copy-start.5 = (bf16[64,2048]{1,0:T(8,128)(2,1)}, bf16[64,2048]{1,0:T(8,128)(2,1)S(1)}, u32[]{:S(2)}) copy-start(bf16[64,2048]{1,0:T(8,128)(2,1)S(1)} %collective-permute-done.7.refs_9_) | copy-start | bytes 786436
  111.3 5.1 %collective-permute-start.8 = (bf16[320,2048]{1,0:T(8,128)(2,1)}, bf16[320,2048]{1,0:T(8,128)(2,1)S(1)}, u32[]{:S(2)}, u32[]{:S(2)}) collective-permute-start(bf16[320,2048]{1,0:T(8,128)(2,1)} %get-tuple-element.60), channel_id=1, source_target_pairs={{0,1},{1,0},{2,3},{3,2},{4,5},{5,4},{6,7},{7,6},{8,9},{9,8},{10,11... | collective-permute-start | bytes 3932168 | tf_op jit(solution)/shard_map/ppermute | solution.py:311
  119.3 16.8 %collective-permute-start.9 = (bf16[192,2048]{1,0:T(8,128)(2,1)}, bf16[192,2048]{1,0:T(8,128)(2,1)}, u32[]{:S(2)}, u32[]{:S(2)}) collective-permute-start(bf16[192,2048]{1,0:T(8,128)(2,1)} %get-tuple-element.61), channel_id=1, source_target_pairs={{0,1},{1,0},{2,3},{3,2},{4,5},{5,4},{6,7},{7,6},{8,9},{9,8},{10,11... | collective-permute-start | bytes 2359304 | tf_op jit(solution)/shard_map/ppermute | solution.py:315
  121.4 45.4 %collective-permute-start.12 = (bf16[320,2048]{1,0:T(8,128)(2,1)}, bf16[320,2048]{1,0:T(8,128)(2,1)S(1)}, u32[]{:S(2)}, u32[]{:S(2)}) collective-permute-start(bf16[320,2048]{1,0:T(8,128)(2,1)} %add_convert_fusion), channel_id=1, source_target_pairs={{0,2},{2,0},{1,3},{3,1},{4,6},{6,4},{5,7},{7,5},{8,10},{10,8},{9,1... | collective-permute-start | bytes 3932168 | tf_op jit(solution)/shard_map/ppermute | solution.py:312
  123.3 60.6 %all-to-all-start.1 = ((bf16[128,40,128]{2,1,0:T(8,128)(2,1)}), bf16[128,40,128]{2,1,0:T(8,128)(2,1)S(1)}, u32[]{:S(2)}, u32[]{:S(2)}) async-start(bf16[128,40,128]{2,1,0:T(8,128)(2,1)} %get-tuple-element.66), calls=%async_computation.1 | async-start | bytes 2621440 | tf_op jit(solution)/shard_map/all_to_all | solution.py:283
  136.1 1.1 copy-start.4
  139.5 53.0 %collective-permute-start.10 = (bf16[192,2048]{1,0:T(8,128)(2,1)}, bf16[192,2048]{1,0:T(8,128)(2,1)S(1)}, u32[]{:S(2)}, u32[]{:S(2)}) collective-permute-start(bf16[192,2048]{1,0:T(8,128)(2,1)} %add_convert_fusion.1), channel_id=1, source_target_pairs={{0,2},{2,0},{1,3},{3,1},{4,6},{6,4},{5,7},{7,5},{8,10},{10,8},{9,1... | collective-permute-start | bytes 2359304 | tf_op jit(solution)/shard_map/ppermute | solution.py:318
  141.4 26.5 %collective-permute-start.11 = (bf16[256,2048]{1,0:T(8,128)(2,1)}, bf16[256,2048]{1,0:T(8,128)(2,1)}, u32[]{:S(2)}, u32[]{:S(2)}) collective-permute-start(bf16[256,2048]{1,0:T(8,128)(2,1)} %get-tuple-element.68), channel_id=1, source_target_pairs={{0,1},{1,0},{2,3},{3,2},{4,5},{5,4},{6,7},{7,6},{8,9},{9,8},{10,11... | collective-permute-start | bytes 3145736 | tf_op jit(solution)/shard_map/ppermute | solution.py:319
  143.3 49.1 %collective-permute-start.13 = (bf16[256,2048]{1,0:T(8,128)(2,1)}, bf16[256,2048]{1,0:T(8,128)(2,1)}, u32[]{:S(2)}, u32[]{:S(2)}) collective-permute-start(bf16[256,2048]{1,0:T(8,128)(2,1)} %get-tuple-element.76), channel_id=1, source_target_pairs={{0,1},{1,0},{2,3},{3,2},{4,5},{5,4},{6,7},{7,6},{8,9},{9,8},{10,11... | collective-permute-start | bytes 3145736 | tf_op jit(solution)/shard_map/ppermute | solution.py:320
  166.8 1.1 copy-start.1
  183.8 1.1 copy-start
  192.4 0.9 copy-start.3

commit v8 on v7

--- a/solution.py
+++ b/solution.py
@@ -14,7 +14,7 @@
 AXES = ("dp", "yh", "yl", "core")
 GATE_ROWS = 8
 AHEAD_OUT = 192
-AHEAD_GRAD = 64
+AHEAD_GRAD = 128
 HOLD_FLOPS = int(3e10)
 SWAP = [(0, 1), (1, 0)]
 f32, bf16 = jnp.float32, jnp.bfloat16
@@ -319,10 +319,9 @@
     near_in = lax.ppermute(peer_gi, "core", SWAP)
     near_out = lax.ppermute(peer_go, "core", SWAP)
     d_first = finish_first(own_gi, near_in, came_a)
-    returned, d_first = lax.optimization_barrier((returned, d_first))
+    d_second = finish_second(own_go, near_out, came_a, came_b)
+    returned, d_first, d_second = lax.optimization_barrier((returned, d_first, d_second))
     d_tokens, d_gates = combine(target, returned, gates, model)
-    came_b, d_tokens, d_gates = lax.optimization_barrier((came_b, d_tokens, d_gates))
-    d_second = finish_second(own_go, near_out, came_a, came_b)
     return (d_tokens, d_gates.T, d_first[None], d_second[None])
 
 

time: 197 us -> 202 us (1.025)
  waiting for transfers between devices: 93.1 us -> 97.8 us
    all_to_all x2, waiting for transfers between devices: 21.8 us -> 9.86 us  [exchange(): lax.all_to_all(x, AXES, split_axis=0, concat_axis=0, axis_index_groups=gr...]
    ppermute x1, waiting for transfers between devices: 4.66 us -> 15 us  [on_device(): came_b = lax.ppermute(sum_b, 'yl', SWAP)]
    ppermute x1, waiting for transfers between devices: 21 us -> 27.1 us  [on_device(): came_a = hold(lax.ppermute(sum_a, 'yl', SWAP), HOLD_FLOPS)]
  transfers between devices with their start and end apart: 16 -> 16, of which waited for: 8 -> 7; matrix products, arithmetic and copies ran while one was open for 2% -> 2% of each run, Pallas kernels for 5% -> 5%
where the time goes in v8:
time: 202 us; the launch traced here: 201 us
  waiting for transfers between devices  97.8 us (48%)
  starting transfers between devices  62.5 us (31%)
  Pallas kernels  24.9 us (12%)
  local copies, waits for them, and re-layouts  9.66 us (5%)
  other arithmetic  5.14 us (3%)
    all_to_all x2, starting transfers between devices, exchange(): lax.all_to_all(x, AXES, split_axis=0, concat_axis=0, axis_index_groups=gr...  32.1 us
    ppermute x1, waiting for transfers between devices, on_device(): came_a = hold(lax.ppermute(sum_a, 'yl', SWAP), HOLD_FLOPS)  27.1 us
    ppermute x1, waiting for transfers between devices, on_device(): oth_upper = hold(lax.ppermute(own_out[:AHEAD_OUT], 'yl', SWAP), HOLD_FLOPS)  23.7 us
    ppermute x1, waiting for transfers between devices, on_device(): oth_lower = hold(lax.ppermute(own_out[AHEAD_OUT:], 'yl', SWAP), HOLD_FLOPS)  17 us
    ppermute x1, waiting for transfers between devices, on_device(): came_b = lax.ppermute(sum_b, 'yl', SWAP)  15 us
    pallas_call x1, Pallas kernels, run_experts(): pl.pallas_call(experts_kernel, out_shape=tuple((jax.ShapeDtypeStruct((r,...  11.5 us
    all_to_all x2, waiting for transfers between devices, exchange(): lax.all_to_all(x, AXES, split_axis=0, concat_axis=0, axis_index_groups=gr...  9.86 us
    ppermute x3, starting transfers between devices, on_device(): far += [lax.ppermute(w, 'core', SWAP) for w in far]  6.23 us
  transfers between devices with their start and end apart: 16, of which 7 were waited for; matrix products, arithmetic and copies ran while one was open for 2% of the time, Pallas kernels for 5%

profile of v8, /device:TPU:48, one launch (start us, length us, event | category | flops | bytes accessed | tf_op | source)
XLA Modules:
  0.0 200.8 jit_solution(3142140608029269306)
XLA Ops:
  0.6 2.6 %collective-permute-start = (bf16[2048,256]{1,0:T(8,128)(2,1)}, bf16[2048,256]{1,0:T(8,128)(2,1)}, u32[]{:S(2)}, u32[]{:S(2)}) collective-permute-start(bf16[2048,256]{1,0:T(8,128)(2,1)} %bitcast.19), channel_id=1, source_target_pairs={{0,2},{2,0},{1,3},{3,1},{4,6},{6,4},{5,7},{7,5},{8,10},{10,8},{9,1... | collective-permute-start | bytes 3145736 | tf_op jit(solution)/shard_map/ppermute | solution.py:295
  3.2 2.1 %slice_bitcast_fusion = bf16[192,2048]{1,0:T(8,128)(2,1)} fusion(bf16[1,256,2048]{2,1,0:T(8,128)(2,1)} %param.11), kind=kLoop, calls=%fused_computation.2 | loop fusion | bytes 1572864 | tf_op jit(solution)/shard_map/slice | solution.py:296
  5.3 3.2 %collective-permute-start.3 = (bf16[192,2048]{1,0:T(8,128)(2,1)}, bf16[192,2048]{1,0:T(8,128)(2,1)}, u32[]{:S(2)}, u32[]{:S(2)}) collective-permute-start(bf16[192,2048]{1,0:T(8,128)(2,1)} %slice_bitcast_fusion), channel_id=1, source_target_pairs={{0,2},{2,0},{1,3},{3,1},{4,6},{6,4},{5,7},{7,5},{8,10},{10,8},{9,1... | collective-permute-start | bytes 2359304 | tf_op jit(solution)/shard_map/ppermute | solution.py:296
  8.6 3.7 %dispatch.1 = (bf16[256,32,128]{2,1,0:T(8,128)(2,1)}, s32[4,32]{1,0:T(4,128)}) custom-call(s32[4,32]{1,0:T(4,128)} %bitcast.18, f32[4,32]{1,0:T(4,128)} %bitcast.16, bf16[32,2048]{1,0:T(8,128)(2,1)} %tok_ref.1, bf16[32,2048]{1,0:T(8,128)(2,1)} %dout_ref.1), custom_call_target="tpu_custom_call" | custom-call | tf_op jit(solution)/shard_map/dispatch/pallas_call | solution.py:62
  12.3 19.3 %all-to-all-start = ((bf16[128,64,128]{2,1,0:T(8,128)(2,1)}), bf16[128,64,128]{2,1,0:T(8,128)(2,1)S(1)}, u32[]{:S(2)}, u32[]{:S(2)}) async-start(bf16[128,64,128]{2,1,0:T(8,128)(2,1)} %bitcast.10), calls=%async_computation | async-start | bytes 4194304 | tf_op jit(solution)/shard_map/all_to_all | solution.py:283
  31.5 0.0 copy-start.2
  31.6 0.0 collective-permute-done.x_ref
  31.6 1.2 copy-done.2
  32.8 1.9 collective-permute-start.4
  34.7 23.7 %collective-permute-done.3.x_ref = bf16[192,2048]{1,0:T(8,128)(2,1)} collective-permute-done((bf16[192,2048]{1,0:T(8,128)(2,1)}, bf16[192,2048]{1,0:T(8,128)(2,1)}, u32[]{:S(2)}, u32[]{:S(2)}) %collective-permute-start.3) | collective-permute-done | bytes 786464 | tf_op jit(solution)/shard_map/ppermute | solution.py:296
  58.4 1.9 collective-permute-start.6
  60.3 2.4 %collective-permute-start.2 = (bf16[256,2048]{1,0:T(8,128)(2,1)S(1)}, bf16[256,2048]{1,0:T(8,128)(2,1)}, u32[]{:S(2)}, u32[]{:S(2)}) collective-permute-start(bf16[256,2048]{1,0:T(8,128)(2,1)S(1)} %bitcast.14), channel_id=1, source_target_pairs={{0,1},{1,0},{2,3},{3,2},{4,5},{5,4},{6,7},{7,6},{8,9},{9,8},{10,11... | collective-permute-start | bytes 3145736 | tf_op jit(solution)/shard_map/ppermute | solution.py:301
  62.7 1.9 collective-permute-start.1
  64.6 2.4 %collective-permute-start.5 = (bf16[2048,256]{1,0:T(8,128)(2,1)}, bf16[2048,256]{1,0:T(8,128)(2,1)}, u32[]{:S(2)}, u32[]{:S(2)}) collective-permute-start(bf16[2048,256]{1,0:T(8,128)(2,1)} %hold.5.refs_4_), channel_id=1, source_target_pairs={{0,1},{1,0},{2,3},{3,2},{4,5},{5,4},{6,7},{7,6},{8,9},{9,8},{10,11... | collective-permute-start | bytes 3145736 | tf_op jit(solution)/shard_map/ppermute | solution.py:303
  67.1 17.0 %collective-permute-done.4.x_ref = bf16[64,2048]{1,0:T(8,128)(2,1)} collective-permute-done((bf16[64,2048]{1,0:T(8,128)(2,1)S(1)}, bf16[64,2048]{1,0:T(8,128)(2,1)}, u32[]{:S(2)}, u32[]{:S(2)}) %collective-permute-start.4) | collective-permute-done | bytes 262176 | tf_op jit(solution)/shard_map/ppermute | solution.py:300
  84.0 1.9 collective-permute-start.7
  85.9 0.0 collective-permute-done.6.refs_8_
  86.0 1.7 collective-permute-done.7.refs_9_
  87.7 0.0 copy-start.5
  87.7 0.0 collective-permute-done.1.refs_2_
  87.7 0.0 collective-permute-done.5.refs_7_
  87.7 0.0 collective-permute-done.2.refs_3_
  87.7 9.9 %all-to-all-done = bf16[128,64,128]{2,1,0:T(8,128)(2,1)S(1)} async-done(((bf16[128,64,128]{2,1,0:T(8,128)(2,1)}), bf16[128,64,128]{2,1,0:T(8,128)(2,1)S(1)}, u32[]{:S(2)}, u32[]{:S(2)}) %all-to-all-start) | async-done | bytes 2097184 | tf_op jit(solution)/shard_map/all_to_all | solution.py:283
  97.5 2.3 %reshape.16.rows_hbm = bf16[256,4096]{1,0:T(8,128)(2,1)} reshape(bf16[128,64,128]{2,1,0:T(8,128)(2,1)S(1)} %all-to-all-done) | data formatting | bytes 4194304 | tf_op jit(solution)/shard_map/reshape | solution.py:305
  99.8 0.0 copy-done.5
  99.8 11.5 %experts.1 = (bf16[256,2048]{1,0:T(8,128)(2,1)}, bf16[256,2048]{1,0:T(8,128)(2,1)}, bf16[256,2048]{1,0:T(8,128)(2,1)}, bf16[256,2048]{1,0:T(8,128)(2,1)}, bf16[3...) custom-call(bf16[256,4096]{1,0:T(8,128)(2,1)} %reshape.16.rows_hbm, ...), custom_call_target="tpu_custom_call" | custom-call | flops 5368709120 | bytes 18874368 | tf_op jit(solution)/shard_map/experts/pallas_call | solution.py:211
  111.3 1.9 collective-permute-start.8
  113.3 3.6 %collective-permute-done.8 = bf16[384,2048]{1,0:T(8,128)(2,1)S(1)} collective-permute-done((bf16[384,2048]{1,0:T(8,128)(2,1)}, bf16[384,2048]{1,0:T(8,128)(2,1)S(1)}, u32[]{:S(2)}, u32[]{:S(2)}) %collective-permute-start.8) | collective-permute-done | bytes 1572896 | tf_op jit(solution)/shard_map/ppermute | solution.py:311
  116.8 3.2 %add_convert_fusion = bf16[384,2048]{1,0:T(8,128)(2,1)} fusion(bf16[384,2048]{1,0:T(8,128)(2,1)S(1)} %collective-permute-done.8, bf16[384,2048]{1,0:T(8,128)(2,1)} %get-tuple-element.57), kind=kLoop, calls=%fused_computation | loop fusion | flops 3145728 | bytes 4718592 | tf_op jit(solution)/shard_map/convert_element_type | solution.py:309
  120.0 2.0 %collective-permute-start.9 = (bf16[128,2048]{1,0:T(8,128)(2,1)}, bf16[128,2048]{1,0:T(8,128)(2,1)}, u32[]{:S(2)}, u32[]{:S(2)}) collective-permute-start(bf16[128,2048]{1,0:T(8,128)(2,1)} %get-tuple-element.62), channel_id=1, source_target_pairs={{0,1},{1,0},{2,3},{3,2},{4,5},{5,4},{6,7},{7,6},{8,9},{9,8},{10,11... | collective-permute-start | bytes 1572872 | tf_op jit(solution)/shard_map/ppermute | solution.py:315
  122.1 1.9 collective-permute-start.11
  124.0 12.8 %all-to-all-start.1 = ((bf16[128,40,128]{2,1,0:T(8,128)(2,1)}), bf16[128,40,128]{2,1,0:T(8,128)(2,1)S(1)}, u32[]{:S(2)}, u32[]{:S(2)}) async-start(bf16[128,40,128]{2,1,0:T(8,128)(2,1)} %get-tuple-element.59), calls=%async_computation.1 | async-start | bytes 2621440 | tf_op jit(solution)/shard_map/all_to_all | solution.py:283
  136.8 0.0 copy-start.3
  136.8 0.0 collective-permute-done.9.x_ref
  136.8 1.0 copy-done.3
  137.9 1.9 add_convert_fusion.1
  139.8 1.9 collective-permute-start.13
  141.7 1.9 collective-permute-start.10
  143.6 2.4 %collective-permute-start.12 = (bf16[256,2048]{1,0:T(8,128)(2,1)}, bf16[256,2048]{1,0:T(8,128)(2,1)}, u32[]{:S(2)}, u32[]{:S(2)}) collective-permute-start(bf16[256,2048]{1,0:T(8,128)(2,1)} %get-tuple-element.67), channel_id=1, source_target_pairs={{0,1},{1,0},{2,3},{3,2},{4,5},{5,4},{6,7},{7,6},{8,9},{9,8},{10,11... | collective-permute-start | bytes 3145736 | tf_op jit(solution)/shard_map/ppermute | solution.py:320
  146.1 27.1 %collective-permute-done.11.x_ref = bf16[384,2048]{1,0:T(8,128)(2,1)S(1)} collective-permute-done((bf16[384,2048]{1,0:T(8,128)(2,1)}, bf16[384,2048]{1,0:T(8,128)(2,1)S(1)}, u32[]{:S(2)}, u32[]{:S(2)}) %collective-permute-start.11) | collective-permute-done | bytes 1572896 | tf_op jit(solution)/shard_map/ppermute | solution.py:312
  173.1 0.0 copy-start
  173.1 1.2 copy-done
  174.3 0.0 collective-permute-done.10.peer_ref
  174.3 4.0 %finish_first.1 = bf16[2048,256]{1,0:T(8,128)(2,1)} custom-call(bf16[256,2048]{1,0:T(8,128)(2,1)} %get-tuple-element.60.own_ref, bf16[256,2048]{1,0:T(8,128)(2,1)} %collective-permute-done.10.peer_ref, bf16[384,2048]{1,0:T(8,128)(2,1)} %hold.9.came_ref.upper_ref), custom_call_target="tpu_custom_call" | custom-call | tf_op jit(solution)/shard_map/finish_first/pallas_call | solution.py:254
  178.3 15.0 %collective-permute-done.13.lower_ref = bf16[128,2048]{1,0:T(8,128)(2,1)S(1)} collective-permute-done((bf16[128,2048]{1,0:T(8,128)(2,1)}, bf16[128,2048]{1,0:T(8,128)(2,1)S(1)}, u32[]{:S(2)}, u32[]{:S(2)}) %collective-permute-start.13) | collective-permute-done | bytes 524320 | tf_op jit(solution)/shard_map/ppermute | solution.py:318
  193.3 0.0 copy-start.4
  193.3 0.0 collective-permute-done.12.peer_ref
  193.3 0.8 copy-done.4
  194.1 2.8 %finish_second.1 = bf16[256,2048]{1,0:T(8,128)(2,1)} custom-call(bf16[256,2048]{1,0:T(8,128)(2,1)} %get-tuple-element.66.own_ref, bf16[256,2048]{1,0:T(8,128)(2,1)} %collective-permute-done.12.peer_ref, bf16[384,2048]{1,0:T(8,128)(2,1)} %hold.9.came_ref.upper_ref, bf16[128,2048]{1,0:T(8,128)(2,1)} %copy-done.4), custom_call_target="tpu_custom_call" | custom-call | tf_op jit(solution)/shard_map/finish_second/pallas_call | solution.py:267
  196.9 0.0 all-to-all-done.1.back_ref
  196.9 0.0 copy-start.1
  196.9 1.1 copy-done.1
  198.0 2.9 %combine.1 = (bf16[32,2048]{1,0:T(8,128)(2,1)}, f32[4,32]{1,0:T(4,128)}) custom-call(s32[4,32]{1,0:T(4,128)} %get-tuple-element.39.target_ref, bf16[128,40,128]{2,1,0:T(8,128)(2,1)} %copy-done.1, f32[4,32]{1,0:T(4,128)} %bitcast.17), custom_call_target="tpu_custom_call" | custom-call | tf_op jit(solution)/shard_map/combine/pallas_call | solution.py:122
  (6 shorter events, 0.0 us)
Async XLA Ops:
  0.6 30.9 %collective-permute-start = (bf16[2048,256]{1,0:T(8,128)(2,1)}, bf16[2048,256]{1,0:T(8,128)(2,1)}, u32[]{:S(2)}, u32[]{:S(2)}) collective-permute-start(bf16[2048,256]{1,0:T(8,128)(2,1)} %bitcast.19), channel_id=1, source_target_pairs={{0,2},{2,0},{1,3},{3,1},{4,6},{6,4},{5,7},{7,5},{8,10},{10,8},{9,1... | collective-permute-start | bytes 3145736 | tf_op jit(solution)/shard_map/ppermute | solution.py:295
  5.3 53.1 %collective-permute-start.3 = (bf16[192,2048]{1,0:T(8,128)(2,1)}, bf16[192,2048]{1,0:T(8,128)(2,1)}, u32[]{:S(2)}, u32[]{:S(2)}) collective-permute-start(bf16[192,2048]{1,0:T(8,128)(2,1)} %slice_bitcast_fusion), channel_id=1, source_target_pairs={{0,2},{2,0},{1,3},{3,1},{4,6},{6,4},{5,7},{7,5},{8,10},{10,8},{9,1... | collective-permute-start | bytes 2359304 | tf_op jit(solution)/shard_map/ppermute | solution.py:296
  12.3 85.3 %all-to-all-start = ((bf16[128,64,128]{2,1,0:T(8,128)(2,1)}), bf16[128,64,128]{2,1,0:T(8,128)(2,1)S(1)}, u32[]{:S(2)}, u32[]{:S(2)}) async-start(bf16[128,64,128]{2,1,0:T(8,128)(2,1)} %bitcast.10), calls=%async_computation | async-start | bytes 4194304 | tf_op jit(solution)/shard_map/all_to_all | solution.py:283
  31.5 1.2 copy-start.2
  32.8 51.2 %collective-permute-start.4 = (bf16[64,2048]{1,0:T(8,128)(2,1)S(1)}, bf16[64,2048]{1,0:T(8,128)(2,1)}, u32[]{:S(2)}, u32[]{:S(2)}) collective-permute-start(bf16[64,2048]{1,0:T(8,128)(2,1)S(1)} %slice.11), channel_id=1, source_target_pairs={{0,2},{2,0},{1,3},{3,1},{4,6},{6,4},{5,7},{7,5},{8,10},{10,8},{9,1... | collective-permute-start | bytes 786440 | tf_op jit(solution)/shard_map/ppermute | solution.py:300
  58.4 27.6 %collective-permute-start.6 = (bf16[192,2048]{1,0:T(8,128)(2,1)}, bf16[192,2048]{1,0:T(8,128)(2,1)}, u32[]{:S(2)}, u32[]{:S(2)}) collective-permute-start(bf16[192,2048]{1,0:T(8,128)(2,1)} %hold.6.refs_5_), channel_id=1, source_target_pairs={{0,1},{1,0},{2,3},{3,2},{4,5},{5,4},{6,7},{7,6},{8,9},{9,8},{10,11... | collective-permute-start | bytes 2359304 | tf_op jit(solution)/shard_map/ppermute | solution.py:303
  60.3 27.4 %collective-permute-start.2 = (bf16[256,2048]{1,0:T(8,128)(2,1)S(1)}, bf16[256,2048]{1,0:T(8,128)(2,1)}, u32[]{:S(2)}, u32[]{:S(2)}) collective-permute-start(bf16[256,2048]{1,0:T(8,128)(2,1)S(1)} %bitcast.14), channel_id=1, source_target_pairs={{0,1},{1,0},{2,3},{3,2},{4,5},{5,4},{6,7},{7,6},{8,9},{9,8},{10,11... | collective-permute-start | bytes 3145736 | tf_op jit(solution)/shard_map/ppermute | solution.py:301
  62.7 24.9 %collective-permute-start.1 = (bf16[2048,256]{1,0:T(8,128)(2,1)}, bf16[2048,256]{1,0:T(8,128)(2,1)}, u32[]{:S(2)}, u32[]{:S(2)}) collective-permute-start(bf16[2048,256]{1,0:T(8,128)(2,1)} %bitcast.20), channel_id=1, source_target_pairs={{0,1},{1,0},{2,3},{3,2},{4,5},{5,4},{6,7},{7,6},{8,9},{9,8},{10,11... | collective-permute-start | bytes 3145736 | tf_op jit(solution)/shard_map/ppermute | solution.py:301
  64.6 23.0 %collective-permute-start.5 = (bf16[2048,256]{1,0:T(8,128)(2,1)}, bf16[2048,256]{1,0:T(8,128)(2,1)}, u32[]{:S(2)}, u32[]{:S(2)}) collective-permute-start(bf16[2048,256]{1,0:T(8,128)(2,1)} %hold.5.refs_4_), channel_id=1, source_target_pairs={{0,1},{1,0},{2,3},{3,2},{4,5},{5,4},{6,7},{7,6},{8,9},{9,8},{10,11... | collective-permute-start | bytes 3145736 | tf_op jit(solution)/shard_map/ppermute | solution.py:303
  84.0 3.6 %collective-permute-start.7 = (bf16[64,2048]{1,0:T(8,128)(2,1)}, bf16[64,2048]{1,0:T(8,128)(2,1)S(1)}, u32[]{:S(2)}, u32[]{:S(2)}) collective-permute-start(bf16[64,2048]{1,0:T(8,128)(2,1)} %hold.7.refs_6_), channel_id=1, source_target_pairs={{0,1},{1,0},{2,3},{3,2},{4,5},{5,4},{6,7},{7,6},{8,9},{9,8},{10,11... | collective-permute-start | bytes 786440 | tf_op jit(solution)/shard_map/ppermute | solution.py:303
  87.7 12.2 %copy-start.5 = (bf16[64,2048]{1,0:T(8,128)(2,1)}, bf16[64,2048]{1,0:T(8,128)(2,1)S(1)}, u32[]{:S(2)}) copy-start(bf16[64,2048]{1,0:T(8,128)(2,1)S(1)} %collective-permute-done.7.refs_9_) | copy-start | bytes 786436
  111.3 5.5 %collective-permute-start.8 = (bf16[384,2048]{1,0:T(8,128)(2,1)}, bf16[384,2048]{1,0:T(8,128)(2,1)S(1)}, u32[]{:S(2)}, u32[]{:S(2)}) collective-permute-start(bf16[384,2048]{1,0:T(8,128)(2,1)} %get-tuple-element.58), channel_id=1, source_target_pairs={{0,1},{1,0},{2,3},{3,2},{4,5},{5,4},{6,7},{7,6},{8,9},{9,8},{10,11... | collective-permute-start | bytes 4718600 | tf_op jit(solution)/shard_map/ppermute | solution.py:311
  120.0 16.8 %collective-permute-start.9 = (bf16[128,2048]{1,0:T(8,128)(2,1)}, bf16[128,2048]{1,0:T(8,128)(2,1)}, u32[]{:S(2)}, u32[]{:S(2)}) collective-permute-start(bf16[128,2048]{1,0:T(8,128)(2,1)} %get-tuple-element.62), channel_id=1, source_target_pairs={{0,1},{1,0},{2,3},{3,2},{4,5},{5,4},{6,7},{7,6},{8,9},{9,8},{10,11... | collective-permute-start | bytes 1572872 | tf_op jit(solution)/shard_map/ppermute | solution.py:315
  122.1 51.0 %collective-permute-start.11 = (bf16[384,2048]{1,0:T(8,128)(2,1)}, bf16[384,2048]{1,0:T(8,128)(2,1)S(1)}, u32[]{:S(2)}, u32[]{:S(2)}) collective-permute-start(bf16[384,2048]{1,0:T(8,128)(2,1)} %add_convert_fusion), channel_id=1, source_target_pairs={{0,2},{2,0},{1,3},{3,1},{4,6},{6,4},{5,7},{7,5},{8,10},{10,8},{9,1... | collective-permute-start | bytes 4718600 | tf_op jit(solution)/shard_map/ppermute | solution.py:312
  124.0 72.9 %all-to-all-start.1 = ((bf16[128,40,128]{2,1,0:T(8,128)(2,1)}), bf16[128,40,128]{2,1,0:T(8,128)(2,1)S(1)}, u32[]{:S(2)}, u32[]{:S(2)}) async-start(bf16[128,40,128]{2,1,0:T(8,128)(2,1)} %get-tuple-element.59), calls=%async_computation.1 | async-start | bytes 2621440 | tf_op jit(solution)/shard_map/all_to_all | solution.py:283
  136.8 1.0 copy-start.3
  139.8 53.5 %collective-permute-start.13 = (bf16[128,2048]{1,0:T(8,128)(2,1)}, bf16[128,2048]{1,0:T(8,128)(2,1)S(1)}, u32[]{:S(2)}, u32[]{:S(2)}) collective-permute-start(bf16[128,2048]{1,0:T(8,128)(2,1)} %add_convert_fusion.1), channel_id=1, source_target_pairs={{0,2},{2,0},{1,3},{3,1},{4,6},{6,4},{5,7},{7,5},{8,10},{10,8},{9,1... | collective-permute-start | bytes 1572872 | tf_op jit(solution)/shard_map/ppermute | solution.py:318
  141.7 32.6 %collective-permute-start.10 = (bf16[256,2048]{1,0:T(8,128)(2,1)}, bf16[256,2048]{1,0:T(8,128)(2,1)}, u32[]{:S(2)}, u32[]{:S(2)}) collective-permute-start(bf16[256,2048]{1,0:T(8,128)(2,1)} %get-tuple-element.65), channel_id=1, source_target_pairs={{0,1},{1,0},{2,3},{3,2},{4,5},{5,4},{6,7},{7,6},{8,9},{9,8},{10,11... | collective-permute-start | bytes 3145736 | tf_op jit(solution)/shard_map/ppermute | solution.py:319
  143.6 49.6 %collective-permute-start.12 = (bf16[256,2048]{1,0:T(8,128)(2,1)}, bf16[256,2048]{1,0:T(8,128)(2,1)}, u32[]{:S(2)}, u32[]{:S(2)}) collective-permute-start(bf16[256,2048]{1,0:T(8,128)(2,1)} %get-tuple-element.67), channel_id=1, source_target_pairs={{0,1},{1,0},{2,3},{3,2},{4,5},{5,4},{6,7},{7,6},{8,9},{9,8},{10,11... | collective-permute-start | bytes 3145736 | tf_op jit(solution)/shard_map/ppermute | solution.py:320
  173.1 1.2 copy-start
  193.3 0.8 copy-start.4
  196.9 1.1 copy-start.1
